TPU v7x, 256 devices: a whole 4x4x8 slice. The times are simulated.
256 devices in a mesh: tm: 64 (over y, z_lo, x, core), floor: 4 (over z_hi).
Axes of the slice: x: 4, y: 4, z: 8 (z_hi: 4, z_lo: 2; z = z_hi * 2 + z_lo), core: 2. Of those that a mesh axis runs over, the one named last changes fastest.
Arguments:
- samples: bfloat16 [64, 16, 32768], P('tm', None, 'floor'), may hold values from -6 to 6
- operator: bfloat16 [64, 512, 32768], P('tm', None, 'floor'), may hold values from -0.00390625 to 0.00390625
Outputs:
- sensor_data: bfloat16 [64, 16, 512], P('tm', None, 'floor')
All inputs are finite; a program needn't handle non-finite values.
Results may differ from a plain program's by a relative error of at most 0.0013.
Values may be sent and summed in bfloat16 or wider, within the bound.
No kernel may reach another device: no remote copies, remote signals or barrier semaphores. Data moves between devices by JAX's collectives and lax.ppermute only.
A program may use at most 64 MiB of HBM per device.

v0:
```python
import jax
import jax.numpy as jnp
from jax import lax
from jax.sharding import PartitionSpec as P


def local(samples, operator):
    lag = lax.axis_index("tm")
    blocks = lax.axis_size("tm")
    kernel = operator[0]
    images = jnp.einsum(
        "cki,si->cks",
        lax.all_gather(samples, "tm", axis=0, tiled=True),
        kernel,
        preferred_element_type=jnp.float32,
    )
    padded = jnp.pad(images, ((blocks, 0), (0, 0), (0, 0)))
    shifted = lax.dynamic_slice_in_dim(padded, blocks - lag, blocks, 0)
    mine = lax.psum_scatter(shifted, "tm", scatter_dimension=0, tiled=True)
    records = lax.psum_scatter(mine, "floor", scatter_dimension=2, tiled=True)
    return records.astype(jnp.bfloat16)


def solution(mesh):
    placed = (P("tm", None, "floor"), P("tm", None, "floor"))
    return jax.shard_map(
        local, mesh=mesh, in_specs=placed, out_specs=P("tm", None, "floor"), check_vma=False
    )
```

profile of v0, /device:TPU:2, one launch (start us, length us, event | category | flops | bytes accessed | tf_op | source)
XLA Modules:
  0.0 480.6 jit_solution(7905404542060301063)
XLA Ops:
  6.5 0.0 all-gather.2.cloned.1.call-start
  6.5 0.7 all-gather.2.cloned.1.call-update
  7.3 0.0 reduce-scatter.3.cloned.1.call-start
  7.3 130.1 %all-gather.2.cloned.1.call-done = bf16[64,16,8192]{2,1,0:T(8,128)(2,1)} async-done(((bf16[1,16,8192]{2,1,0:T(8,128)(2,1)}), bf16[64,16,8192]{2,1,0:T(8,128)(2,1)}) %all-gather.2.cloned.1.call-update) | async-done | bytes 16777232 | tf_op jit(solution)/shard_map/all_gather | solution.py:13
  137.4 21.5 %fusion = f32[128,16,512]{2,1,0:T(8,128)S(1)} fusion(bf16[64,16,8192]{2,1,0:T(8,128)(2,1)} %all-gather.2.cloned.1.call-done, bf16[1,512,8192]{2,1,0:T(8,128)(2,1)} %param.3), kind=kOutput, calls=%fused_computation | convolution fusion | flops 8589934592 | bytes 29360128 | tf_op jit(solution)/shard_map/jit(_pad)/pad | solution.py:17
  158.9 1.5 constant_dynamic-slice_fusion
  160.4 0.0 reduce-scatter.3.cloned.1.call-update
  160.4 0.0 reduce-scatter.5.cloned.1.call-start
  160.5 283.9 %reduce-scatter.3.cloned.1.call-done = f32[1,16,512]{2,1,0:T(8,128)} async-done(((f32[64,16,512]{2,1,0:T(8,128)}), f32[1,16,512]{2,1,0:T(8,128)}) %reduce-scatter.3.cloned.1.call-update) | async-done | bytes 32784 | tf_op jit(solution)/shard_map/reduce_scatter | solution.py:19
  444.3 0.0 reduce-scatter.5.cloned.1.call-update
  444.4 28.4 %reduce-scatter.5.cloned.1.call-done = f32[1,16,128]{2,1,0:T(8,128)} async-done(((f32[1,16,512]{2,1,0:T(8,128)}), f32[1,16,128]{2,1,0:T(8,128)}) %reduce-scatter.5.cloned.1.call-update) | async-done | bytes 8208 | tf_op jit(solution)/shard_map/reduce_scatter | solution.py:20
  472.8 1.3 convert_element_type.5
Async XLA Ops:
  6.5 130.8 %all-gather.2.cloned.1.call-start = ((), (), s32[]{:S(2)}) async-start(), calls=%async_computation.2 | async-start | bytes 17039360 | tf_op jit(solution)/shard_map/all_gather | solution.py:13
  7.3 437.1 %reduce-scatter.3.cloned.1.call-start = ((), (), s32[]{:S(2)}) async-start(), calls=%async_computation.3 | async-start | bytes 2129920 | tf_op jit(solution)/shard_map/reduce_scatter | solution.py:19
  160.4 312.3 %reduce-scatter.5.cloned.1.call-start = ((), (), s32[]{:S(2)}) async-start(), calls=%async_computation.4 | async-start | bytes 40960 | tf_op jit(solution)/shard_map/reduce_scatter | solution.py:20
Sparse Core Ops, SparseCore 0:
  9.2 128.1 all-gather.1
  160.6 283.7 reduce-scatter.2
  447.0 25.7 reduce-scatter.4
where the time goes:
time: 481 us
  waiting for transfers between devices  443 us (92%)
  matrix products  21.5 us (4%)
  between operations  13.1 us (3%)
    reduce_scatter x1, waiting for transfers between devices, local(): mine = lax.psum_scatter(shifted, 'tm', scatter_dimension=0, tiled=True)  284 us
    all_gather x1, waiting for transfers between devices, local(): lax.all_gather(samples, 'tm', axis=0, tiled=True)  130 us
    reduce_scatter x1, waiting for transfers between devices, local(): records = lax.psum_scatter(mine, 'floor', scatter_dimension=2, tiled=True)  28.4 us
    pad x1, matrix products, local(): padded = jnp.pad(images, ((blocks, 0), (0, 0), (0, 0)))  21.5 us
  transfers between devices with their start and end apart: 3, of which 3 were waited for; matrix products, arithmetic and copies ran while one was open for 0% of the time, Pallas kernels for 0%

commit v1 on v0

--- a/solution.py
+++ b/solution.py
@@ -16,9 +16,10 @@
     )
     padded = jnp.pad(images, ((blocks, 0), (0, 0), (0, 0)))
     shifted = lax.dynamic_slice_in_dim(padded, blocks - lag, blocks, 0)
-    mine = lax.psum_scatter(shifted, "tm", scatter_dimension=0, tiled=True)
-    records = lax.psum_scatter(mine, "floor", scatter_dimension=2, tiled=True)
-    return records.astype(jnp.bfloat16)
+    mine = lax.all_to_all(shifted, "tm", 0, 0, tiled=True).sum(0)
+    parts = mine.reshape(mine.shape[0], lax.axis_size("floor"), -1).swapaxes(0, 1)
+    records = lax.all_to_all(parts, "floor", 0, 0, tiled=True).sum(0)
+    return records[None].astype(jnp.bfloat16)
 
 
 def solution(mesh):

time: 481 us -> 216 us (0.45)
  waiting for transfers between devices: 443 us -> 131 us
  blocking collectives: 0 us -> 49.2 us
    reduce_scatter x2 -> x0, waiting for transfers between devices: 312 us -> none  [the longest x1 284 us: local(): mine = lax.psum_scatter(shifted, 'tm', scatter_dimension=0, tiled=True)]
    all_to_all x0 -> x2, blocking collectives: none -> 49.2 us  [the longest x1 35.2 us: local(): mine = lax.all_to_all(shifted, 'tm', 0, 0, tiled=True).sum(0)]
  transfers between devices with their start and end apart: 3 -> 1, of which waited for: 3 -> 1; matrix products, arithmetic and copies ran while one was open for 0% -> 0% of each run, Pallas kernels for 0% -> 0%
where the time goes in v1:
time: 216 us
  waiting for transfers between devices  131 us (61%)
  blocking collectives  49.2 us (23%)
  matrix products  21.5 us (10%)
  between operations  13.4 us (6%)
    all_gather x1, waiting for transfers between devices, local(): lax.all_gather(samples, 'tm', axis=0, tiled=True)  130 us
    all_to_all x1, blocking collectives, local(): mine = lax.all_to_all(shifted, 'tm', 0, 0, tiled=True).sum(0)  35.2 us
    pad x1, matrix products, local(): padded = jnp.pad(images, ((blocks, 0), (0, 0), (0, 0)))  21.5 us
    all_to_all x1, blocking collectives, local(): records = lax.all_to_all(parts, 'floor', 0, 0, tiled=True).sum(0)  14 us
  transfers between devices with their start and end apart: 1, of which 1 were waited for; matrix products, arithmetic and copies ran while one was open for 0% of the time, Pallas kernels for 0%

profile of v1, /device:TPU:2, one launch (start us, length us, event | category | flops | bytes accessed | tf_op | source)
XLA Modules:
  0.0 215.9 jit_solution(414119215055207284)
XLA Ops:
  6.5 0.0 all-gather.2.cloned.1.call-start
  6.5 0.7 all-gather.2.cloned.1.call-update
  7.3 130.1 %all-gather.2.cloned.1.call-done = bf16[64,16,8192]{2,1,0:T(8,128)(2,1)} async-done(((bf16[1,16,8192]{2,1,0:T(8,128)(2,1)}), bf16[64,16,8192]{2,1,0:T(8,128)(2,1)}) %all-gather.2.cloned.1.call-update) | async-done | bytes 16777232 | tf_op jit(solution)/shard_map/all_gather | solution.py:13
  137.4 21.5 %fusion = f32[128,16,512]{2,1,0:T(8,128)S(1)} fusion(bf16[64,16,8192]{2,1,0:T(8,128)(2,1)} %all-gather.2.cloned.1.call-done, bf16[1,512,8192]{2,1,0:T(8,128)(2,1)} %param.3), kind=kOutput, calls=%fused_computation | convolution fusion | flops 8589934592 | bytes 29360128 | tf_op jit(solution)/shard_map/jit(_pad)/pad | solution.py:17
  158.9 0.2 constant_dynamic-slice_fusion
  159.1 35.2 %all_to_all.10 = f32[64,16,512]{2,1,0:T(8,128)S(1)} all-to-all(f32[64,16,512]{2,1,0:T(8,128)S(1)} %constant_dynamic-slice_fusion), channel_id=1, replica_groups=mesh['tm'=64,'floor'=4] {'tm'}, dimensions={0} | all-to-all | bytes 4194304 | tf_op jit(solution)/shard_map/all_to_all | solution.py:19
  194.3 0.1 reduce_sum.18
  194.5 14.0 %all_to_all.11 = f32[4,16,128]{2,1,0:T(8,128)S(1)} all-to-all(f32[4,16,128]{2,1,0:T(8,128)S(1)} %copy.3), channel_id=1, replica_groups=mesh['tm'=64,'floor'=4] {'floor'}, dimensions={0} | all-to-all | bytes 65536 | tf_op jit(solution)/shard_map/all_to_all | solution.py:21
  208.5 0.6 reduce_sum.19
  (2 shorter events, 0.0 us)
Async XLA Ops:
  6.5 130.8 %all-gather.2.cloned.1.call-start = ((), (), s32[]{:S(2)}) async-start(), calls=%async_computation.2 | async-start | bytes 17039360 | tf_op jit(solution)/shard_map/all_gather | solution.py:13
Sparse Core Ops, SparseCore 0:
  9.2 128.1 all-gather.1

commit v2 on v1

v2 whole, which is shorter than its diff:
```python
import functools

import jax
import jax.numpy as jnp
from jax import lax
from jax.experimental import pallas as pl
from jax.experimental.pallas import tpu as pltpu
from jax.sharding import PartitionSpec as P

Y, Z, X, CORES = 4, 2, 4, 2
CHIPS = Y * Z * X

XP, XM, YP, YM, ZZ = (1, 0, 0), (3, 0, 0), (0, 1, 0), (0, 3, 0), (0, 0, 1)
LINKS = (XP, XM, YP, YM, ZZ)
SLOTS = (
    ((1, 0, 0), (3, 0, 0), (0, 1, 0), (0, 3, 0), (0, 0, 1)),
    ((1, 1, 0), (3, 3, 0), (0, 2, 0), (1, 3, 0), (3, 0, 1)),
    ((2, 0, 0), (3, 1, 0), (0, 1, 1), (0, 3, 1), (1, 0, 1)),
    ((2, 1, 0), (2, 3, 0), (3, 1, 1), (1, 2, 0), (0, 2, 1)),
    ((1, 1, 1), (3, 3, 1), (3, 2, 0), (1, 3, 1), (2, 0, 1)),
    ((1, 2, 1), (2, 1, 1), (3, 2, 1), (2, 2, 0), (2, 3, 1)),
)
OWN, LAST = (0, 0, 0), (2, 2, 1)
EARLY = (OWN,) + SLOTS[0] + SLOTS[1] + SLOTS[2]
LATE = SLOTS[3] + SLOTS[4] + SLOTS[5] + (LAST,)


def number(y, z, x, core):
    return ((y * Z + z) * X + x) * CORES + core


def moved(d, link):
    return ((d[0] - link[0]) % X, (d[1] - link[1]) % Y, (d[2] - link[2]) % Z)


def pairs(link):
    return [
        (number(y, z, x, c), number((y + link[1]) % Y, (z + link[2]) % Z, (x + link[0]) % X, c))
        for y in range(Y)
        for z in range(Z)
        for x in range(X)
        for c in range(CORES)
    ]


OTHER_CORE = [(2 * i + c, 2 * i + 1 - c) for i in range(CHIPS) for c in range(CORES)]
SAME_CORE = [[2 * i + c for i in range(CHIPS)] for c in range(CORES)]


def gather(block):
    held = {OWN: block}
    for slot in SLOTS:
        for link, d in zip(LINKS, slot):
            held[d] = lax.ppermute(held[moved(d, link)], "tm", pairs(link))
    lanes = block.shape[-1] // 128
    cuts = [128 * (lanes * n // len(LINKS)) for n in range(len(LINKS) + 1)]
    held[LAST] = jnp.concatenate(
        [
            lax.ppermute(held[moved(LAST, link)][:, a:b], "tm", pairs(link))
            for link, a, b in zip(LINKS, cuts, cuts[1:])
        ],
        axis=1,
    )
    return held


def source(me, d):
    chip = me // CORES
    x, z, y = chip % X, (chip // X) % Z, chip // (X * Z)
    return (((y - d[1] + Y) % Y) * Z + (z - d[2] + Z) % Z) * X + (x - d[0] + X) % X


def product(blocks, weights, depth):
    total = None
    for k in range(0, weights.shape[1], depth):
        rows = jnp.concatenate([b[:, k : k + depth] for b in blocks], axis=0)
        term = lax.dot_general(
            rows,
            weights[:, k : k + depth],
            (((1,), (1,)), ((), ())),
            preferred_element_type=jnp.float32,
        )
        total = term if total is None else total + term
    return total


def early_kernel(count, steps, depth, *refs):
    blocks, (own, other, out) = refs[:count], refs[count:]
    n = pl.program_id(0)

    @pl.when(n < steps)
    def _():
        out[0] = product(blocks, own, depth)

    @pl.when(n >= steps)
    def _():
        out[0] = product(blocks, other, depth)


def late_kernel(count, steps, depth, *refs):
    me_ref, refs = refs[0], refs[1:]
    blocks, (own, other, early, keep, send) = refs[:count], refs[count:]
    n = pl.program_id(0)
    me = me_ref[0]
    core, chip = me % CORES, me // CORES
    k = blocks[0].shape[0]
    width = own.shape[0]

    def place(which, rows, offsets, columns):
        first = chip + (core if which == 0 else 0)
        keeps = core == which
        for b, d in enumerate(offsets):
            to = source(me, d) + first

            @pl.when(jnp.logical_and(to < CHIPS, keeps))
            def _():
                keep[to, :, columns] = rows[b * k : (b + 1) * k]

            @pl.when(jnp.logical_and(to < CHIPS, jnp.logical_not(keeps)))
            def _():
                send[to, :, columns] = rows[b * k : (b + 1) * k]

    @pl.when(n == 0)
    def _():
        keep[...] = jnp.zeros_like(keep)
        send[...] = jnp.zeros_like(send)
        for which in range(2):
            place(which, early.at[which], EARLY, slice(None))

    for which, weights in enumerate((own, other)):
        for step in range(steps):

            @pl.when(n == which * steps + step)
            def _():
                place(
                    which,
                    product(blocks, weights, depth),
                    LATE,
                    slice(step * width, (step + 1) * width),
                )


def specs(blocks, own, tile):
    k, p = blocks[0].shape
    steps = own.shape[0] // tile
    whole = pl.BlockSpec((k, p), lambda n, *_: (0, 0))
    first = pl.BlockSpec((tile, p), lambda n, *_: (jnp.minimum(n, steps - 1), 0))
    second = pl.BlockSpec((tile, p), lambda n, *_: (jnp.maximum(n - steps, 0), 0))
    return steps, [whole] * len(blocks) + [first, second]


def cost(blocks, own):
    k, p = blocks[0].shape
    rows, s = k * len(blocks), own.shape[0]
    return pl.CostEstimate(
        flops=4 * rows * p * s, bytes_accessed=2 * p * (rows + 2 * s) + 8 * rows * s, transcendentals=0
    )


TILE, DEPTH, VMEM = 256, 2048, 48 << 20


def multiply_early(blocks, own, other):
    rows, s = blocks[0].shape[0] * len(blocks), own.shape[0]
    steps, in_specs = specs(blocks, own, TILE)
    return pl.pallas_call(
        functools.partial(early_kernel, len(blocks), steps, DEPTH),
        out_shape=jax.ShapeDtypeStruct((2, rows, s), jnp.float32),
        grid=(2 * steps,),
        in_specs=in_specs,
        out_specs=pl.BlockSpec((1, rows, TILE), lambda n: (n // steps, 0, n % steps)),
        compiler_params=pltpu.CompilerParams(vmem_limit_bytes=VMEM),
        cost_estimate=cost(blocks, own),
        name="early",
    )(*blocks, own, other)


def multiply_late(me, blocks, own, other, early):
    k, s = blocks[0].shape[0], own.shape[0]
    steps, in_specs = specs(blocks, own, TILE)
    out = jax.ShapeDtypeStruct((CHIPS, k, s), jnp.float32)
    out_spec = pl.BlockSpec((CHIPS, k, s), lambda n, *_: (0, 0, 0))
    return pl.pallas_call(
        functools.partial(late_kernel, len(blocks), steps, DEPTH),
        out_shape=[out, out],
        grid_spec=pltpu.PrefetchScalarGridSpec(
            num_scalar_prefetch=1,
            grid=(2 * steps,),
            in_specs=in_specs + [pl.BlockSpec(early.shape, lambda n, *_: (0, 0, 0))],
            out_specs=[out_spec, out_spec],
        ),
        compiler_params=pltpu.CompilerParams(vmem_limit_bytes=VMEM),
        cost_estimate=cost(blocks, own),
        name="late",
    )(me, *blocks, own, other, early)


def local(samples, operator):
    me = lax.axis_index("tm")
    own = operator[0]
    held = gather(samples[0])
    other = lax.ppermute(own, "tm", OTHER_CORE)
    early = multiply_early([held[d] for d in EARLY], own, other)
    keep, send = multiply_late(me.reshape(1), [held[d] for d in LATE], own, other, early)
    both = keep + lax.ppermute(send, "tm", OTHER_CORE)
    mine = lax.all_to_all(both, "tm", 0, 0, tiled=True, axis_index_groups=SAME_CORE).sum(0)
    parts = mine.reshape(mine.shape[0], lax.axis_size("floor"), -1).swapaxes(0, 1)
    records = lax.all_to_all(parts, "floor", 0, 0, tiled=True).sum(0)
    return records[None].astype(jnp.bfloat16)


def solution(mesh):
    placed = (P("tm", None, "floor"), P("tm", None, "floor"))
    return jax.shard_map(
        local, mesh=mesh, in_specs=placed, out_specs=P("tm", None, "floor"), check_vma=False
    )
```

time: 216 us -> 144 us (0.67)
  waiting for transfers between devices: 131 us -> 29.2 us
  starting transfers between devices: 0.01 us -> 48.4 us
  Pallas kernels: 0 us -> 21.9 us
  matrix products: 21.5 us -> 0 us
  between operations: 13.4 us -> 0.15 us
  blocking collectives: 49.2 us -> 39.6 us
  local copies, waits for them, and re-layouts: 0.21 us -> 3.7 us
    all_gather x1 -> x0, waiting for transfers between devices: 130 us -> none  [local(): lax.all_gather(samples, 'tm', axis=0, tiled=True)]
    ppermute x0 -> x37, starting transfers between devices: none -> 48.4 us  [the longest x30 41.1 us: gather(): held[d] = lax.ppermute(held[moved(d, link)], 'tm', pairs(link))]
    ppermute x0 -> x37, waiting for transfers between devices: none -> 29.2 us  [the longest x30 21.5 us: gather(): held[d] = lax.ppermute(held[moved(d, link)], 'tm', pairs(link))]
    pallas_call x0 -> x2, Pallas kernels: none -> 21.9 us  [the longest x1 12.1 us: multiply_late(): pl.pallas_call(functools.partial(late_kernel, len(blocks), steps, DEPTH),...]
    pad x1 -> x0, matrix products: 21.5 us -> none  [local(): padded = jnp.pad(images, ((blocks, 0), (0, 0), (0, 0)))]
    all_to_all x1, blocking collectives: 35.2 us -> 24.3 us  [local(): lax.all_to_all(both, 'tm', 0, 0, tiled=True, axis_index_groups=SAME_CORE)]
    unnamed x0 -> x12, local copies, waits for them, and re-layouts: none -> 3.65 us
  transfers between devices with their start and end apart: 1 -> 37, of which waited for: 1 -> 11; matrix products, arithmetic and copies ran while one was open for 0% -> 0% of each run, Pallas kernels for 0% -> 7%
where the time goes in v2:
time: 144 us
  starting transfers between devices  48.4 us (34%)
  blocking collectives  39.6 us (28%)
  waiting for transfers between devices  29.2 us (20%)
  Pallas kernels  21.9 us (15%)
  local copies, waits for them, and re-layouts  3.7 us (3%)
    ppermute x30, starting transfers between devices, gather(): held[d] = lax.ppermute(held[moved(d, link)], 'tm', pairs(link))  41.1 us
    all_to_all x1, blocking collectives, local(): lax.all_to_all(both, 'tm', 0, 0, tiled=True, axis_index_groups=SAME_CORE)  24.3 us
    ppermute x30, waiting for transfers between devices, gather(): held[d] = lax.ppermute(held[moved(d, link)], 'tm', pairs(link))  21.5 us
    all_to_all x1, blocking collectives, local(): records = lax.all_to_all(parts, 'floor', 0, 0, tiled=True).sum(0)  15.3 us
    pallas_call x1, Pallas kernels, multiply_late(): pl.pallas_call(functools.partial(late_kernel, len(blocks), steps, DEPTH),...  12.1 us
    pallas_call x1, Pallas kernels, multiply_early(): pl.pallas_call(functools.partial(early_kernel, len(blocks), steps, DEPTH)...  9.88 us
    ppermute x5, starting transfers between devices, gather(): lax.ppermute(held[moved(LAST, link)][:, a:b], 'tm', pairs(link))  7.27 us
    ppermute x5, waiting for transfers between devices, gather(): lax.ppermute(held[moved(LAST, link)][:, a:b], 'tm', pairs(link))  4.83 us
  transfers between devices with their start and end apart: 37, of which 11 were waited for; matrix products, arithmetic and copies ran while one was open for 0% of the time, Pallas kernels for 7%

profile of v2, /device:TPU:2, one launch (start us, length us, event | category | flops | bytes accessed | tf_op | source)
XLA Modules:
  0.0 143.8 jit_solution(11638823503903707476)
XLA Ops:
  0.0 0.0 collective-permute-start.35
  0.0 1.6 %collective-permute-start = (bf16[16,8192]{1,0:T(8,128)(2,1)}, bf16[16,8192]{1,0:T(8,128)(2,1)S(1)}, u32[]{:S(2)}, u32[]{:S(2)}) collective-permute-start(bf16[16,8192]{1,0:T(8,128)(2,1)} %bitcast.7), channel_id=1, source_target_pairs={{0,64},{4,68},{8,72},{12,76},{16,80},{20,84},{24,88},{28,92},{32,9... | collective-permute-start | bytes 786440 | tf_op jit(solution)/shard_map/ppermute | solution.py:54
  1.6 0.7 collective-permute-start.6
  2.3 3.2 %collective-permute-start.3 = (bf16[16,8192]{1,0:T(8,128)(2,1)}, bf16[16,8192]{1,0:T(8,128)(2,1)S(1)}, u32[]{:S(2)}, u32[]{:S(2)}) collective-permute-start(bf16[16,8192]{1,0:T(8,128)(2,1)} %bitcast.9), channel_id=1, source_target_pairs={{0,192},{4,196},{8,200},{12,204},{16,208},{20,212},{24,216},{28,22... | collective-permute-start | bytes 786440 | tf_op jit(solution)/shard_map/ppermute | solution.py:54
  5.5 4.7 %collective-permute-done.refs_3_ = bf16[16,8192]{1,0:T(8,128)(2,1)S(1)} collective-permute-done((bf16[16,8192]{1,0:T(8,128)(2,1)}, bf16[16,8192]{1,0:T(8,128)(2,1)S(1)}, u32[]{:S(2)}, u32[]{:S(2)}) %collective-permute-start) | collective-permute-done | bytes 262176 | tf_op jit(solution)/shard_map/ppermute | solution.py:54
  10.2 0.3 collective-permute-start.12
  10.5 0.0 collective-permute-done.6.refs_2_
  10.5 1.9 %collective-permute-start.7 = (bf16[16,8192]{1,0:T(8,128)(2,1)S(1)}, bf16[16,8192]{1,0:T(8,128)(2,1)S(1)}, u32[]{:S(2)}, u32[]{:S(2)}) collective-permute-start(bf16[16,8192]{1,0:T(8,128)(2,1)S(1)} %collective-permute-done.6.refs_2_), channel_id=1, source_target_pairs={{0,32},{4,36},{8,40},{12,44},{16,48},{20,52},{24,56},{28,60},{32,0... | collective-permute-start | bytes 786440 | tf_op jit(solution)/shard_map/ppermute | solution.py:54
  12.4 0.0 collective-permute-done.3.refs_4_
  12.4 0.8 collective-permute-start.4
  13.2 6.2 %collective-permute-done.12.refs_8_ = bf16[16,8192]{1,0:T(8,128)(2,1)S(1)} collective-permute-done((bf16[16,8192]{1,0:T(8,128)(2,1)S(1)}, bf16[16,8192]{1,0:T(8,128)(2,1)S(1)}, u32[]{:S(2)}, u32[]{:S(2)}) %collective-permute-start.12) | collective-permute-done | bytes 262176 | tf_op jit(solution)/shard_map/ppermute | solution.py:54
  19.4 1.9 %collective-permute-start.13 = (bf16[16,8192]{1,0:T(8,128)(2,1)S(1)}, bf16[16,8192]{1,0:T(8,128)(2,1)S(1)}, u32[]{:S(2)}, u32[]{:S(2)}) collective-permute-start(bf16[16,8192]{1,0:T(8,128)(2,1)S(1)} %collective-permute-done.12.refs_8_), channel_id=1, source_target_pairs={{0,32},{4,36},{8,40},{12,44},{16,48},{20,52},{24,56},{28,60},{32,0... | collective-permute-start | bytes 786440 | tf_op jit(solution)/shard_map/ppermute | solution.py:54
  21.3 0.0 collective-permute-done.7.refs_10_
  21.3 0.0 collective-permute-start.8
  21.3 1.5 %collective-permute-start.9 = (bf16[16,8192]{1,0:T(8,128)(2,1)}, bf16[16,8192]{1,0:T(8,128)(2,1)}, u32[]{:S(2)}, u32[]{:S(2)}) collective-permute-start(bf16[16,8192]{1,0:T(8,128)(2,1)} %bitcast.10), channel_id=1, source_target_pairs={{0,8},{4,12},{8,16},{12,20},{16,24},{20,28},{24,0},{28,4},{32,40},... | collective-permute-start | bytes 786440 | tf_op jit(solution)/shard_map/ppermute | solution.py:54
  22.8 0.0 collective-permute-done.4.refs_7_
  22.8 0.5 collective-permute-start.5
  23.4 0.7 copy-done.2
  24.1 2.6 %collective-permute-done.13.refs_5_ = bf16[16,8192]{1,0:T(8,128)(2,1)S(1)} collective-permute-done((bf16[16,8192]{1,0:T(8,128)(2,1)S(1)}, bf16[16,8192]{1,0:T(8,128)(2,1)S(1)}, u32[]{:S(2)}, u32[]{:S(2)}) %collective-permute-start.13) | collective-permute-done | bytes 262176 | tf_op jit(solution)/shard_map/ppermute | solution.py:54
  26.7 1.5 %collective-permute-start.25 = (bf16[16,8192]{1,0:T(8,128)(2,1)S(1)}, bf16[16,8192]{1,0:T(8,128)(2,1)S(1)}, u32[]{:S(2)}, u32[]{:S(2)}) collective-permute-start(bf16[16,8192]{1,0:T(8,128)(2,1)S(1)} %collective-permute-done.13.refs_5_), channel_id=1, source_target_pairs={{0,8},{4,12},{8,16},{12,20},{16,24},{20,28},{24,0},{28,4},{32,40},... | collective-permute-start | bytes 786440 | tf_op jit(solution)/shard_map/ppermute | solution.py:54
  28.2 1.2 collective-permute-done.8.refs_3_
  29.4 0.0 collective-permute-start.27
  29.4 0.0 collective-permute-done.9.refs_1_
  29.4 0.8 collective-permute-start.26
  30.3 0.0 collective-permute-done.5.refs_2_
  30.3 2.5 %collective-permute-start.29 = (bf16[16,8192]{1,0:T(8,128)(2,1)S(1)}, bf16[16,8192]{1,0:T(8,128)(2,1)S(1)}, u32[]{:S(2)}, u32[]{:S(2)}) collective-permute-start(bf16[16,8192]{1,0:T(8,128)(2,1)S(1)} %collective-permute-done.5.refs_2_), channel_id=1, source_target_pairs={{0,32},{4,36},{8,40},{12,44},{16,48},{20,52},{24,56},{28,60},{32,0... | collective-permute-start | bytes 786440 | tf_op jit(solution)/shard_map/ppermute | solution.py:54
  32.8 1.2 collective-permute-done.25.refs_11_
  34.0 3.3 %collective-permute-start.28 = (bf16[16,8192]{1,0:T(8,128)(2,1)S(1)}, bf16[16,8192]{1,0:T(8,128)(2,1)S(1)}, u32[]{:S(2)}, u32[]{:S(2)}) collective-permute-start(bf16[16,8192]{1,0:T(8,128)(2,1)S(1)} %collective-permute-done.5.refs_2_), channel_id=1, source_target_pairs={{0,192},{4,196},{8,200},{12,204},{16,208},{20,212},{24,216},{28,22... | collective-permute-start | bytes 786440 | tf_op jit(solution)/shard_map/ppermute | solution.py:54
  37.4 0.0 collective-permute-done.27.refs_13_
  37.4 0.2 collective-permute-start.14
  37.6 1.5 %collective-permute-start.30 = (bf16[16,1536]{1,0:T(8,128)(2,1)S(1)}, bf16[16,1536]{1,0:T(8,128)(2,1)S(1)}, u32[]{:S(2)}, u32[]{:S(2)}) collective-permute-start(bf16[16,1536]{1,0:T(8,128)(2,1)S(1)} %slice.20), channel_id=1, source_target_pairs={{0,8},{4,12},{8,16},{12,20},{16,24},{20,28},{24,0},{28,4},{32,40},... | collective-permute-start | bytes 147464 | tf_op jit(solution)/shard_map/ppermute | solution.py:59
  39.0 0.0 collective-permute-done.29.refs_15_
  39.0 1.2 collective-permute-start.1
  40.2 1.0 collective-permute-done.28.refs_14_
  41.3 3.7 %collective-permute-start.10 = (bf16[16,8192]{1,0:T(8,128)(2,1)}, bf16[16,8192]{1,0:T(8,128)(2,1)}, u32[]{:S(2)}, u32[]{:S(2)}) collective-permute-start(bf16[16,8192]{1,0:T(8,128)(2,1)} %collective-permute-done.9.refs_1_), channel_id=1, source_target_pairs={{0,192},{4,196},{8,200},{12,204},{16,208},{20,212},{24,216},{28,22... | collective-permute-start | bytes 786440 | tf_op jit(solution)/shard_map/ppermute | solution.py:54
  45.0 1.7 %collective-permute-start.19 = (bf16[16,8192]{1,0:T(8,128)(2,1)S(1)}, bf16[16,8192]{1,0:T(8,128)(2,1)S(1)}, u32[]{:S(2)}, u32[]{:S(2)}) collective-permute-start(bf16[16,8192]{1,0:T(8,128)(2,1)S(1)} %collective-permute-done.refs_3_), channel_id=1, source_target_pairs={{0,24},{4,28},{8,0},{12,4},{16,8},{20,12},{24,16},{28,20},{32,56},... | collective-permute-start | bytes 786440 | tf_op jit(solution)/shard_map/ppermute | solution.py:54
  46.8 2.2 %collective-permute-start.31 = (bf16[16,1664]{1,0:T(8,128)(2,1)S(1)}, bf16[16,1664]{1,0:T(8,128)(2,1)S(1)}, u32[]{:S(2)}, u32[]{:S(2)}) collective-permute-start(bf16[16,1664]{1,0:T(8,128)(2,1)S(1)} %slice.21), channel_id=1, source_target_pairs={{0,24},{4,28},{8,0},{12,4},{16,8},{20,12},{24,16},{28,20},{32,56},... | collective-permute-start | bytes 159752 | tf_op jit(solution)/shard_map/ppermute | solution.py:59
  49.0 0.8 collective-permute-start.21
  49.9 0.4 collective-permute-start.23
  50.3 1.8 %collective-permute-done.31 = bf16[16,1664]{1,0:T(8,128)(2,1)S(1)} collective-permute-done((bf16[16,1664]{1,0:T(8,128)(2,1)S(1)}, bf16[16,1664]{1,0:T(8,128)(2,1)S(1)}, u32[]{:S(2)}, u32[]{:S(2)}) %collective-permute-start.31) | collective-permute-done | bytes 53280 | tf_op jit(solution)/shard_map/ppermute | solution.py:59
  52.1 3.3 %collective-permute-start.33 = (bf16[16,1664]{1,0:T(8,128)(2,1)S(1)}, bf16[16,1664]{1,0:T(8,128)(2,1)S(1)}, u32[]{:S(2)}, u32[]{:S(2)}) collective-permute-start(bf16[16,1664]{1,0:T(8,128)(2,1)S(1)} %slice.23), channel_id=1, source_target_pairs={{0,192},{4,196},{8,200},{12,204},{16,208},{20,212},{24,216},{28,22... | collective-permute-start | bytes 159752 | tf_op jit(solution)/shard_map/ppermute | solution.py:59
  55.4 2.6 %collective-permute-done.32 = bf16[16,1664]{1,0:T(8,128)(2,1)S(1)} collective-permute-done((bf16[16,1664]{1,0:T(8,128)(2,1)S(1)}, bf16[16,1664]{1,0:T(8,128)(2,1)S(1)}, u32[]{:S(2)}, u32[]{:S(2)}) %collective-permute-start.32) | collective-permute-done | bytes 53280 | tf_op jit(solution)/shard_map/ppermute | solution.py:59
  57.9 0.2 collective-permute-start.34
  58.2 0.1 collective-permute-start.15
  58.3 3.2 %collective-permute-start.17 = (bf16[16,8192]{1,0:T(8,128)(2,1)}, bf16[16,8192]{1,0:T(8,128)(2,1)S(1)}, u32[]{:S(2)}, u32[]{:S(2)}) collective-permute-start(bf16[16,8192]{1,0:T(8,128)(2,1)} %collective-permute-done.14.refs_5_), channel_id=1, source_target_pairs={{0,192},{4,196},{8,200},{12,204},{16,208},{20,212},{24,216},{28,22... | collective-permute-start | bytes 786440 | tf_op jit(solution)/shard_map/ppermute | solution.py:54
  61.5 0.1 collective-permute-start.11
  61.6 0.5 collective-permute-done.34
  62.1 1.7 %collective-permute-start.2 = (bf16[16,8192]{1,0:T(8,128)(2,1)}, bf16[16,8192]{1,0:T(8,128)(2,1)S(1)}, u32[]{:S(2)}, u32[]{:S(2)}) collective-permute-start(bf16[16,8192]{1,0:T(8,128)(2,1)} %collective-permute-done.1.refs_6_), channel_id=1, source_target_pairs={{0,8},{4,12},{8,16},{12,20},{16,24},{20,28},{24,0},{28,4},{32,40},... | collective-permute-start | bytes 786440 | tf_op jit(solution)/shard_map/ppermute | solution.py:54
  63.8 4.5 %collective-permute-done.15.refs_13_ = bf16[16,8192]{1,0:T(8,128)(2,1)S(1)} collective-permute-done((bf16[16,8192]{1,0:T(8,128)(2,1)}, bf16[16,8192]{1,0:T(8,128)(2,1)S(1)}, u32[]{:S(2)}, u32[]{:S(2)}) %collective-permute-start.15) | collective-permute-done | bytes 262176 | tf_op jit(solution)/shard_map/ppermute | solution.py:54
  68.4 3.4 %collective-permute-start.22 = (bf16[16,8192]{1,0:T(8,128)(2,1)S(1)}, bf16[16,8192]{1,0:T(8,128)(2,1)S(1)}, u32[]{:S(2)}, u32[]{:S(2)}) collective-permute-start(bf16[16,8192]{1,0:T(8,128)(2,1)S(1)} %collective-permute-done.21.refs_15_), channel_id=1, source_target_pairs={{0,192},{4,196},{8,200},{12,204},{16,208},{20,212},{24,216},{28,22... | collective-permute-start | bytes 786440 | tf_op jit(solution)/shard_map/ppermute | solution.py:54
  71.8 1.4 %collective-permute-start.24 = (bf16[16,8192]{1,0:T(8,128)(2,1)S(1)}, bf16[16,8192]{1,0:T(8,128)(2,1)S(1)}, u32[]{:S(2)}, u32[]{:S(2)}) collective-permute-start(bf16[16,8192]{1,0:T(8,128)(2,1)S(1)} %collective-permute-done.23.refs_11_), channel_id=1, source_target_pairs={{0,32},{4,36},{8,40},{12,44},{16,48},{20,52},{24,56},{28,60},{32,0... | collective-permute-start | bytes 786440 | tf_op jit(solution)/shard_map/ppermute | solution.py:54
  73.3 1.0 collective-permute-start.16
  74.3 1.3 collective-permute-start.18
  75.6 0.9 copy-done.1
  76.5 0.9 copy-done.3
  77.5 9.9 %early.1.refs_19_ = f32[2,256,512]{2,1,0:T(8,128)S(1)} custom-call(bf16[16,8192]{1,0:T(8,128)(2,1)S(1)} %bitcast.12, bf16[16,8192]{1,0:T(8,128)(2,1)} %collective-permute-done.9.refs_1_, bf16[16,8192]{1,0:T(8,128)(2,1)S(1)} %collective-permute-done.6.refs_2_, bf16[16,8192]{1,0:T(8,128)(2,1)S(1)} %collective-permute-done.refs_3_, ...), custom_call_target="tpu_custom_call" | custom-call | flops 4294967296 | bytes 22020096 | tf_op jit(solution)/shard_map/early/pallas_call | solution.py:166
  87.4 1.0 copy-done
  88.4 12.1 %late.1 = (f32[32,16,512]{2,1,0:T(8,128)S(1)}, f32[32,16,512]{2,1,0:T(8,128)}) custom-call(s32[1]{0:T(128)} %bitcast.refs_0_, bf16[16,8192]{1,0:T(8,128)(2,1)S(1)} %collective-permute-done.2.refs_1_, bf16[16,8192]{1,0:T(8,128)(2,1)S(1)} %collective-permute-done.5.refs_2_, bf16[16,8192]{1,0:T(8,128)(2,1)S(1)} %collective-permute-done.8.refs_3_, ...), custom_call_target="tpu_custom_call" | custom-call | flops 4294967296 | bytes 22020096 | tf_op jit(solution)/shard_map/late/pallas_call | solution.py:183
  100.5 2.9 %collective-permute-done.36 = f32[32,16,512]{2,1,0:T(8,128)S(1)} collective-permute-done((f32[32,16,512]{2,1,0:T(8,128)}, f32[32,16,512]{2,1,0:T(8,128)S(1)}, u32[]{:S(2)}, u32[]{:S(2)}) %collective-permute-start.36) | collective-permute-done | bytes 1048608 | tf_op jit(solution)/shard_map/ppermute | solution.py:205
  103.3 0.2 add.3
  103.6 24.3 %all_to_all.10 = f32[32,16,512]{2,1,0:T(8,128)S(1)} all-to-all(f32[32,16,512]{2,1,0:T(8,128)S(1)} %add.3), channel_id=1, replica_groups={{0,8,16,24,32,40,48,56,64,72,80,88,96,104,112,120,128,136,144,152,160,1..., dimensions={0} | all-to-all | bytes 2097152 | tf_op jit(solution)/shard_map/all_to_all | solution.py:206
  127.9 0.1 reduce_sum.18
  128.0 15.3 %all_to_all.11 = f32[4,16,128]{2,1,0:T(8,128)S(1)} all-to-all(f32[4,16,128]{2,1,0:T(8,128)S(1)} %copy.3), channel_id=1, replica_groups=mesh['tm'=64,'floor'=4] {'floor'}, dimensions={0} | all-to-all | bytes 65536 | tf_op jit(solution)/shard_map/all_to_all | solution.py:208
  143.2 0.6 reduce_sum.19
  (37 shorter events, 0.2 us)
Async XLA Ops:
  0.0 74.3 %collective-permute-start.35 = (bf16[512,8192]{1,0:T(8,128)(2,1)}, bf16[512,8192]{1,0:T(8,128)(2,1)}, u32[]{:S(2)}, u32[]{:S(2)}) collective-permute-start(bf16[512,8192]{1,0:T(8,128)(2,1)} %bitcast.13), channel_id=1, source_target_pairs={{0,4},{4,0},{8,12},{12,8},{16,20},{20,16},{24,28},{28,24},{32,36},... | collective-permute-start | bytes 25165832 | tf_op jit(solution)/shard_map/ppermute | solution.py:202
  0.0 10.2 %collective-permute-start = (bf16[16,8192]{1,0:T(8,128)(2,1)}, bf16[16,8192]{1,0:T(8,128)(2,1)S(1)}, u32[]{:S(2)}, u32[]{:S(2)}) collective-permute-start(bf16[16,8192]{1,0:T(8,128)(2,1)} %bitcast.7), channel_id=1, source_target_pairs={{0,64},{4,68},{8,72},{12,76},{16,80},{20,84},{24,88},{28,92},{32,9... | collective-permute-start | bytes 786440 | tf_op jit(solution)/shard_map/ppermute | solution.py:54
  1.6 8.9 %collective-permute-start.6 = (bf16[16,8192]{1,0:T(8,128)(2,1)}, bf16[16,8192]{1,0:T(8,128)(2,1)S(1)}, u32[]{:S(2)}, u32[]{:S(2)}) collective-permute-start(bf16[16,8192]{1,0:T(8,128)(2,1)} %bitcast.8), channel_id=1, source_target_pairs={{0,24},{4,28},{8,0},{12,4},{16,8},{20,12},{24,16},{28,20},{32,56},... | collective-permute-start | bytes 786440 | tf_op jit(solution)/shard_map/ppermute | solution.py:54
  2.3 10.2 %collective-permute-start.3 = (bf16[16,8192]{1,0:T(8,128)(2,1)}, bf16[16,8192]{1,0:T(8,128)(2,1)S(1)}, u32[]{:S(2)}, u32[]{:S(2)}) collective-permute-start(bf16[16,8192]{1,0:T(8,128)(2,1)} %bitcast.9), channel_id=1, source_target_pairs={{0,192},{4,196},{8,200},{12,204},{16,208},{20,212},{24,216},{28,22... | collective-permute-start | bytes 786440 | tf_op jit(solution)/shard_map/ppermute | solution.py:54
  10.2 9.2 %collective-permute-start.12 = (bf16[16,8192]{1,0:T(8,128)(2,1)S(1)}, bf16[16,8192]{1,0:T(8,128)(2,1)S(1)}, u32[]{:S(2)}, u32[]{:S(2)}) collective-permute-start(bf16[16,8192]{1,0:T(8,128)(2,1)S(1)} %collective-permute-done.refs_3_), channel_id=1, source_target_pairs={{0,64},{4,68},{8,72},{12,76},{16,80},{20,84},{24,88},{28,92},{32,9... | collective-permute-start | bytes 786440 | tf_op jit(solution)/shard_map/ppermute | solution.py:54
  10.5 10.8 %collective-permute-start.7 = (bf16[16,8192]{1,0:T(8,128)(2,1)S(1)}, bf16[16,8192]{1,0:T(8,128)(2,1)S(1)}, u32[]{:S(2)}, u32[]{:S(2)}) collective-permute-start(bf16[16,8192]{1,0:T(8,128)(2,1)S(1)} %collective-permute-done.6.refs_2_), channel_id=1, source_target_pairs={{0,32},{4,36},{8,40},{12,44},{16,48},{20,52},{24,56},{28,60},{32,0... | collective-permute-start | bytes 786440 | tf_op jit(solution)/shard_map/ppermute | solution.py:54
  12.4 10.4 %collective-permute-start.4 = (bf16[16,8192]{1,0:T(8,128)(2,1)S(1)}, bf16[16,8192]{1,0:T(8,128)(2,1)S(1)}, u32[]{:S(2)}, u32[]{:S(2)}) collective-permute-start(bf16[16,8192]{1,0:T(8,128)(2,1)S(1)} %collective-permute-done.3.refs_4_), channel_id=1, source_target_pairs={{0,24},{4,28},{8,0},{12,4},{16,8},{20,12},{24,16},{28,20},{32,56},... | collective-permute-start | bytes 786440 | tf_op jit(solution)/shard_map/ppermute | solution.py:54
  19.4 7.3 %collective-permute-start.13 = (bf16[16,8192]{1,0:T(8,128)(2,1)S(1)}, bf16[16,8192]{1,0:T(8,128)(2,1)S(1)}, u32[]{:S(2)}, u32[]{:S(2)}) collective-permute-start(bf16[16,8192]{1,0:T(8,128)(2,1)S(1)} %collective-permute-done.12.refs_8_), channel_id=1, source_target_pairs={{0,32},{4,36},{8,40},{12,44},{16,48},{20,52},{24,56},{28,60},{32,0... | collective-permute-start | bytes 786440 | tf_op jit(solution)/shard_map/ppermute | solution.py:54
  21.3 8.1 %collective-permute-start.8 = (bf16[16,8192]{1,0:T(8,128)(2,1)S(1)}, bf16[16,8192]{1,0:T(8,128)(2,1)S(1)}, u32[]{:S(2)}, u32[]{:S(2)}) collective-permute-start(bf16[16,8192]{1,0:T(8,128)(2,1)S(1)} %collective-permute-done.7.refs_10_), channel_id=1, source_target_pairs={{0,64},{4,68},{8,72},{12,76},{16,80},{20,84},{24,88},{28,92},{32,9... | collective-permute-start | bytes 786440 | tf_op jit(solution)/shard_map/ppermute | solution.py:54
  21.3 8.1 %collective-permute-start.9 = (bf16[16,8192]{1,0:T(8,128)(2,1)}, bf16[16,8192]{1,0:T(8,128)(2,1)}, u32[]{:S(2)}, u32[]{:S(2)}) collective-permute-start(bf16[16,8192]{1,0:T(8,128)(2,1)} %bitcast.10), channel_id=1, source_target_pairs={{0,8},{4,12},{8,16},{12,20},{16,24},{20,28},{24,0},{28,4},{32,40},... | collective-permute-start | bytes 786440 | tf_op jit(solution)/shard_map/ppermute | solution.py:54
  22.8 7.4 %collective-permute-start.5 = (bf16[16,8192]{1,0:T(8,128)(2,1)S(1)}, bf16[16,8192]{1,0:T(8,128)(2,1)S(1)}, u32[]{:S(2)}, u32[]{:S(2)}) collective-permute-start(bf16[16,8192]{1,0:T(8,128)(2,1)S(1)} %collective-permute-done.4.refs_7_), channel_id=1, source_target_pairs={{0,24},{4,28},{8,0},{12,4},{16,8},{20,12},{24,16},{28,20},{32,56},... | collective-permute-start | bytes 786440 | tf_op jit(solution)/shard_map/ppermute | solution.py:54
  23.4 0.7 copy-start.2
  26.7 7.3 %collective-permute-start.25 = (bf16[16,8192]{1,0:T(8,128)(2,1)S(1)}, bf16[16,8192]{1,0:T(8,128)(2,1)S(1)}, u32[]{:S(2)}, u32[]{:S(2)}) collective-permute-start(bf16[16,8192]{1,0:T(8,128)(2,1)S(1)} %collective-permute-done.13.refs_5_), channel_id=1, source_target_pairs={{0,8},{4,12},{8,16},{12,20},{16,24},{20,28},{24,0},{28,4},{32,40},... | collective-permute-start | bytes 786440 | tf_op jit(solution)/shard_map/ppermute | solution.py:54
  29.4 8.0 %collective-permute-start.27 = (bf16[16,8192]{1,0:T(8,128)(2,1)S(1)}, bf16[16,8192]{1,0:T(8,128)(2,1)S(1)}, u32[]{:S(2)}, u32[]{:S(2)}) collective-permute-start(bf16[16,8192]{1,0:T(8,128)(2,1)S(1)} %collective-permute-done.8.refs_3_), channel_id=1, source_target_pairs={{0,64},{4,68},{8,72},{12,76},{16,80},{20,84},{24,88},{28,92},{32,9... | collective-permute-start | bytes 786440 | tf_op jit(solution)/shard_map/ppermute | solution.py:54
  29.4 8.1 %collective-permute-start.26 = (bf16[16,8192]{1,0:T(8,128)(2,1)S(1)}, bf16[16,8192]{1,0:T(8,128)(2,1)S(1)}, u32[]{:S(2)}, u32[]{:S(2)}) collective-permute-start(bf16[16,8192]{1,0:T(8,128)(2,1)S(1)} %collective-permute-done.8.refs_3_), channel_id=1, source_target_pairs={{0,24},{4,28},{8,0},{12,4},{16,8},{20,12},{24,16},{28,20},{32,56},... | collective-permute-start | bytes 786440 | tf_op jit(solution)/shard_map/ppermute | solution.py:54
  30.3 8.8 %collective-permute-start.29 = (bf16[16,8192]{1,0:T(8,128)(2,1)S(1)}, bf16[16,8192]{1,0:T(8,128)(2,1)S(1)}, u32[]{:S(2)}, u32[]{:S(2)}) collective-permute-start(bf16[16,8192]{1,0:T(8,128)(2,1)S(1)} %collective-permute-done.5.refs_2_), channel_id=1, source_target_pairs={{0,32},{4,36},{8,40},{12,44},{16,48},{20,52},{24,56},{28,60},{32,0... | collective-permute-start | bytes 786440 | tf_op jit(solution)/shard_map/ppermute | solution.py:54
  34.0 7.2 %collective-permute-start.28 = (bf16[16,8192]{1,0:T(8,128)(2,1)S(1)}, bf16[16,8192]{1,0:T(8,128)(2,1)S(1)}, u32[]{:S(2)}, u32[]{:S(2)}) collective-permute-start(bf16[16,8192]{1,0:T(8,128)(2,1)S(1)} %collective-permute-done.5.refs_2_), channel_id=1, source_target_pairs={{0,192},{4,196},{8,200},{12,204},{16,208},{20,212},{24,216},{28,22... | collective-permute-start | bytes 786440 | tf_op jit(solution)/shard_map/ppermute | solution.py:54
  37.4 7.6 %collective-permute-start.14 = (bf16[16,8192]{1,0:T(8,128)(2,1)}, bf16[16,8192]{1,0:T(8,128)(2,1)}, u32[]{:S(2)}, u32[]{:S(2)}) collective-permute-start(bf16[16,8192]{1,0:T(8,128)(2,1)} %bitcast.11), channel_id=1, source_target_pairs={{0,32},{4,36},{8,40},{12,44},{16,48},{20,52},{24,56},{28,60},{32,0... | collective-permute-start | bytes 786440 | tf_op jit(solution)/shard_map/ppermute | solution.py:54
  37.6 9.2 %collective-permute-start.30 = (bf16[16,1536]{1,0:T(8,128)(2,1)S(1)}, bf16[16,1536]{1,0:T(8,128)(2,1)S(1)}, u32[]{:S(2)}, u32[]{:S(2)}) collective-permute-start(bf16[16,1536]{1,0:T(8,128)(2,1)S(1)} %slice.20), channel_id=1, source_target_pairs={{0,8},{4,12},{8,16},{12,20},{16,24},{20,28},{24,0},{28,4},{32,40},... | collective-permute-start | bytes 147464 | tf_op jit(solution)/shard_map/ppermute | solution.py:59
  39.0 10.0 %collective-permute-start.1 = (bf16[16,8192]{1,0:T(8,128)(2,1)S(1)}, bf16[16,8192]{1,0:T(8,128)(2,1)}, u32[]{:S(2)}, u32[]{:S(2)}) collective-permute-start(bf16[16,8192]{1,0:T(8,128)(2,1)S(1)} %collective-permute-done.refs_3_), channel_id=1, source_target_pairs={{0,8},{4,12},{8,16},{12,20},{16,24},{20,28},{24,0},{28,4},{32,40},... | collective-permute-start | bytes 786440 | tf_op jit(solution)/shard_map/ppermute | solution.py:54
  41.3 8.6 %collective-permute-start.10 = (bf16[16,8192]{1,0:T(8,128)(2,1)}, bf16[16,8192]{1,0:T(8,128)(2,1)}, u32[]{:S(2)}, u32[]{:S(2)}) collective-permute-start(bf16[16,8192]{1,0:T(8,128)(2,1)} %collective-permute-done.9.refs_1_), channel_id=1, source_target_pairs={{0,192},{4,196},{8,200},{12,204},{16,208},{20,212},{24,216},{28,22... | collective-permute-start | bytes 786440 | tf_op jit(solution)/shard_map/ppermute | solution.py:54
  45.0 7.0 %collective-permute-start.19 = (bf16[16,8192]{1,0:T(8,128)(2,1)S(1)}, bf16[16,8192]{1,0:T(8,128)(2,1)S(1)}, u32[]{:S(2)}, u32[]{:S(2)}) collective-permute-start(bf16[16,8192]{1,0:T(8,128)(2,1)S(1)} %collective-permute-done.refs_3_), channel_id=1, source_target_pairs={{0,24},{4,28},{8,0},{12,4},{16,8},{20,12},{24,16},{28,20},{32,56},... | collective-permute-start | bytes 786440 | tf_op jit(solution)/shard_map/ppermute | solution.py:54
  46.8 5.3 %collective-permute-start.31 = (bf16[16,1664]{1,0:T(8,128)(2,1)S(1)}, bf16[16,1664]{1,0:T(8,128)(2,1)S(1)}, u32[]{:S(2)}, u32[]{:S(2)}) collective-permute-start(bf16[16,1664]{1,0:T(8,128)(2,1)S(1)} %slice.21), channel_id=1, source_target_pairs={{0,24},{4,28},{8,0},{12,4},{16,8},{20,12},{24,16},{28,20},{32,56},... | collective-permute-start | bytes 159752 | tf_op jit(solution)/shard_map/ppermute | solution.py:59
  49.0 9.2 %collective-permute-start.21 = (bf16[16,8192]{1,0:T(8,128)(2,1)}, bf16[16,8192]{1,0:T(8,128)(2,1)S(1)}, u32[]{:S(2)}, u32[]{:S(2)}) collective-permute-start(bf16[16,8192]{1,0:T(8,128)(2,1)} %collective-permute-done.9.refs_1_), channel_id=1, source_target_pairs={{0,32},{4,36},{8,40},{12,44},{16,48},{20,52},{24,56},{28,60},{32,0... | collective-permute-start | bytes 786440 | tf_op jit(solution)/shard_map/ppermute | solution.py:54
  49.9 8.4 %collective-permute-start.23 = (bf16[16,8192]{1,0:T(8,128)(2,1)}, bf16[16,8192]{1,0:T(8,128)(2,1)S(1)}, u32[]{:S(2)}, u32[]{:S(2)}) collective-permute-start(bf16[16,8192]{1,0:T(8,128)(2,1)} %collective-permute-done.9.refs_1_), channel_id=1, source_target_pairs={{0,8},{4,12},{8,16},{12,20},{16,24},{20,28},{24,0},{28,4},{32,40},... | collective-permute-start | bytes 786440 | tf_op jit(solution)/shard_map/ppermute | solution.py:54
  52.0 5.9 %collective-permute-start.32 = (bf16[16,1664]{1,0:T(8,128)(2,1)S(1)}, bf16[16,1664]{1,0:T(8,128)(2,1)S(1)}, u32[]{:S(2)}, u32[]{:S(2)}) collective-permute-start(bf16[16,1664]{1,0:T(8,128)(2,1)S(1)} %slice.22), channel_id=1, source_target_pairs={{0,64},{4,68},{8,72},{12,76},{16,80},{20,84},{24,88},{28,92},{32,9... | collective-permute-start | bytes 159752 | tf_op jit(solution)/shard_map/ppermute | solution.py:59
  52.1 9.4 %collective-permute-start.33 = (bf16[16,1664]{1,0:T(8,128)(2,1)S(1)}, bf16[16,1664]{1,0:T(8,128)(2,1)S(1)}, u32[]{:S(2)}, u32[]{:S(2)}) collective-permute-start(bf16[16,1664]{1,0:T(8,128)(2,1)S(1)} %slice.23), channel_id=1, source_target_pairs={{0,192},{4,196},{8,200},{12,204},{16,208},{20,212},{24,216},{28,22... | collective-permute-start | bytes 159752 | tf_op jit(solution)/shard_map/ppermute | solution.py:59
  57.9 4.1 %collective-permute-start.34 = (bf16[16,1664]{1,0:T(8,128)(2,1)S(1)}, bf16[16,1664]{1,0:T(8,128)(2,1)S(1)}, u32[]{:S(2)}, u32[]{:S(2)}) collective-permute-start(bf16[16,1664]{1,0:T(8,128)(2,1)S(1)} %slice.24), channel_id=1, source_target_pairs={{0,32},{4,36},{8,40},{12,44},{16,48},{20,52},{24,56},{28,60},{32,0... | collective-permute-start | bytes 159752 | tf_op jit(solution)/shard_map/ppermute | solution.py:59
  58.2 10.2 %collective-permute-start.15 = (bf16[16,8192]{1,0:T(8,128)(2,1)}, bf16[16,8192]{1,0:T(8,128)(2,1)S(1)}, u32[]{:S(2)}, u32[]{:S(2)}) collective-permute-start(bf16[16,8192]{1,0:T(8,128)(2,1)} %collective-permute-done.14.refs_5_), channel_id=1, source_target_pairs={{0,64},{4,68},{8,72},{12,76},{16,80},{20,84},{24,88},{28,92},{32,9... | collective-permute-start | bytes 786440 | tf_op jit(solution)/shard_map/ppermute | solution.py:54
  58.3 10.1 %collective-permute-start.17 = (bf16[16,8192]{1,0:T(8,128)(2,1)}, bf16[16,8192]{1,0:T(8,128)(2,1)S(1)}, u32[]{:S(2)}, u32[]{:S(2)}) collective-permute-start(bf16[16,8192]{1,0:T(8,128)(2,1)} %collective-permute-done.14.refs_5_), channel_id=1, source_target_pairs={{0,192},{4,196},{8,200},{12,204},{16,208},{20,212},{24,216},{28,22... | collective-permute-start | bytes 786440 | tf_op jit(solution)/shard_map/ppermute | solution.py:54
  61.5 10.3 %collective-permute-start.11 = (bf16[16,8192]{1,0:T(8,128)(2,1)}, bf16[16,8192]{1,0:T(8,128)(2,1)S(1)}, u32[]{:S(2)}, u32[]{:S(2)}) collective-permute-start(bf16[16,8192]{1,0:T(8,128)(2,1)} %collective-permute-done.10.refs_9_), channel_id=1, source_target_pairs={{0,192},{4,196},{8,200},{12,204},{16,208},{20,212},{24,216},{28,22... | collective-permute-start | bytes 786440 | tf_op jit(solution)/shard_map/ppermute | solution.py:54
  62.1 11.2 %collective-permute-start.2 = (bf16[16,8192]{1,0:T(8,128)(2,1)}, bf16[16,8192]{1,0:T(8,128)(2,1)S(1)}, u32[]{:S(2)}, u32[]{:S(2)}) collective-permute-start(bf16[16,8192]{1,0:T(8,128)(2,1)} %collective-permute-done.1.refs_6_), channel_id=1, source_target_pairs={{0,8},{4,12},{8,16},{12,20},{16,24},{20,28},{24,0},{28,4},{32,40},... | collective-permute-start | bytes 786440 | tf_op jit(solution)/shard_map/ppermute | solution.py:54
  68.4 20.0 %collective-permute-start.20 = (bf16[16,8192]{1,0:T(8,128)(2,1)S(1)}, bf16[16,8192]{1,0:T(8,128)(2,1)S(1)}, u32[]{:S(2)}, u32[]{:S(2)}) collective-permute-start(bf16[16,8192]{1,0:T(8,128)(2,1)S(1)} %collective-permute-done.19.refs_12_), channel_id=1, source_target_pairs={{0,64},{4,68},{8,72},{12,76},{16,80},{20,84},{24,88},{28,92},{32,9... | collective-permute-start | bytes 786440 | tf_op jit(solution)/shard_map/ppermute | solution.py:54
  68.4 20.0 %collective-permute-start.22 = (bf16[16,8192]{1,0:T(8,128)(2,1)S(1)}, bf16[16,8192]{1,0:T(8,128)(2,1)S(1)}, u32[]{:S(2)}, u32[]{:S(2)}) collective-permute-start(bf16[16,8192]{1,0:T(8,128)(2,1)S(1)} %collective-permute-done.21.refs_15_), channel_id=1, source_target_pairs={{0,192},{4,196},{8,200},{12,204},{16,208},{20,212},{24,216},{28,22... | collective-permute-start | bytes 786440 | tf_op jit(solution)/shard_map/ppermute | solution.py:54
  71.8 16.6 %collective-permute-start.24 = (bf16[16,8192]{1,0:T(8,128)(2,1)S(1)}, bf16[16,8192]{1,0:T(8,128)(2,1)S(1)}, u32[]{:S(2)}, u32[]{:S(2)}) collective-permute-start(bf16[16,8192]{1,0:T(8,128)(2,1)S(1)} %collective-permute-done.23.refs_11_), channel_id=1, source_target_pairs={{0,32},{4,36},{8,40},{12,44},{16,48},{20,52},{24,56},{28,60},{32,0... | collective-permute-start | bytes 786440 | tf_op jit(solution)/shard_map/ppermute | solution.py:54
  73.3 15.1 %collective-permute-start.16 = (bf16[16,8192]{1,0:T(8,128)(2,1)S(1)}, bf16[16,8192]{1,0:T(8,128)(2,1)S(1)}, u32[]{:S(2)}, u32[]{:S(2)}) collective-permute-start(bf16[16,8192]{1,0:T(8,128)(2,1)S(1)} %collective-permute-done.15.refs_13_), channel_id=1, source_target_pairs={{0,8},{4,12},{8,16},{12,20},{16,24},{20,28},{24,0},{28,4},{32,40},... | collective-permute-start | bytes 786440 | tf_op jit(solution)/shard_map/ppermute | solution.py:54
  74.3 14.1 %collective-permute-start.18 = (bf16[16,8192]{1,0:T(8,128)(2,1)S(1)}, bf16[16,8192]{1,0:T(8,128)(2,1)S(1)}, u32[]{:S(2)}, u32[]{:S(2)}) collective-permute-start(bf16[16,8192]{1,0:T(8,128)(2,1)S(1)} %collective-permute-done.17.refs_14_), channel_id=1, source_target_pairs={{0,24},{4,28},{8,0},{12,4},{16,8},{20,12},{24,16},{28,20},{32,56},... | collective-permute-start | bytes 786440 | tf_op jit(solution)/shard_map/ppermute | solution.py:54
  75.6 0.9 copy-start.1
  76.5 0.9 copy-start.3
  87.4 1.0 copy-start
  100.5 2.9 %collective-permute-start.36 = (f32[32,16,512]{2,1,0:T(8,128)}, f32[32,16,512]{2,1,0:T(8,128)S(1)}, u32[]{:S(2)}, u32[]{:S(2)}) collective-permute-start(f32[32,16,512]{2,1,0:T(8,128)} %get-tuple-element.8), channel_id=1, source_target_pairs={{0,4},{4,0},{8,12},{12,8},{16,20},{20,16},{24,28},{28,24},{32,36},... | collective-permute-start | bytes 3145736 | tf_op jit(solution)/shard_map/ppermute | solution.py:205

commit v3 on v0

v3 whole, which is shorter than its diff:
```python
import functools

import jax
import jax.numpy as jnp
from jax import lax
from jax.experimental import pallas as pl
from jax.experimental.pallas import tpu as pltpu
from jax.sharding import PartitionSpec as P

Y, Z, X, CORES = 4, 2, 4, 2
CHIPS = Y * Z * X

XP, XM, YP, YM, ZZ = (1, 0, 0), (3, 0, 0), (0, 1, 0), (0, 3, 0), (0, 0, 1)
LINKS = (XP, XM, YP, YM, ZZ)
OWN, LAST = (0, 0, 0), (2, 2, 1)
DETOURS = ((3, 1, 0), (3, 3, 0))
PHASES = (
    ((XM, ((3, 0, 0),)), (YP, ((0, 1, 0),)), (ZZ, ((0, 0, 1),)), (XP, ((1, 0, 0),)), (YM, ((0, 3, 0),))),
    (
        (YP, ((0, 2, 0), (3, 1, 0))),
        (XM, ((2, 0, 0), (3, 0, 1))),
        (XP, ((1, 0, 1), (1, 1, 0))),
        (YM, ((1, 3, 0), (3, 3, 0))),
    ),
    (
        (XM, ((3, 2, 0), (2, 1, 0))),
        (YM, ((2, 3, 0), (3, 3, 1))),
        (YP, ((1, 1, 1), (3, 1, 1))),
        (ZZ, ((0, 2, 1), (1, 3, 1))),
        (XP, ((2, 0, 1), (1, 2, 0))),
    ),
    (
        (ZZ, ((0, 1, 1), (0, 3, 1))),
        (XP, ((2, 1, 1), (2, 2, 0))),
        (XM, ((2, 3, 1),)),
        (YP, ((1, 2, 1),)),
        (YM, ((3, 2, 1),)),
    ),
)


def number(y, z, x, core):
    return ((y * Z + z) * X + x) * CORES + core


def moved(d, link):
    return ((d[0] - link[0]) % X, (d[1] - link[1]) % Y, (d[2] - link[2]) % Z)


def pairs(link):
    return [
        (number(y, z, x, c), number((y + link[1]) % Y, (z + link[2]) % Z, (x + link[0]) % X, c))
        for y in range(Y)
        for z in range(Z)
        for x in range(X)
        for c in range(CORES)
    ]


OTHER_CORE = [(2 * i + c, 2 * i + 1 - c) for i in range(CHIPS) for c in range(CORES)]
SAME_CORE = [[2 * i + c for i in range(CHIPS)] for c in range(CORES)]


def fetch(held, wanted):
    for names, rows in held:
        if names == wanted:
            return rows
    k = held[0][1].shape[0] // len(held[0][0])
    parts = []
    for name in wanted:
        names, rows = next((n, r) for n, r in held if name in n)
        at = names.index(name) * k
        parts.append(rows if len(names) == 1 else rows[at : at + k])
    return parts[0] if len(parts) == 1 else jnp.concatenate(parts, axis=0)


def after(value, *others):
    return lax.optimization_barrier((value, *others))[0]


def send(held, phase, chain, waits=()):
    rows = [fetch(held, tuple(moved(d, link) for d in names)) for link, names in phase]
    got = []
    for (link, names), r in zip(phase, rows):
        ties = chain.get(link, []) + list(waits)
        if ties:
            r = after(r, *ties)
        chain[link] = [lax.ppermute(r, "tm", pairs(link))]
        got.append((names, chain[link][0]))
    return got


def send_last(held, wait):
    rows = [fetch(held, (moved(LAST, route),)) for route in DETOURS]
    k = rows[0].shape[0] // len(DETOURS)
    return [
        lax.ppermute(after(r[n * k : (n + 1) * k], wait), "tm", pairs(route))
        for n, (route, r) in enumerate(zip(DETOURS, rows))
    ]


def source(me, d):
    chip = me // CORES
    x, z, y = chip % X, (chip // X) % Z, chip // (X * Z)
    return (((y - d[1] + Y) % Y) * Z + (z - d[2] + Z) % Z) * X + (x - d[0] + X) % X


def multiply_kernel(names, count, k, steps, first, *refs):
    me_ref, refs = refs[0], refs[1:]
    bundles, refs = refs[:count], refs[count:]
    weights, refs = refs[:CORES], refs[CORES:]
    keep, out, rows = refs[-3:]
    n = pl.program_id(0)
    me = me_ref[0]
    core, chip = me % CORES, me // CORES
    width = weights[0].shape[0] // steps

    @pl.when(n == 0)
    def _():
        if first:
            keep[...] = jnp.zeros_like(keep)
            out[...] = jnp.zeros_like(out)
        else:
            keep[...] = refs[0][...]
            out[...] = refs[1][...]

    def place(even, odd, shift, columns):
        for b, d in enumerate(names):
            to = source(me, d) + chip
            after = to + shift

            @pl.when(to < CHIPS)
            def _():
                even[to, :, columns] += rows[2 * b * k : (2 * b + 1) * k]

            @pl.when(after < CHIPS)
            def _():
                odd[after, :, columns] += rows[(2 * b + 1) * k : (2 * b + 2) * k]

    for which, tiles in enumerate(weights):
        for step in range(steps):

            @pl.when(n == which * steps + step)
            def _():
                left = jnp.concatenate([b[...] for b in bundles], axis=0)
                rows[...] = lax.dot_general(
                    left,
                    tiles[step * width : (step + 1) * width],
                    (((1,), (1,)), ((), ())),
                    preferred_element_type=jnp.float32,
                )

    for step in range(steps):
        columns = slice(step * width, (step + 1) * width)

        @pl.when(n == step)
        def _():
            place(keep, out, core, columns)

        @pl.when(n == steps + step)
        def _():
            place(out, keep, 1 - core, columns)


TILE, VMEM = 256, 18 << 20


def multiply(me, names, bundles, weights, before, name):
    total, p = sum(r.shape[0] for r in bundles), bundles[0].shape[1]
    s = weights[0].shape[0]
    k, steps = total // (2 * len(names)), s // TILE
    once = pl.Buffered(1)
    kept = pl.BlockSpec((CHIPS, k, s), lambda n, me: (0, 0, 0), pipeline_mode=once)
    whole = [
        pl.BlockSpec(r.shape, lambda n, me: (0, 0), pipeline_mode=once) for r in (*bundles, *weights)
    ]
    out = jax.ShapeDtypeStruct((CHIPS, k, s), jnp.float32)
    return pl.pallas_call(
        functools.partial(multiply_kernel, names, len(bundles), k, steps, not before),
        out_shape=[out, out],
        grid_spec=pltpu.PrefetchScalarGridSpec(
            num_scalar_prefetch=1,
            grid=(2 * steps,),
            in_specs=whole + [kept] * len(before),
            out_specs=[kept, kept],
            scratch_shapes=[pltpu.VMEM((total, TILE), jnp.float32)],
        ),
        compiler_params=pltpu.CompilerParams(vmem_limit_bytes=VMEM),
        cost_estimate=pl.CostEstimate(
            flops=4 * total * p * s, bytes_accessed=2 * p * (total + 2 * s) + 16 * CHIPS * k * s, transcendentals=0
        ),
        name=name,
    )(me, *bundles, *weights, *before)


def across_floors(rows, at):
    width = rows.shape[1] // len(at)

    def parts(*owners):
        return jnp.concatenate(
            [lax.dynamic_slice_in_dim(rows, q * width, width, 1) for q in owners], axis=1
        )

    def swap(value, by):
        return lax.ppermute(value, "floor", [(f, f ^ by) for f in range(len(at))])

    two = parts(at[0], at[3]) + swap(parts(at[1], at[2]), 1)
    return two[:, :width] + swap(two[:, width:], 3)


def local(samples, operator):
    me = lax.axis_index("tm")
    core = me % CORES
    half = samples.shape[2] // CORES
    own = operator[0]

    def columns(rows, which):
        return lax.dynamic_slice_in_dim(rows, which * half, half, 1)

    theirs = lax.ppermute(columns(samples[0], 1 - core), "tm", OTHER_CORE)
    mine = columns(samples[0], core)
    block = jnp.concatenate(
        [jnp.where(core == 0, mine, theirs), jnp.where(core == 0, theirs, mine)], axis=0
    )
    at = me.reshape(1)

    def names(bundles):
        return [d for n, _ in bundles for d in n]

    def rows(bundles):
        return [r for _, r in bundles]

    chain = {}
    held = [((OWN,), block)]
    held = held + send(held, PHASES[0], chain)
    other = columns(after(own, block), 1 - core)
    other = lax.ppermute(after(other, *rows(held)), "tm", OTHER_CORE)
    chain[ZZ] = [other]
    weights = (columns(after(own, *rows(held)), core), other)
    held = held + send(held, PHASES[1], chain)
    got = send(held, PHASES[2], chain, (other,))
    early = multiply(at, names(held), rows(held), weights, (), "early")
    mid_blocks = got
    last = send_last(held + mid_blocks, early[0])
    got = send(held + mid_blocks, PHASES[3], chain, early[:1])
    mid = multiply(at, names(mid_blocks), rows(mid_blocks), weights, early, "mid")
    keep, out = multiply(
        at, names(got) + [LAST], rows(got) + last, weights, mid, "late"
    )

    both = keep + lax.ppermute(out, "tm", OTHER_CORE)
    floor = lax.axis_index("floor")
    floors = [floor ^ n for n in range(lax.axis_size("floor"))]
    sums = lax.all_to_all(both, "tm", 0, 0, tiled=True, axis_index_groups=SAME_CORE).sum(0)
    return across_floors(sums, floors)[None].astype(jnp.bfloat16)


def solution(mesh):
    placed = (P("tm", None, "floor"), P("tm", None, "floor"))
    return jax.shard_map(
        local, mesh=mesh, in_specs=placed, out_specs=P("tm", None, "floor"), check_vma=False
    )
```

time: 481 us -> 116 us (0.24)
  waiting for transfers between devices: 443 us -> 42.3 us
  starting transfers between devices: 0.08 us -> 52.2 us
  matrix products: 21.5 us -> 0 us
  Pallas kernels: 0 us -> 14 us
  between operations: 13.1 us -> 0.28 us
    reduce_scatter x2 -> x0, waiting for transfers between devices: 312 us -> none  [the longest x1 284 us: local(): mine = lax.psum_scatter(shifted, 'tm', scatter_dimension=0, tiled=True)]
    all_gather x1 -> x0, waiting for transfers between devices: 130 us -> none  [local(): lax.all_gather(samples, 'tm', axis=0, tiled=True)]
    ppermute x0 -> x26, starting transfers between devices: none -> 41.7 us  [the longest x19 26.8 us: send(): chain[link] = [lax.ppermute(r, 'tm', pairs(link))]]
    ppermute x0 -> x26, waiting for transfers between devices: none -> 25.6 us  [the longest x19 16.5 us: send(): chain[link] = [lax.ppermute(r, 'tm', pairs(link))]]
    pad x1 -> x0, matrix products: 21.5 us -> none  [local(): padded = jnp.pad(images, ((blocks, 0), (0, 0), (0, 0)))]
    all_to_all x0 -> x1, waiting for transfers between devices: none -> 16.6 us  [local(): lax.all_to_all(both, 'tm', 0, 0, tiled=True, axis_index_groups=SAME_CORE)]
    pallas_call x0 -> x3, Pallas kernels: none -> 14 us  [multiply(): pl.pallas_call(functools.partial(multiply_kernel, names, len(bundles), k,...]
    all_to_all x0 -> x1, starting transfers between devices: none -> 10.5 us  [local(): lax.all_to_all(both, 'tm', 0, 0, tiled=True, axis_index_groups=SAME_CORE)]
  transfers between devices with their start and end apart: 3 -> 27, of which waited for: 3 -> 16; matrix products, arithmetic and copies ran while one was open for 0% -> 3% of each run, Pallas kernels for 0% -> 9%
where the time goes in v3:
time: 116 us
  starting transfers between devices  52.2 us (45%)
  waiting for transfers between devices  42.3 us (36%)
  Pallas kernels  14 us (12%)
  local copies, waits for them, and re-layouts  4.19 us (4%)
  other arithmetic  3.33 us (3%)
    ppermute x19, starting transfers between devices, send(): chain[link] = [lax.ppermute(r, 'tm', pairs(link))]  26.8 us
    all_to_all x1, waiting for transfers between devices, local(): lax.all_to_all(both, 'tm', 0, 0, tiled=True, axis_index_groups=SAME_CORE)  16.6 us
    ppermute x19, waiting for transfers between devices, send(): chain[link] = [lax.ppermute(r, 'tm', pairs(link))]  16.5 us
    pallas_call x3, Pallas kernels, multiply(): pl.pallas_call(functools.partial(multiply_kernel, names, len(bundles), k,...  14 us
    all_to_all x1, starting transfers between devices, local(): lax.all_to_all(both, 'tm', 0, 0, tiled=True, axis_index_groups=SAME_CORE)  10.5 us
    ppermute x2, starting transfers between devices, swap(): return lax.ppermute(value, 'floor', [(f, f ^ by) for f in range(len(at))])  8.39 us
    ppermute x2, starting transfers between devices, send_last(): lax.ppermute(after(r[n * k:(n + 1) * k], wait), 'tm', pairs(route))  6.36 us
    dynamic_slice x3, local copies, waits for them, and re-layouts, columns(): return lax.dynamic_slice_in_dim(rows, which * half, half, 1)  4.01 us
  transfers between devices with their start and end apart: 27, of which 16 were waited for; matrix products, arithmetic and copies ran while one was open for 3% of the time, Pallas kernels for 9%

profile of v3, /device:TPU:2, one launch (start us, length us, event | category | flops | bytes accessed | tf_op | source)
XLA Modules:
  0.0 116.3 jit_solution(11628448141368726034)
XLA Ops:
  0.0 0.9 dynamic-slice_bitcast_fusion
  0.9 0.1 collective-permute-start
  1.0 1.3 %collective-permute-done = bf16[16,4096]{1,0:T(8,128)(2,1)S(1)} collective-permute-done((bf16[16,4096]{1,0:T(8,128)(2,1)S(1)}, bf16[16,4096]{1,0:T(8,128)(2,1)S(1)}, u32[]{:S(2)}, u32[]{:S(2)}) %collective-permute-start) | collective-permute-done | bytes 131104 | tf_op jit(solution)/shard_map/ppermute | solution.py:220
  2.4 0.9 bitcast_select_fusion.1
  3.3 1.7 %collective-permute-start.1 = (bf16[32,4096]{1,0:T(8,128)(2,1)S(1)}, bf16[32,4096]{1,0:T(8,128)(2,1)S(1)}, u32[]{:S(2)}, u32[]{:S(2)}) collective-permute-start(bf16[32,4096]{1,0:T(8,128)(2,1)S(1)} %pad_maximum_fusion.9.refs_1_), channel_id=1, source_target_pairs={{0,64},{4,68},{8,72},{12,76},{16,80},{20,84},{24,88},{28,92},{32,9... | collective-permute-start | bytes 786440 | tf_op jit(solution)/shard_map/ppermute | solution.py:88
  5.0 1.9 %collective-permute-start.7 = (bf16[32,4096]{1,0:T(8,128)(2,1)S(1)}, bf16[32,4096]{1,0:T(8,128)(2,1)S(1)}, u32[]{:S(2)}, u32[]{:S(2)}) collective-permute-start(bf16[32,4096]{1,0:T(8,128)(2,1)S(1)} %pad_maximum_fusion.9.refs_1_), channel_id=1, source_target_pairs={{0,32},{4,36},{8,40},{12,44},{16,48},{20,52},{24,56},{28,60},{32,0... | collective-permute-start | bytes 786440 | tf_op jit(solution)/shard_map/ppermute | solution.py:88
  6.9 0.5 collective-permute-start.3
  7.4 1.5 %collective-permute-start.5 = (bf16[32,4096]{1,0:T(8,128)(2,1)S(1)}, bf16[32,4096]{1,0:T(8,128)(2,1)S(1)}, u32[]{:S(2)}, u32[]{:S(2)}) collective-permute-start(bf16[32,4096]{1,0:T(8,128)(2,1)S(1)} %pad_maximum_fusion.9.refs_1_), channel_id=1, source_target_pairs={{0,8},{4,12},{8,16},{12,20},{16,24},{20,28},{24,0},{28,4},{32,40},... | collective-permute-start | bytes 786440 | tf_op jit(solution)/shard_map/ppermute | solution.py:88
  8.9 1.7 %collective-permute-start.2 = (bf16[32,4096]{1,0:T(8,128)(2,1)S(1)}, bf16[32,4096]{1,0:T(8,128)(2,1)S(1)}, u32[]{:S(2)}, u32[]{:S(2)}) collective-permute-start(bf16[32,4096]{1,0:T(8,128)(2,1)S(1)} %pad_maximum_fusion.9.refs_1_), channel_id=1, source_target_pairs={{0,192},{4,196},{8,200},{12,204},{16,208},{20,212},{24,216},{28,22... | collective-permute-start | bytes 786440 | tf_op jit(solution)/shard_map/ppermute | solution.py:88
  10.6 2.6 %constant_dynamic-slice_fusion.5 = bf16[512,4096]{1,0:T(8,128)(2,1)S(1)} fusion(bf16[512,8192]{1,0:T(8,128)(2,1)} %bitcast.9, s32[]{:T(128)S(6)} %select_n.42), kind=kLoop, calls=%fused_computation.23 | loop fusion | bytes 8388612 | tf_op jit(solution)/shard_map/dynamic_slice | solution.py:218
  13.2 0.0 slice-start.1
  13.2 0.0 collective-permute-done.1.refs_3_
  13.2 0.0 collective-permute-done.7.refs_4_
  13.2 1.5 %collective-permute-done.3.refs_2_ = bf16[32,4096]{1,0:T(8,128)(2,1)S(1)} collective-permute-done((bf16[32,4096]{1,0:T(8,128)(2,1)S(1)}, bf16[32,4096]{1,0:T(8,128)(2,1)S(1)}, u32[]{:S(2)}, u32[]{:S(2)}) %collective-permute-start.3) | collective-permute-done | bytes 262176 | tf_op jit(solution)/shard_map/ppermute | solution.py:88
  14.7 1.3 %collective-permute-done.5.refs_5_ = bf16[32,4096]{1,0:T(8,128)(2,1)S(1)} collective-permute-done((bf16[32,4096]{1,0:T(8,128)(2,1)S(1)}, bf16[32,4096]{1,0:T(8,128)(2,1)S(1)}, u32[]{:S(2)}, u32[]{:S(2)}) %collective-permute-start.5) | collective-permute-done | bytes 262176 | tf_op jit(solution)/shard_map/ppermute | solution.py:88
  16.0 0.2 collective-permute-done.2.refs_6_
  16.2 0.0 collective-permute-start.8
  16.2 0.3 pad_maximum_fusion.7
  16.5 1.6 %collective-permute-start.11 = (bf16[64,4096]{1,0:T(8,128)(2,1)S(1)}, bf16[64,4096]{1,0:T(8,128)(2,1)S(1)}, u32[]{:S(2)}, u32[]{:S(2)}) collective-permute-start(bf16[64,4096]{1,0:T(8,128)(2,1)S(1)} %get-tuple-element.36), channel_id=1, source_target_pairs={{0,8},{4,12},{8,16},{12,20},{16,24},{20,28},{24,0},{28,4},{32,40},... | collective-permute-start | bytes 1572872 | tf_op jit(solution)/shard_map/ppermute | solution.py:88
  18.1 1.4 %collective-permute-start.10 = (bf16[64,4096]{1,0:T(8,128)(2,1)S(1)}, bf16[64,4096]{1,0:T(8,128)(2,1)S(1)}, u32[]{:S(2)}, u32[]{:S(2)}) collective-permute-start(bf16[64,4096]{1,0:T(8,128)(2,1)S(1)} %get-tuple-element.35), channel_id=1, source_target_pairs={{0,24},{4,28},{8,0},{12,4},{16,8},{20,12},{24,16},{28,20},{32,56},... | collective-permute-start | bytes 1572872 | tf_op jit(solution)/shard_map/ppermute | solution.py:88
  19.4 1.6 %collective-permute-start.4 = (bf16[64,4096]{1,0:T(8,128)(2,1)S(1)}, bf16[64,4096]{1,0:T(8,128)(2,1)S(1)}, u32[]{:S(2)}, u32[]{:S(2)}) collective-permute-start(bf16[64,4096]{1,0:T(8,128)(2,1)S(1)} %get-tuple-element.30), channel_id=1, source_target_pairs={{0,64},{4,68},{8,72},{12,76},{16,80},{20,84},{24,88},{28,92},{32,9... | collective-permute-start | bytes 1572872 | tf_op jit(solution)/shard_map/ppermute | solution.py:88
  21.0 1.7 %collective-permute-start.6 = (bf16[64,4096]{1,0:T(8,128)(2,1)S(1)}, bf16[64,4096]{1,0:T(8,128)(2,1)S(1)}, u32[]{:S(2)}, u32[]{:S(2)}) collective-permute-start(bf16[64,4096]{1,0:T(8,128)(2,1)S(1)} %get-tuple-element.31), channel_id=1, source_target_pairs={{0,192},{4,196},{8,200},{12,204},{16,208},{20,212},{24,216},{28,22... | collective-permute-start | bytes 1572872 | tf_op jit(solution)/shard_map/ppermute | solution.py:88
  22.7 9.3 %collective-permute-done.11.refs_9_ = bf16[64,4096]{1,0:T(8,128)(2,1)S(1)} collective-permute-done((bf16[64,4096]{1,0:T(8,128)(2,1)S(1)}, bf16[64,4096]{1,0:T(8,128)(2,1)S(1)}, u32[]{:S(2)}, u32[]{:S(2)}) %collective-permute-start.11) | collective-permute-done | bytes 524320 | tf_op jit(solution)/shard_map/ppermute | solution.py:88
  31.9 0.8 collective-permute-done.10.refs_8_
  32.8 1.9 %collective-permute-done.4.refs_7_ = bf16[64,4096]{1,0:T(8,128)(2,1)S(1)} collective-permute-done((bf16[64,4096]{1,0:T(8,128)(2,1)S(1)}, bf16[64,4096]{1,0:T(8,128)(2,1)S(1)}, u32[]{:S(2)}, u32[]{:S(2)}) %collective-permute-start.4) | collective-permute-done | bytes 524320 | tf_op jit(solution)/shard_map/ppermute | solution.py:88
  34.7 0.1 collective-permute-done.6.refs_10_
  34.8 0.2 pad_maximum_fusion.4
  35.0 0.4 collective-permute-start.9
  35.3 1.2 %collective-permute-start.14 = (bf16[64,4096]{1,0:T(8,128)(2,1)S(1)}, bf16[64,4096]{1,0:T(8,128)(2,1)S(1)}, u32[]{:S(2)}, u32[]{:S(2)}) collective-permute-start(bf16[64,4096]{1,0:T(8,128)(2,1)S(1)} %get-tuple-element.41), channel_id=1, source_target_pairs={{0,8},{4,12},{8,16},{12,20},{16,24},{20,28},{24,0},{28,4},{32,40},... | collective-permute-start | bytes 1572872 | tf_op jit(solution)/shard_map/ppermute | solution.py:88
  36.5 1.2 %collective-permute-start.13 = (bf16[64,4096]{1,0:T(8,128)(2,1)S(1)}, bf16[64,4096]{1,0:T(8,128)(2,1)S(1)}, u32[]{:S(2)}, u32[]{:S(2)}) collective-permute-start(bf16[64,4096]{1,0:T(8,128)(2,1)S(1)} %get-tuple-element.40), channel_id=1, source_target_pairs={{0,64},{4,68},{8,72},{12,76},{16,80},{20,84},{24,88},{28,92},{32,9... | collective-permute-start | bytes 1572872 | tf_op jit(solution)/shard_map/ppermute | solution.py:88
  37.7 0.5 constant_dynamic-slice_fusion.4.refs_11_.refs_6_.refs_8_
  38.2 2.1 %collective-permute-start.16 = (bf16[64,4096]{1,0:T(8,128)(2,1)S(1)}, bf16[64,4096]{1,0:T(8,128)(2,1)S(1)}, u32[]{:S(2)}, u32[]{:S(2)}) collective-permute-start(bf16[64,4096]{1,0:T(8,128)(2,1)S(1)} %collective-permute-done.10.refs_8_), channel_id=1, source_target_pairs={{0,192},{4,196},{8,200},{12,204},{16,208},{20,212},{24,216},{28,22... | collective-permute-start | bytes 1572872 | tf_op jit(solution)/shard_map/ppermute | solution.py:88
  40.3 1.7 %collective-permute-start.17 = (bf16[64,4096]{1,0:T(8,128)(2,1)S(1)}, bf16[64,4096]{1,0:T(8,128)(2,1)S(1)}, u32[]{:S(2)}, u32[]{:S(2)}) collective-permute-start(bf16[64,4096]{1,0:T(8,128)(2,1)S(1)} %collective-permute-done.4.refs_7_), channel_id=1, source_target_pairs={{0,24},{4,28},{8,0},{12,4},{16,8},{20,12},{24,16},{28,20},{32,56},... | collective-permute-start | bytes 1572872 | tf_op jit(solution)/shard_map/ppermute | solution.py:88
  42.0 5.7 %early.1 = (f32[32,16,512]{2,1,0:T(8,128)S(1)}, f32[32,16,512]{2,1,0:T(8,128)S(1)}) custom-call(s32[1]{0:T(128)} %bitcast.refs_0_, bf16[32,4096]{1,0:T(8,128)(2,1)S(1)} %pad_maximum_fusion.9.refs_1_, bf16[32,4096]{1,0:T(8,128)(2,1)S(1)} %collective-permute-done.3.refs_2_, bf16[32,4096]{1,0:T(8,128)(2,1)S(1)} %collective-permute-done.1.refs_3_, ...), custom_call_target="tpu_custom_call" | custom-call | flops 3758096384 | bytes 16252928 | tf_op jit(solution)/shard_map/early/pallas_call | solution.py:178
  47.7 0.5 collective-permute-done.9.refs_4_
  48.2 1.3 %collective-permute-start.12 = (bf16[64,4096]{1,0:T(8,128)(2,1)S(1)}, bf16[64,4096]{1,0:T(8,128)(2,1)S(1)}, u32[]{:S(2)}, u32[]{:S(2)}) collective-permute-start(bf16[64,4096]{1,0:T(8,128)(2,1)S(1)} %get-tuple-element.39), channel_id=1, source_target_pairs={{0,32},{4,36},{8,40},{12,44},{16,48},{20,52},{24,56},{28,60},{32,0... | collective-permute-start | bytes 1572872 | tf_op jit(solution)/shard_map/ppermute | solution.py:88
  49.6 0.0 collective-permute-done.14.refs_5_
  49.6 1.0 collective-permute-done.13.refs_3_
  50.6 1.5 %collective-permute-start.15 = (bf16[64,4096]{1,0:T(8,128)(2,1)S(1)}, bf16[64,4096]{1,0:T(8,128)(2,1)S(1)}, u32[]{:S(2)}, u32[]{:S(2)}) collective-permute-start(bf16[64,4096]{1,0:T(8,128)(2,1)S(1)} %pad_maximum_fusion.8), channel_id=1, source_target_pairs={{0,8},{4,12},{8,16},{12,20},{16,24},{20,28},{24,0},{28,4},{32,40},... | collective-permute-start | bytes 1572872 | tf_op jit(solution)/shard_map/ppermute | solution.py:88
  52.2 0.7 collective-permute-start.21
  52.8 0.0 collective-permute-done.16.refs_2_
  52.9 5.7 %collective-permute-start.22 = (bf16[16,4096]{1,0:T(8,128)(2,1)S(1)}, bf16[16,4096]{1,0:T(8,128)(2,1)S(1)}, u32[]{:S(2)}, u32[]{:S(2)}) collective-permute-start(bf16[16,4096]{1,0:T(8,128)(2,1)S(1)} %slice.60), channel_id=1, source_target_pairs={{0,216},{4,220},{8,192},{12,196},{16,200},{20,204},{24,208},{28,21... | collective-permute-start | bytes 393224 | tf_op jit(solution)/shard_map/ppermute | solution.py:97
  58.6 0.0 collective-permute-done.17.refs_1_
  58.6 1.1 collective-permute-start.18
  59.6 0.8 collective-permute-done.21.refs_6_
  60.5 0.0 collective-permute-start.19
  60.5 1.0 collective-permute-done.22.refs_7_
  61.5 2.9 %collective-permute-start.20 = (bf16[32,4096]{1,0:T(8,128)(2,1)S(1)}, bf16[32,4096]{1,0:T(8,128)(2,1)S(1)}, u32[]{:S(2)}, u32[]{:S(2)}) collective-permute-start(bf16[32,4096]{1,0:T(8,128)(2,1)S(1)} %slice.58), channel_id=1, source_target_pairs={{0,192},{4,196},{8,200},{12,204},{16,208},{20,212},{24,216},{28,22... | collective-permute-start | bytes 786440 | tf_op jit(solution)/shard_map/ppermute | solution.py:88
  64.4 4.5 %mid.1 = (f32[32,16,512]{2,1,0:T(8,128)S(1)}, f32[32,16,512]{2,1,0:T(8,128)S(1)}) custom-call(s32[1]{0:T(128)} %bitcast.refs_0_, bf16[64,4096]{1,0:T(8,128)(2,1)S(1)} %collective-permute-done.17.refs_1_, bf16[64,4096]{1,0:T(8,128)(2,1)S(1)} %collective-permute-done.16.refs_2_, bf16[64,4096]{1,0:T(8,128)(2,1)S(1)} %collective-permute-done.13.refs_3_, ...), custom_call_target="tpu_custom_call" | custom-call | flops 2684354560 | bytes 15204352 | tf_op jit(solution)/shard_map/mid/pallas_call | solution.py:178
  68.8 0.0 collective-permute-done.18.refs_3_
  68.9 0.0 collective-permute-done.19.refs_4_
  68.9 0.0 collective-permute-done.12.refs_1_
  68.9 3.8 %late.1 = (f32[32,16,512]{2,1,0:T(8,128)S(1)}, f32[32,16,512]{2,1,0:T(8,128)S(1)}) custom-call(s32[1]{0:T(128)} %bitcast.refs_0_, bf16[64,4096]{1,0:T(8,128)(2,1)S(1)} %collective-permute-done.12.refs_1_, bf16[64,4096]{1,0:T(8,128)(2,1)S(1)} %collective-permute-done.15.refs_2_, bf16[32,4096]{1,0:T(8,128)(2,1)S(1)} %collective-permute-done.18.refs_3_, ...), custom_call_target="tpu_custom_call" | custom-call | flops 2147483648 | bytes 14680064 | tf_op jit(solution)/shard_map/late/pallas_call | solution.py:178
  72.7 0.1 collective-permute-start.23
  72.8 2.6 %collective-permute-done.23 = f32[32,16,512]{2,1,0:T(8,128)S(1)} collective-permute-done((f32[32,16,512]{2,1,0:T(8,128)S(1)}, f32[32,16,512]{2,1,0:T(8,128)S(1)}, u32[]{:S(2)}, u32[]{:S(2)}) %collective-permute-start.23) | collective-permute-done | bytes 1048608 | tf_op jit(solution)/shard_map/ppermute | solution.py:251
  75.5 1.2 %add.36 = f32[32,16,512]{2,1,0:T(8,128)} add(f32[32,16,512]{2,1,0:T(8,128)S(1)} %get-tuple-element.53, f32[32,16,512]{2,1,0:T(8,128)S(1)} %collective-permute-done.23) | non-fusion elementwise | flops 262144 | bytes 3145728 | tf_op jit(solution)/shard_map/add | solution.py:251
  76.7 10.5 %all-to-all-start = ((f32[32,16,512]{2,1,0:T(8,128)}), f32[32,16,512]{2,1,0:T(8,128)S(1)}, u32[]{:S(2)}, u32[]{:S(2)}) async-start(f32[32,16,512]{2,1,0:T(8,128)} %add.36), calls=%async_computation | async-start | bytes 2097152 | tf_op jit(solution)/shard_map/all_to_all | solution.py:254
  87.1 16.6 %all-to-all-done = f32[32,16,512]{2,1,0:T(8,128)S(1)} async-done(((f32[32,16,512]{2,1,0:T(8,128)}), f32[32,16,512]{2,1,0:T(8,128)S(1)}, u32[]{:S(2)}, u32[]{:S(2)}) %all-to-all-start) | async-done | bytes 1048608 | tf_op jit(solution)/shard_map/all_to_all | solution.py:254
  103.8 0.1 reduce_sum.9
  103.9 3.4 %collective-permute-start.24 = (f32[16,256]{1,0:T(8,128)S(1)}, f32[16,256]{1,0:T(8,128)S(1)}, u32[]{:S(2)}, u32[]{:S(2)}) collective-permute-start(f32[16,256]{1,0:T(8,128)S(1)} %pad_maximum_fusion.10), channel_id=1, source_target_pairs={{0,1},{1,0},{2,3},{3,2},{4,5},{5,4},{6,7},{7,6},{8,9},{9,8},{10,11... | collective-permute-start | bytes 49160 | tf_op jit(solution)/shard_map/ppermute | solution.py:205
  107.3 1.7 %collective-permute-done.24 = f32[16,256]{1,0:T(8,128)S(1)} collective-permute-done((f32[16,256]{1,0:T(8,128)S(1)}, f32[16,256]{1,0:T(8,128)S(1)}, u32[]{:S(2)}, u32[]{:S(2)}) %collective-permute-start.24) | collective-permute-done | bytes 16416 | tf_op jit(solution)/shard_map/ppermute | solution.py:205
  109.0 5.0 %collective-permute-start.25 = (f32[16,128]{1,0:T(8,128)S(1)}, f32[16,128]{1,0:T(8,128)S(1)}, u32[]{:S(2)}, u32[]{:S(2)}) collective-permute-start(f32[16,128]{1,0:T(8,128)S(1)} %slice.62), channel_id=1, source_target_pairs={{0,3},{1,2},{2,1},{3,0},{4,7},{5,6},{6,5},{7,4},{8,11},{9,10},{10,... | collective-permute-start | bytes 24584 | tf_op jit(solution)/shard_map/ppermute | solution.py:205
  114.0 1.6 %collective-permute-done.25 = f32[16,128]{1,0:T(8,128)S(1)} collective-permute-done((f32[16,128]{1,0:T(8,128)S(1)}, f32[16,128]{1,0:T(8,128)S(1)}, u32[]{:S(2)}, u32[]{:S(2)}) %collective-permute-start.25) | collective-permute-done | bytes 8224 | tf_op jit(solution)/shard_map/ppermute | solution.py:205
  115.7 0.6 fusion.1
  (22 shorter events, 0.2 us)
Async XLA Ops:
  0.9 1.4 %collective-permute-start = (bf16[16,4096]{1,0:T(8,128)(2,1)S(1)}, bf16[16,4096]{1,0:T(8,128)(2,1)S(1)}, u32[]{:S(2)}, u32[]{:S(2)}) collective-permute-start(bf16[16,4096]{1,0:T(8,128)(2,1)S(1)} %dynamic-slice_bitcast_fusion), channel_id=1, source_target_pairs={{0,4},{4,0},{8,12},{12,8},{16,20},{20,16},{24,28},{28,24},{32,36},... | collective-permute-start | bytes 393224 | tf_op jit(solution)/shard_map/ppermute | solution.py:220
  3.3 9.9 %collective-permute-start.1 = (bf16[32,4096]{1,0:T(8,128)(2,1)S(1)}, bf16[32,4096]{1,0:T(8,128)(2,1)S(1)}, u32[]{:S(2)}, u32[]{:S(2)}) collective-permute-start(bf16[32,4096]{1,0:T(8,128)(2,1)S(1)} %pad_maximum_fusion.9.refs_1_), channel_id=1, source_target_pairs={{0,64},{4,68},{8,72},{12,76},{16,80},{20,84},{24,88},{28,92},{32,9... | collective-permute-start | bytes 786440 | tf_op jit(solution)/shard_map/ppermute | solution.py:88
  5.0 8.3 %collective-permute-start.7 = (bf16[32,4096]{1,0:T(8,128)(2,1)S(1)}, bf16[32,4096]{1,0:T(8,128)(2,1)S(1)}, u32[]{:S(2)}, u32[]{:S(2)}) collective-permute-start(bf16[32,4096]{1,0:T(8,128)(2,1)S(1)} %pad_maximum_fusion.9.refs_1_), channel_id=1, source_target_pairs={{0,32},{4,36},{8,40},{12,44},{16,48},{20,52},{24,56},{28,60},{32,0... | collective-permute-start | bytes 786440 | tf_op jit(solution)/shard_map/ppermute | solution.py:88
  6.9 7.8 %collective-permute-start.3 = (bf16[32,4096]{1,0:T(8,128)(2,1)S(1)}, bf16[32,4096]{1,0:T(8,128)(2,1)S(1)}, u32[]{:S(2)}, u32[]{:S(2)}) collective-permute-start(bf16[32,4096]{1,0:T(8,128)(2,1)S(1)} %pad_maximum_fusion.9.refs_1_), channel_id=1, source_target_pairs={{0,24},{4,28},{8,0},{12,4},{16,8},{20,12},{24,16},{28,20},{32,56},... | collective-permute-start | bytes 786440 | tf_op jit(solution)/shard_map/ppermute | solution.py:88
  7.4 8.5 %collective-permute-start.5 = (bf16[32,4096]{1,0:T(8,128)(2,1)S(1)}, bf16[32,4096]{1,0:T(8,128)(2,1)S(1)}, u32[]{:S(2)}, u32[]{:S(2)}) collective-permute-start(bf16[32,4096]{1,0:T(8,128)(2,1)S(1)} %pad_maximum_fusion.9.refs_1_), channel_id=1, source_target_pairs={{0,8},{4,12},{8,16},{12,20},{16,24},{20,28},{24,0},{28,4},{32,40},... | collective-permute-start | bytes 786440 | tf_op jit(solution)/shard_map/ppermute | solution.py:88
  8.9 7.2 %collective-permute-start.2 = (bf16[32,4096]{1,0:T(8,128)(2,1)S(1)}, bf16[32,4096]{1,0:T(8,128)(2,1)S(1)}, u32[]{:S(2)}, u32[]{:S(2)}) collective-permute-start(bf16[32,4096]{1,0:T(8,128)(2,1)S(1)} %pad_maximum_fusion.9.refs_1_), channel_id=1, source_target_pairs={{0,192},{4,196},{8,200},{12,204},{16,208},{20,212},{24,216},{28,22... | collective-permute-start | bytes 786440 | tf_op jit(solution)/shard_map/ppermute | solution.py:88
  10.6 27.1 %slice-start = ((s8[8388608]{0:T(1024)(128)(4,1)}), s8[4194304]{0:T(1024)(128)(4,1)S(1)}, s32[]{:S(2)}) async-start(s8[8388608]{0:T(1024)(128)(4,1)} %bitcast.10), calls=%async_computation.1 | async-start | bytes 8388608
  13.2 24.5 %slice-start.1 = ((s8[8388608]{0:T(1024)(128)(4,1)}), s8[4194304]{0:T(1024)(128)(4,1)S(1)}, s32[]{:S(2)}) async-start(s8[8388608]{0:T(1024)(128)(4,1)} %bitcast.10), calls=%async_computation.2 | async-start | bytes 8388608
  16.2 18.8 %collective-permute-start.8 = (bf16[512,4096]{1,0:T(8,128)(2,1)S(1)}, bf16[512,4096]{1,0:T(8,128)(2,1)S(1)}, u32[]{:S(2)}, u32[]{:S(2)}) collective-permute-start(bf16[512,4096]{1,0:T(8,128)(2,1)S(1)} %constant_dynamic-slice_fusion.5), channel_id=1, source_target_pairs={{0,4},{4,0},{8,12},{12,8},{16,20},{20,16},{24,28},{28,24},{32,36},... | collective-permute-start | bytes 12582920 | tf_op jit(solution)/shard_map/ppermute | solution.py:237
  16.5 15.4 %collective-permute-start.11 = (bf16[64,4096]{1,0:T(8,128)(2,1)S(1)}, bf16[64,4096]{1,0:T(8,128)(2,1)S(1)}, u32[]{:S(2)}, u32[]{:S(2)}) collective-permute-start(bf16[64,4096]{1,0:T(8,128)(2,1)S(1)} %get-tuple-element.36), channel_id=1, source_target_pairs={{0,8},{4,12},{8,16},{12,20},{16,24},{20,28},{24,0},{28,4},{32,40},... | collective-permute-start | bytes 1572872 | tf_op jit(solution)/shard_map/ppermute | solution.py:88
  18.1 14.7 %collective-permute-start.10 = (bf16[64,4096]{1,0:T(8,128)(2,1)S(1)}, bf16[64,4096]{1,0:T(8,128)(2,1)S(1)}, u32[]{:S(2)}, u32[]{:S(2)}) collective-permute-start(bf16[64,4096]{1,0:T(8,128)(2,1)S(1)} %get-tuple-element.35), channel_id=1, source_target_pairs={{0,24},{4,28},{8,0},{12,4},{16,8},{20,12},{24,16},{28,20},{32,56},... | collective-permute-start | bytes 1572872 | tf_op jit(solution)/shard_map/ppermute | solution.py:88
  19.4 15.3 %collective-permute-start.4 = (bf16[64,4096]{1,0:T(8,128)(2,1)S(1)}, bf16[64,4096]{1,0:T(8,128)(2,1)S(1)}, u32[]{:S(2)}, u32[]{:S(2)}) collective-permute-start(bf16[64,4096]{1,0:T(8,128)(2,1)S(1)} %get-tuple-element.30), channel_id=1, source_target_pairs={{0,64},{4,68},{8,72},{12,76},{16,80},{20,84},{24,88},{28,92},{32,9... | collective-permute-start | bytes 1572872 | tf_op jit(solution)/shard_map/ppermute | solution.py:88
  21.0 13.8 %collective-permute-start.6 = (bf16[64,4096]{1,0:T(8,128)(2,1)S(1)}, bf16[64,4096]{1,0:T(8,128)(2,1)S(1)}, u32[]{:S(2)}, u32[]{:S(2)}) collective-permute-start(bf16[64,4096]{1,0:T(8,128)(2,1)S(1)} %get-tuple-element.31), channel_id=1, source_target_pairs={{0,192},{4,196},{8,200},{12,204},{16,208},{20,212},{24,216},{28,22... | collective-permute-start | bytes 1572872 | tf_op jit(solution)/shard_map/ppermute | solution.py:88
  35.0 13.3 %collective-permute-start.9 = (bf16[64,4096]{1,0:T(8,128)(2,1)S(1)}, bf16[64,4096]{1,0:T(8,128)(2,1)S(1)}, u32[]{:S(2)}, u32[]{:S(2)}) collective-permute-start(bf16[64,4096]{1,0:T(8,128)(2,1)S(1)} %get-tuple-element.34), channel_id=1, source_target_pairs={{0,32},{4,36},{8,40},{12,44},{16,48},{20,52},{24,56},{28,60},{32,0... | collective-permute-start | bytes 1572872 | tf_op jit(solution)/shard_map/ppermute | solution.py:88
  35.3 14.2 %collective-permute-start.14 = (bf16[64,4096]{1,0:T(8,128)(2,1)S(1)}, bf16[64,4096]{1,0:T(8,128)(2,1)S(1)}, u32[]{:S(2)}, u32[]{:S(2)}) collective-permute-start(bf16[64,4096]{1,0:T(8,128)(2,1)S(1)} %get-tuple-element.41), channel_id=1, source_target_pairs={{0,8},{4,12},{8,16},{12,20},{16,24},{20,28},{24,0},{28,4},{32,40},... | collective-permute-start | bytes 1572872 | tf_op jit(solution)/shard_map/ppermute | solution.py:88
  36.5 14.1 %collective-permute-start.13 = (bf16[64,4096]{1,0:T(8,128)(2,1)S(1)}, bf16[64,4096]{1,0:T(8,128)(2,1)S(1)}, u32[]{:S(2)}, u32[]{:S(2)}) collective-permute-start(bf16[64,4096]{1,0:T(8,128)(2,1)S(1)} %get-tuple-element.40), channel_id=1, source_target_pairs={{0,64},{4,68},{8,72},{12,76},{16,80},{20,84},{24,88},{28,92},{32,9... | collective-permute-start | bytes 1572872 | tf_op jit(solution)/shard_map/ppermute | solution.py:88
  38.2 14.7 %collective-permute-start.16 = (bf16[64,4096]{1,0:T(8,128)(2,1)S(1)}, bf16[64,4096]{1,0:T(8,128)(2,1)S(1)}, u32[]{:S(2)}, u32[]{:S(2)}) collective-permute-start(bf16[64,4096]{1,0:T(8,128)(2,1)S(1)} %collective-permute-done.10.refs_8_), channel_id=1, source_target_pairs={{0,192},{4,196},{8,200},{12,204},{16,208},{20,212},{24,216},{28,22... | collective-permute-start | bytes 1572872 | tf_op jit(solution)/shard_map/ppermute | solution.py:88
  40.3 18.2 %collective-permute-start.17 = (bf16[64,4096]{1,0:T(8,128)(2,1)S(1)}, bf16[64,4096]{1,0:T(8,128)(2,1)S(1)}, u32[]{:S(2)}, u32[]{:S(2)}) collective-permute-start(bf16[64,4096]{1,0:T(8,128)(2,1)S(1)} %collective-permute-done.4.refs_7_), channel_id=1, source_target_pairs={{0,24},{4,28},{8,0},{12,4},{16,8},{20,12},{24,16},{28,20},{32,56},... | collective-permute-start | bytes 1572872 | tf_op jit(solution)/shard_map/ppermute | solution.py:88
  48.2 20.6 %collective-permute-start.12 = (bf16[64,4096]{1,0:T(8,128)(2,1)S(1)}, bf16[64,4096]{1,0:T(8,128)(2,1)S(1)}, u32[]{:S(2)}, u32[]{:S(2)}) collective-permute-start(bf16[64,4096]{1,0:T(8,128)(2,1)S(1)} %get-tuple-element.39), channel_id=1, source_target_pairs={{0,32},{4,36},{8,40},{12,44},{16,48},{20,52},{24,56},{28,60},{32,0... | collective-permute-start | bytes 1572872 | tf_op jit(solution)/shard_map/ppermute | solution.py:88
  50.6 18.2 %collective-permute-start.15 = (bf16[64,4096]{1,0:T(8,128)(2,1)S(1)}, bf16[64,4096]{1,0:T(8,128)(2,1)S(1)}, u32[]{:S(2)}, u32[]{:S(2)}) collective-permute-start(bf16[64,4096]{1,0:T(8,128)(2,1)S(1)} %pad_maximum_fusion.8), channel_id=1, source_target_pairs={{0,8},{4,12},{8,16},{12,20},{16,24},{20,28},{24,0},{28,4},{32,40},... | collective-permute-start | bytes 1572872 | tf_op jit(solution)/shard_map/ppermute | solution.py:88
  52.2 8.3 %collective-permute-start.21 = (bf16[16,4096]{1,0:T(8,128)(2,1)S(1)}, bf16[16,4096]{1,0:T(8,128)(2,1)S(1)}, u32[]{:S(2)}, u32[]{:S(2)}) collective-permute-start(bf16[16,4096]{1,0:T(8,128)(2,1)S(1)} %slice.59), channel_id=1, source_target_pairs={{0,88},{4,92},{8,64},{12,68},{16,72},{20,76},{24,80},{28,84},{32,1... | collective-permute-start | bytes 393224 | tf_op jit(solution)/shard_map/ppermute | solution.py:97
  52.9 8.6 %collective-permute-start.22 = (bf16[16,4096]{1,0:T(8,128)(2,1)S(1)}, bf16[16,4096]{1,0:T(8,128)(2,1)S(1)}, u32[]{:S(2)}, u32[]{:S(2)}) collective-permute-start(bf16[16,4096]{1,0:T(8,128)(2,1)S(1)} %slice.60), channel_id=1, source_target_pairs={{0,216},{4,220},{8,192},{12,196},{16,200},{20,204},{24,208},{28,21... | collective-permute-start | bytes 393224 | tf_op jit(solution)/shard_map/ppermute | solution.py:97
  58.6 10.3 %collective-permute-start.18 = (bf16[32,4096]{1,0:T(8,128)(2,1)S(1)}, bf16[32,4096]{1,0:T(8,128)(2,1)S(1)}, u32[]{:S(2)}, u32[]{:S(2)}) collective-permute-start(bf16[32,4096]{1,0:T(8,128)(2,1)S(1)} %slice.58), channel_id=1, source_target_pairs={{0,24},{4,28},{8,0},{12,4},{16,8},{20,12},{24,16},{28,20},{32,56},... | collective-permute-start | bytes 786440 | tf_op jit(solution)/shard_map/ppermute | solution.py:88
  60.5 8.4 %collective-permute-start.19 = (bf16[32,4096]{1,0:T(8,128)(2,1)S(1)}, bf16[32,4096]{1,0:T(8,128)(2,1)S(1)}, u32[]{:S(2)}, u32[]{:S(2)}) collective-permute-start(bf16[32,4096]{1,0:T(8,128)(2,1)S(1)} %slice.56), channel_id=1, source_target_pairs={{0,64},{4,68},{8,72},{12,76},{16,80},{20,84},{24,88},{28,92},{32,9... | collective-permute-start | bytes 786440 | tf_op jit(solution)/shard_map/ppermute | solution.py:88
  61.5 7.4 %collective-permute-start.20 = (bf16[32,4096]{1,0:T(8,128)(2,1)S(1)}, bf16[32,4096]{1,0:T(8,128)(2,1)S(1)}, u32[]{:S(2)}, u32[]{:S(2)}) collective-permute-start(bf16[32,4096]{1,0:T(8,128)(2,1)S(1)} %slice.58), channel_id=1, source_target_pairs={{0,192},{4,196},{8,200},{12,204},{16,208},{20,212},{24,216},{28,22... | collective-permute-start | bytes 786440 | tf_op jit(solution)/shard_map/ppermute | solution.py:88
  72.7 2.7 %collective-permute-start.23 = (f32[32,16,512]{2,1,0:T(8,128)S(1)}, f32[32,16,512]{2,1,0:T(8,128)S(1)}, u32[]{:S(2)}, u32[]{:S(2)}) collective-permute-start(f32[32,16,512]{2,1,0:T(8,128)S(1)} %get-tuple-element.54), channel_id=1, source_target_pairs={{0,4},{4,0},{8,12},{12,8},{16,20},{20,16},{24,28},{28,24},{32,36},... | collective-permute-start | bytes 3145736 | tf_op jit(solution)/shard_map/ppermute | solution.py:251
  76.7 27.1 %all-to-all-start = ((f32[32,16,512]{2,1,0:T(8,128)}), f32[32,16,512]{2,1,0:T(8,128)S(1)}, u32[]{:S(2)}, u32[]{:S(2)}) async-start(f32[32,16,512]{2,1,0:T(8,128)} %add.36), calls=%async_computation | async-start | bytes 2097152 | tf_op jit(solution)/shard_map/all_to_all | solution.py:254
  103.9 5.1 %collective-permute-start.24 = (f32[16,256]{1,0:T(8,128)S(1)}, f32[16,256]{1,0:T(8,128)S(1)}, u32[]{:S(2)}, u32[]{:S(2)}) collective-permute-start(f32[16,256]{1,0:T(8,128)S(1)} %pad_maximum_fusion.10), channel_id=1, source_target_pairs={{0,1},{1,0},{2,3},{3,2},{4,5},{5,4},{6,7},{7,6},{8,9},{9,8},{10,11... | collective-permute-start | bytes 49160 | tf_op jit(solution)/shard_map/ppermute | solution.py:205
  109.0 6.7 %collective-permute-start.25 = (f32[16,128]{1,0:T(8,128)S(1)}, f32[16,128]{1,0:T(8,128)S(1)}, u32[]{:S(2)}, u32[]{:S(2)}) collective-permute-start(f32[16,128]{1,0:T(8,128)S(1)} %slice.62), channel_id=1, source_target_pairs={{0,3},{1,2},{2,1},{3,0},{4,7},{5,6},{6,5},{7,4},{8,11},{9,10},{10,... | collective-permute-start | bytes 24584 | tf_op jit(solution)/shard_map/ppermute | solution.py:205

commit v4 on v3

--- a/solution.py
+++ b/solution.py
@@ -13,7 +13,7 @@
 XP, XM, YP, YM, ZZ = (1, 0, 0), (3, 0, 0), (0, 1, 0), (0, 3, 0), (0, 0, 1)
 LINKS = (XP, XM, YP, YM, ZZ)
 OWN, LAST = (0, 0, 0), (2, 2, 1)
-DETOURS = ((3, 1, 0), (3, 3, 0))
+FINISH = (XM, YM)
 PHASES = (
     ((XM, ((3, 0, 0),)), (YP, ((0, 1, 0),)), (ZZ, ((0, 0, 1),)), (XP, ((1, 0, 0),)), (YM, ((0, 3, 0),))),
     (
@@ -29,14 +29,10 @@
         (ZZ, ((0, 2, 1), (1, 3, 1))),
         (XP, ((2, 0, 1), (1, 2, 0))),
     ),
-    (
-        (ZZ, ((0, 1, 1), (0, 3, 1))),
-        (XP, ((2, 1, 1), (2, 2, 0))),
-        (XM, ((2, 3, 1),)),
-        (YP, ((1, 2, 1),)),
-        (YM, ((3, 2, 1),)),
-    ),
+    ((ZZ, ((0, 1, 1), (0, 3, 1))), (YM, ((3, 2, 1),)), (XM, ((2, 3, 1),))),
 )
+SHARED = (2, 2, 0)
+SHARING = ((XP, (2, 1, 1)), (YP, (1, 2, 1)))
 
 
 def number(y, z, x, core):
@@ -78,25 +74,42 @@
     return lax.optimization_barrier((value, *others))[0]
 
 
-def send(held, phase, chain, waits=()):
+def send(held, phase, chain, waits=(), sent=None):
     rows = [fetch(held, tuple(moved(d, link) for d in names)) for link, names in phase]
     got = []
     for (link, names), r in zip(phase, rows):
         ties = chain.get(link, []) + list(waits)
         if ties:
             r = after(r, *ties)
+        if sent is not None:
+            sent.append(r)
         chain[link] = [lax.ppermute(r, "tm", pairs(link))]
         got.append((names, chain[link][0]))
     return got
 
 
-def send_last(held, wait):
-    rows = [fetch(held, (moved(LAST, route),)) for route in DETOURS]
-    k = rows[0].shape[0] // len(DETOURS)
+def send_last(held, chain, wait):
+    rows = [fetch(held, (moved(LAST, link),)) for link in FINISH]
+    k = rows[0].shape[0] // len(FINISH)
     return [
-        lax.ppermute(after(r[n * k : (n + 1) * k], wait), "tm", pairs(route))
-        for n, (route, r) in enumerate(zip(DETOURS, rows))
+        lax.ppermute(after(r[n * k : (n + 1) * k], wait, *chain[link]), "tm", pairs(link))
+        for n, (link, r) in enumerate(zip(FINISH, rows))
     ]
+
+
+def send_shared(held, chain, wait):
+    (first, before), (second, behind) = SHARING
+    k = held[0][1].shape[0] // len(held[0][0])
+    parts = (
+        (first, [fetch(held, (moved(before, first),)), fetch(held, (moved(SHARED, first),))[: k // 2]]),
+        (second, [fetch(held, (moved(SHARED, second),))[k // 2 :], fetch(held, (moved(behind, second),))]),
+    )
+    got = []
+    for link, rows in parts:
+        rows = after(jnp.concatenate(rows, axis=0), wait, *chain[link])
+        chain[link] = [lax.ppermute(rows, "tm", pairs(link))]
+        got.append(chain[link][0])
+    return got
 
 
 def source(me, d):
@@ -162,7 +175,7 @@
             place(out, keep, 1 - core, columns)
 
 
-TILE, VMEM = 256, 18 << 20
+TILE = 256
 
 
 def multiply(me, names, bundles, weights, before, name):
@@ -175,6 +188,7 @@
         pl.BlockSpec(r.shape, lambda n, me: (0, 0), pipeline_mode=once) for r in (*bundles, *weights)
     ]
     out = jax.ShapeDtypeStruct((CHIPS, k, s), jnp.float32)
+    vmem = 2 * p * (total + CORES * s) + 4 * CHIPS * k * s * (2 + len(before)) + 4 * total * TILE
     return pl.pallas_call(
         functools.partial(multiply_kernel, names, len(bundles), k, steps, not before),
         out_shape=[out, out],
@@ -185,7 +199,7 @@
             out_specs=[kept, kept],
             scratch_shapes=[pltpu.VMEM((total, TILE), jnp.float32)],
         ),
-        compiler_params=pltpu.CompilerParams(vmem_limit_bytes=VMEM),
+        compiler_params=pltpu.CompilerParams(vmem_limit_bytes=vmem + (1 << 20)),
         cost_estimate=pl.CostEstimate(
             flops=4 * total * p * s, bytes_accessed=2 * p * (total + 2 * s) + 16 * CHIPS * k * s, transcendentals=0
         ),
@@ -217,8 +231,10 @@
     def columns(rows, which):
         return lax.dynamic_slice_in_dim(rows, which * half, half, 1)
 
-    theirs = lax.ppermute(columns(samples[0], 1 - core), "tm", OTHER_CORE)
-    mine = columns(samples[0], core)
+    mine, theirs = lax.optimization_barrier(
+        (columns(samples[0], core), columns(samples[0], 1 - core))
+    )
+    theirs = lax.ppermute(theirs, "tm", OTHER_CORE)
     block = jnp.concatenate(
         [jnp.where(core == 0, mine, theirs), jnp.where(core == 0, theirs, mine)], axis=0
     )
@@ -234,18 +250,26 @@
     held = [((OWN,), block)]
     held = held + send(held, PHASES[0], chain)
     other = columns(after(own, block), 1 - core)
-    other = lax.ppermute(after(other, *rows(held)), "tm", OTHER_CORE)
+    mine = columns(after(own, *rows(held)), core)
+    sent = []
+    held = held + send(held, PHASES[1], chain, (), sent)
+    other = lax.ppermute(after(other, *sent), "tm", OTHER_CORE)
     chain[ZZ] = [other]
-    weights = (columns(after(own, *rows(held)), core), other)
-    held = held + send(held, PHASES[1], chain)
+    weights = (mine, other)
     got = send(held, PHASES[2], chain, (other,))
     early = multiply(at, names(held), rows(held), weights, (), "early")
     mid_blocks = got
-    last = send_last(held + mid_blocks, early[0])
     got = send(held + mid_blocks, PHASES[3], chain, early[:1])
+    shared = send_shared(held + mid_blocks, chain, early[0])
     mid = multiply(at, names(mid_blocks), rows(mid_blocks), weights, early, "mid")
+    last = send_last(got, chain, mid[0])
     keep, out = multiply(
-        at, names(got) + [LAST], rows(got) + last, weights, mid, "late"
+        at,
+        names(got) + [SHARING[0][1], SHARED, SHARING[1][1], LAST],
+        rows(got) + shared + last,
+        weights,
+        mid,
+        "late",
     )
 
     both = keep + lax.ppermute(out, "tm", OTHER_CORE)

time: 116 us -> 112 us (0.966)
  starting transfers between devices: 52.2 us -> 49.1 us
    all_to_all x1, starting transfers between devices: 10.5 us -> 8.07 us  [local(): lax.all_to_all(both, 'tm', 0, 0, tiled=True, axis_index_groups=SAME_CORE)]
    ppermute x19 -> x17, waiting for transfers between devices: 16.5 us -> 15.4 us  [send(): chain[link] = [lax.ppermute(r, 'tm', pairs(link))]]
    ppermute x4 -> x6, waiting for transfers between devices: 3.16 us -> 3.85 us  [the longest x2 2.51 us: send_last(): lax.ppermute(after(r[n * k:(n + 1) * k], wait, *chain[link]), 'tm', pairs...]
    ppermute x4 -> x6, starting transfers between devices: 6.46 us -> 5.85 us  [the longest x2 5.5 us: send_last(): lax.ppermute(after(r[n * k:(n + 1) * k], wait, *chain[link]), 'tm', pairs...]
    ppermute x19 -> x17, starting transfers between devices: 26.8 us -> 26.4 us  [send(): chain[link] = [lax.ppermute(r, 'tm', pairs(link))]]
  transfers between devices with their start and end apart: 27 -> 27, of which waited for: 16 -> 14; matrix products, arithmetic and copies ran while one was open for 3% -> 3% of each run, Pallas kernels for 9% -> 9%
where the time goes in v4:
time: 112 us
  starting transfers between devices  49.1 us (44%)
  waiting for transfers between devices  41.9 us (37%)
  Pallas kernels  14 us (12%)
  local copies, waits for them, and re-layouts  4.27 us (4%)
  other arithmetic  2.42 us (2%)
    ppermute x17, starting transfers between devices, send(): chain[link] = [lax.ppermute(r, 'tm', pairs(link))]  26.4 us
    all_to_all x1, waiting for transfers between devices, local(): lax.all_to_all(both, 'tm', 0, 0, tiled=True, axis_index_groups=SAME_CORE)  16.6 us
    ppermute x17, waiting for transfers between devices, send(): chain[link] = [lax.ppermute(r, 'tm', pairs(link))]  15.4 us
    pallas_call x3, Pallas kernels, multiply(): pl.pallas_call(functools.partial(multiply_kernel, names, len(bundles), k,...  14 us
    ppermute x2, starting transfers between devices, swap(): return lax.ppermute(value, 'floor', [(f, f ^ by) for f in range(len(at))])  8.7 us
    all_to_all x1, starting transfers between devices, local(): lax.all_to_all(both, 'tm', 0, 0, tiled=True, axis_index_groups=SAME_CORE)  8.07 us
    ppermute x2, starting transfers between devices, send_last(): lax.ppermute(after(r[n * k:(n + 1) * k], wait, *chain[link]), 'tm', pairs...  5.5 us
    dynamic_slice x3, local copies, waits for them, and re-layouts, columns(): return lax.dynamic_slice_in_dim(rows, which * half, half, 1)  4.09 us
  transfers between devices with their start and end apart: 27, of which 14 were waited for; matrix products, arithmetic and copies ran while one was open for 3% of the time, Pallas kernels for 9%

profile of v4, /device:TPU:2, one launch (start us, length us, event | category | flops | bytes accessed | tf_op | source)
XLA Modules:
  0.0 112.0 jit_solution(15652302641979133743)
XLA Ops:
  0.0 1.0 dynamic-slice_bitcast_fusion
  1.0 0.1 collective-permute-start
  1.1 1.3 %collective-permute-done = bf16[16,4096]{1,0:T(8,128)(2,1)S(1)} collective-permute-done((bf16[16,4096]{1,0:T(8,128)(2,1)S(1)}, bf16[16,4096]{1,0:T(8,128)(2,1)S(1)}, u32[]{:S(2)}, u32[]{:S(2)}) %collective-permute-start) | collective-permute-done | bytes 131104 | tf_op jit(solution)/shard_map/ppermute | solution.py:237
  2.5 1.7 %collective-permute-start.1 = (bf16[32,4096]{1,0:T(8,128)(2,1)S(1)}, bf16[32,4096]{1,0:T(8,128)(2,1)S(1)}, u32[]{:S(2)}, u32[]{:S(2)}) collective-permute-start(bf16[32,4096]{1,0:T(8,128)(2,1)S(1)} %pad_maximum_fusion.10.refs_1_), channel_id=1, source_target_pairs={{0,64},{4,68},{8,72},{12,76},{16,80},{20,84},{24,88},{28,92},{32,9... | collective-permute-start | bytes 786440 | tf_op jit(solution)/shard_map/ppermute | solution.py:86
  4.1 1.9 %collective-permute-start.7 = (bf16[32,4096]{1,0:T(8,128)(2,1)S(1)}, bf16[32,4096]{1,0:T(8,128)(2,1)S(1)}, u32[]{:S(2)}, u32[]{:S(2)}) collective-permute-start(bf16[32,4096]{1,0:T(8,128)(2,1)S(1)} %pad_maximum_fusion.10.refs_1_), channel_id=1, source_target_pairs={{0,32},{4,36},{8,40},{12,44},{16,48},{20,52},{24,56},{28,60},{32,0... | collective-permute-start | bytes 786440 | tf_op jit(solution)/shard_map/ppermute | solution.py:86
  6.0 0.5 collective-permute-start.3
  6.6 1.5 %collective-permute-start.5 = (bf16[32,4096]{1,0:T(8,128)(2,1)S(1)}, bf16[32,4096]{1,0:T(8,128)(2,1)S(1)}, u32[]{:S(2)}, u32[]{:S(2)}) collective-permute-start(bf16[32,4096]{1,0:T(8,128)(2,1)S(1)} %pad_maximum_fusion.10.refs_1_), channel_id=1, source_target_pairs={{0,8},{4,12},{8,16},{12,20},{16,24},{20,28},{24,0},{28,4},{32,40},... | collective-permute-start | bytes 786440 | tf_op jit(solution)/shard_map/ppermute | solution.py:86
  8.1 1.7 %collective-permute-start.2 = (bf16[32,4096]{1,0:T(8,128)(2,1)S(1)}, bf16[32,4096]{1,0:T(8,128)(2,1)S(1)}, u32[]{:S(2)}, u32[]{:S(2)}) collective-permute-start(bf16[32,4096]{1,0:T(8,128)(2,1)S(1)} %pad_maximum_fusion.10.refs_1_), channel_id=1, source_target_pairs={{0,192},{4,196},{8,200},{12,204},{16,208},{20,212},{24,216},{28,22... | collective-permute-start | bytes 786440 | tf_op jit(solution)/shard_map/ppermute | solution.py:86
  9.7 2.6 %constant_dynamic-slice_fusion.5 = bf16[512,4096]{1,0:T(8,128)(2,1)S(1)} fusion(bf16[512,8192]{1,0:T(8,128)(2,1)} %bitcast.8, s32[]{:T(128)S(6)} %select_n.42), kind=kLoop, calls=%fused_computation.25 | loop fusion | bytes 8388612 | tf_op jit(solution)/shard_map/dynamic_slice | solution.py:232
  12.4 0.0 slice-start.1
  12.4 0.0 collective-permute-done.1.refs_3_
  12.4 0.0 collective-permute-done.7.refs_4_
  12.4 1.5 %collective-permute-done.3.refs_2_ = bf16[32,4096]{1,0:T(8,128)(2,1)S(1)} collective-permute-done((bf16[32,4096]{1,0:T(8,128)(2,1)S(1)}, bf16[32,4096]{1,0:T(8,128)(2,1)S(1)}, u32[]{:S(2)}, u32[]{:S(2)}) %collective-permute-start.3) | collective-permute-done | bytes 262176 | tf_op jit(solution)/shard_map/ppermute | solution.py:86
  13.8 1.3 %collective-permute-done.5.refs_5_ = bf16[32,4096]{1,0:T(8,128)(2,1)S(1)} collective-permute-done((bf16[32,4096]{1,0:T(8,128)(2,1)S(1)}, bf16[32,4096]{1,0:T(8,128)(2,1)S(1)}, u32[]{:S(2)}, u32[]{:S(2)}) %collective-permute-start.5) | collective-permute-done | bytes 262176 | tf_op jit(solution)/shard_map/ppermute | solution.py:86
  15.1 0.2 collective-permute-done.2.refs_6_
  15.3 0.3 pad_maximum_fusion.7
  15.6 0.1 collective-permute-start.8
  15.7 1.6 %collective-permute-start.11 = (bf16[64,4096]{1,0:T(8,128)(2,1)S(1)}, bf16[64,4096]{1,0:T(8,128)(2,1)S(1)}, u32[]{:S(2)}, u32[]{:S(2)}) collective-permute-start(bf16[64,4096]{1,0:T(8,128)(2,1)S(1)} %get-tuple-element.38), channel_id=1, source_target_pairs={{0,8},{4,12},{8,16},{12,20},{16,24},{20,28},{24,0},{28,4},{32,40},... | collective-permute-start | bytes 1572872 | tf_op jit(solution)/shard_map/ppermute | solution.py:86
  17.3 1.4 %collective-permute-start.10 = (bf16[64,4096]{1,0:T(8,128)(2,1)S(1)}, bf16[64,4096]{1,0:T(8,128)(2,1)S(1)}, u32[]{:S(2)}, u32[]{:S(2)}) collective-permute-start(bf16[64,4096]{1,0:T(8,128)(2,1)S(1)} %get-tuple-element.37), channel_id=1, source_target_pairs={{0,24},{4,28},{8,0},{12,4},{16,8},{20,12},{24,16},{28,20},{32,56},... | collective-permute-start | bytes 1572872 | tf_op jit(solution)/shard_map/ppermute | solution.py:86
  18.7 1.6 %collective-permute-start.4 = (bf16[64,4096]{1,0:T(8,128)(2,1)S(1)}, bf16[64,4096]{1,0:T(8,128)(2,1)S(1)}, u32[]{:S(2)}, u32[]{:S(2)}) collective-permute-start(bf16[64,4096]{1,0:T(8,128)(2,1)S(1)} %get-tuple-element.34), channel_id=1, source_target_pairs={{0,64},{4,68},{8,72},{12,76},{16,80},{20,84},{24,88},{28,92},{32,9... | collective-permute-start | bytes 1572872 | tf_op jit(solution)/shard_map/ppermute | solution.py:86
  20.2 1.7 %collective-permute-start.6 = (bf16[64,4096]{1,0:T(8,128)(2,1)S(1)}, bf16[64,4096]{1,0:T(8,128)(2,1)S(1)}, u32[]{:S(2)}, u32[]{:S(2)}) collective-permute-start(bf16[64,4096]{1,0:T(8,128)(2,1)S(1)} %get-tuple-element.35), channel_id=1, source_target_pairs={{0,192},{4,196},{8,200},{12,204},{16,208},{20,212},{24,216},{28,22... | collective-permute-start | bytes 1572872 | tf_op jit(solution)/shard_map/ppermute | solution.py:86
  21.9 9.2 %collective-permute-done.11.refs_9_ = bf16[64,4096]{1,0:T(8,128)(2,1)S(1)} collective-permute-done((bf16[64,4096]{1,0:T(8,128)(2,1)S(1)}, bf16[64,4096]{1,0:T(8,128)(2,1)S(1)}, u32[]{:S(2)}, u32[]{:S(2)}) %collective-permute-start.11) | collective-permute-done | bytes 524320 | tf_op jit(solution)/shard_map/ppermute | solution.py:86
  31.1 0.8 collective-permute-done.10.refs_8_
  32.0 1.8 %collective-permute-done.4.refs_7_ = bf16[64,4096]{1,0:T(8,128)(2,1)S(1)} collective-permute-done((bf16[64,4096]{1,0:T(8,128)(2,1)S(1)}, bf16[64,4096]{1,0:T(8,128)(2,1)S(1)}, u32[]{:S(2)}, u32[]{:S(2)}) %collective-permute-start.4) | collective-permute-done | bytes 524320 | tf_op jit(solution)/shard_map/ppermute | solution.py:86
  33.8 0.1 collective-permute-done.6.refs_10_
  33.9 0.2 pad_maximum_fusion.4
  34.0 0.0 collective-permute-done.8.refs_12_.refs_7_.refs_9_
  34.0 0.4 collective-permute-start.9
  34.4 2.9 %collective-permute-start.13 = (bf16[64,4096]{1,0:T(8,128)(2,1)S(1)}, bf16[64,4096]{1,0:T(8,128)(2,1)S(1)}, u32[]{:S(2)}, u32[]{:S(2)}) collective-permute-start(bf16[64,4096]{1,0:T(8,128)(2,1)S(1)} %collective-permute-done.10.refs_8_), channel_id=1, source_target_pairs={{0,192},{4,196},{8,200},{12,204},{16,208},{20,212},{24,216},{28,22... | collective-permute-start | bytes 1572872 | tf_op jit(solution)/shard_map/ppermute | solution.py:86
  37.3 3.0 %collective-permute-start.15 = (bf16[64,4096]{1,0:T(8,128)(2,1)S(1)}, bf16[64,4096]{1,0:T(8,128)(2,1)S(1)}, u32[]{:S(2)}, u32[]{:S(2)}) collective-permute-start(bf16[64,4096]{1,0:T(8,128)(2,1)S(1)} %collective-permute-done.4.refs_7_), channel_id=1, source_target_pairs={{0,24},{4,28},{8,0},{12,4},{16,8},{20,12},{24,16},{28,20},{32,56},... | collective-permute-start | bytes 1572872 | tf_op jit(solution)/shard_map/ppermute | solution.py:86
  40.2 0.0 collective-permute-start.17
  40.2 0.0 collective-permute-start.18
  40.3 0.5 constant_dynamic-slice_fusion.4.refs_11_.refs_6_.refs_8_
  40.8 5.7 %early.1 = (f32[32,16,512]{2,1,0:T(8,128)S(1)}, f32[32,16,512]{2,1,0:T(8,128)S(1)}) custom-call(s32[1]{0:T(128)} %bitcast.refs_0_, bf16[32,4096]{1,0:T(8,128)(2,1)S(1)} %pad_maximum_fusion.10.refs_1_, bf16[32,4096]{1,0:T(8,128)(2,1)S(1)} %collective-permute-done.3.refs_2_, bf16[32,4096]{1,0:T(8,128)(2,1)S(1)} %collective-permute-done.1.refs_3_, ...), custom_call_target="tpu_custom_call" | custom-call | flops 3758096384 | bytes 16252928 | tf_op jit(solution)/shard_map/early/pallas_call | solution.py:192
  46.5 0.6 collective-permute-done.9.refs_4_
  47.1 1.3 %collective-permute-start.12 = (bf16[64,4096]{1,0:T(8,128)(2,1)S(1)}, bf16[64,4096]{1,0:T(8,128)(2,1)S(1)}, u32[]{:S(2)}, u32[]{:S(2)}) collective-permute-start(bf16[64,4096]{1,0:T(8,128)(2,1)S(1)} %get-tuple-element.43), channel_id=1, source_target_pairs={{0,32},{4,36},{8,40},{12,44},{16,48},{20,52},{24,56},{28,60},{32,0... | collective-permute-start | bytes 1572872 | tf_op jit(solution)/shard_map/ppermute | solution.py:86
  48.4 0.0 collective-permute-done.13.refs_2_
  48.4 3.3 %collective-permute-start.14 = (bf16[32,4096]{1,0:T(8,128)(2,1)S(1)}, bf16[32,4096]{1,0:T(8,128)(2,1)S(1)}, u32[]{:S(2)}, u32[]{:S(2)}) collective-permute-start(bf16[32,4096]{1,0:T(8,128)(2,1)S(1)} %slice.58), channel_id=1, source_target_pairs={{0,192},{4,196},{8,200},{12,204},{16,208},{20,212},{24,216},{28,22... | collective-permute-start | bytes 786440 | tf_op jit(solution)/shard_map/ppermute | solution.py:86
  51.7 0.0 collective-permute-done.15.refs_1_
  51.7 2.2 %collective-permute-start.16 = (bf16[32,4096]{1,0:T(8,128)(2,1)S(1)}, bf16[32,4096]{1,0:T(8,128)(2,1)S(1)}, u32[]{:S(2)}, u32[]{:S(2)}) collective-permute-start(bf16[32,4096]{1,0:T(8,128)(2,1)S(1)} %slice.58), channel_id=1, source_target_pairs={{0,24},{4,28},{8,0},{12,4},{16,8},{20,12},{24,16},{28,20},{32,56},... | collective-permute-start | bytes 786440 | tf_op jit(solution)/shard_map/ppermute | solution.py:86
  53.9 0.0 collective-permute-done.17.refs_3_
  53.9 0.0 collective-permute-done.18.refs_5_
  54.0 0.1 pad_maximum_fusion.9
  54.0 0.1 collective-permute-start.19
  54.1 0.1 collective-permute-start.20
  54.2 4.5 %mid.1 = (f32[32,16,512]{2,1,0:T(8,128)S(1)}, f32[32,16,512]{2,1,0:T(8,128)S(1)}) custom-call(s32[1]{0:T(128)} %bitcast.refs_0_, bf16[64,4096]{1,0:T(8,128)(2,1)S(1)} %collective-permute-done.15.refs_1_, bf16[64,4096]{1,0:T(8,128)(2,1)S(1)} %collective-permute-done.13.refs_2_, bf16[64,4096]{1,0:T(8,128)(2,1)S(1)} %collective-permute-done.17.refs_3_, ...), custom_call_target="tpu_custom_call" | custom-call | flops 2684354560 | bytes 15204352 | tf_op jit(solution)/shard_map/mid/pallas_call | solution.py:192
  58.7 0.0 collective-permute-done.16.refs_3_
  58.7 2.2 %collective-permute-start.21 = (bf16[16,4096]{1,0:T(8,128)(2,1)S(1)}, bf16[16,4096]{1,0:T(8,128)(2,1)S(1)}, u32[]{:S(2)}, u32[]{:S(2)}) collective-permute-start(bf16[16,4096]{1,0:T(8,128)(2,1)S(1)} %slice.64), channel_id=1, source_target_pairs={{0,24},{4,28},{8,0},{12,4},{16,8},{20,12},{24,16},{28,20},{32,56},... | collective-permute-start | bytes 393224 | tf_op jit(solution)/shard_map/ppermute | solution.py:95
  61.0 3.3 %collective-permute-start.22 = (bf16[16,4096]{1,0:T(8,128)(2,1)S(1)}, bf16[16,4096]{1,0:T(8,128)(2,1)S(1)}, u32[]{:S(2)}, u32[]{:S(2)}) collective-permute-start(bf16[16,4096]{1,0:T(8,128)(2,1)S(1)} %slice.65), channel_id=1, source_target_pairs={{0,192},{4,196},{8,200},{12,204},{16,208},{20,212},{24,216},{28,22... | collective-permute-start | bytes 393224 | tf_op jit(solution)/shard_map/ppermute | solution.py:95
  64.3 0.0 collective-permute-done.21.refs_6_
  64.3 2.5 %collective-permute-done.22.refs_7_ = bf16[16,4096]{1,0:T(8,128)(2,1)S(1)} collective-permute-done((bf16[16,4096]{1,0:T(8,128)(2,1)S(1)}, bf16[16,4096]{1,0:T(8,128)(2,1)S(1)}, u32[]{:S(2)}, u32[]{:S(2)}) %collective-permute-start.22) | collective-permute-done | bytes 131104 | tf_op jit(solution)/shard_map/ppermute | solution.py:95
  66.8 0.0 collective-permute-done.12.refs_1_
  66.8 3.8 %late.1 = (f32[32,16,512]{2,1,0:T(8,128)S(1)}, f32[32,16,512]{2,1,0:T(8,128)S(1)}) custom-call(s32[1]{0:T(128)} %bitcast.refs_0_, bf16[64,4096]{1,0:T(8,128)(2,1)S(1)} %collective-permute-done.12.refs_1_, bf16[32,4096]{1,0:T(8,128)(2,1)S(1)} %collective-permute-done.14.refs_2_, bf16[32,4096]{1,0:T(8,128)(2,1)S(1)} %collective-permute-done.16.refs_3_, ...), custom_call_target="tpu_custom_call" | custom-call | flops 2147483648 | bytes 14680064 | tf_op jit(solution)/shard_map/late/pallas_call | solution.py:192
  70.6 0.1 collective-permute-start.23
  70.7 2.6 %collective-permute-done.23 = f32[32,16,512]{2,1,0:T(8,128)S(1)} collective-permute-done((f32[32,16,512]{2,1,0:T(8,128)S(1)}, f32[32,16,512]{2,1,0:T(8,128)S(1)}, u32[]{:S(2)}, u32[]{:S(2)}) %collective-permute-start.23) | collective-permute-done | bytes 1048608 | tf_op jit(solution)/shard_map/ppermute | solution.py:275
  73.3 1.2 %add.36 = f32[32,16,512]{2,1,0:T(8,128)} add(f32[32,16,512]{2,1,0:T(8,128)S(1)} %get-tuple-element.57, f32[32,16,512]{2,1,0:T(8,128)S(1)} %collective-permute-done.23) | non-fusion elementwise | flops 262144 | bytes 3145728 | tf_op jit(solution)/shard_map/add | solution.py:275
  74.5 8.1 %all-to-all-start = ((f32[32,16,512]{2,1,0:T(8,128)}), f32[32,16,512]{2,1,0:T(8,128)S(1)}, u32[]{:S(2)}, u32[]{:S(2)}) async-start(f32[32,16,512]{2,1,0:T(8,128)} %add.36), calls=%async_computation | async-start | bytes 2097152 | tf_op jit(solution)/shard_map/all_to_all | solution.py:278
  82.6 16.6 %all-to-all-done = f32[32,16,512]{2,1,0:T(8,128)S(1)} async-done(((f32[32,16,512]{2,1,0:T(8,128)}), f32[32,16,512]{2,1,0:T(8,128)S(1)}, u32[]{:S(2)}, u32[]{:S(2)}) %all-to-all-start) | async-done | bytes 1048608 | tf_op jit(solution)/shard_map/all_to_all | solution.py:278
  99.3 0.1 reduce_sum.9
  99.4 3.4 %collective-permute-start.24 = (f32[16,256]{1,0:T(8,128)S(1)}, f32[16,256]{1,0:T(8,128)S(1)}, u32[]{:S(2)}, u32[]{:S(2)}) collective-permute-start(f32[16,256]{1,0:T(8,128)S(1)} %pad_maximum_fusion.11), channel_id=1, source_target_pairs={{0,1},{1,0},{2,3},{3,2},{4,5},{5,4},{6,7},{7,6},{8,9},{9,8},{10,11... | collective-permute-start | bytes 49160 | tf_op jit(solution)/shard_map/ppermute | solution.py:219
  102.7 1.7 %collective-permute-done.24 = f32[16,256]{1,0:T(8,128)S(1)} collective-permute-done((f32[16,256]{1,0:T(8,128)S(1)}, f32[16,256]{1,0:T(8,128)S(1)}, u32[]{:S(2)}, u32[]{:S(2)}) %collective-permute-start.24) | collective-permute-done | bytes 16416 | tf_op jit(solution)/shard_map/ppermute | solution.py:219
  104.5 5.3 %collective-permute-start.25 = (f32[16,128]{1,0:T(8,128)S(1)}, f32[16,128]{1,0:T(8,128)S(1)}, u32[]{:S(2)}, u32[]{:S(2)}) collective-permute-start(f32[16,128]{1,0:T(8,128)S(1)} %slice.67), channel_id=1, source_target_pairs={{0,3},{1,2},{2,1},{3,0},{4,7},{5,6},{6,5},{7,4},{8,11},{9,10},{10,... | collective-permute-start | bytes 24584 | tf_op jit(solution)/shard_map/ppermute | solution.py:219
  109.8 1.6 %collective-permute-done.25 = f32[16,128]{1,0:T(8,128)S(1)} collective-permute-done((f32[16,128]{1,0:T(8,128)S(1)}, f32[16,128]{1,0:T(8,128)S(1)}, u32[]{:S(2)}, u32[]{:S(2)}) %collective-permute-start.25) | collective-permute-done | bytes 8224 | tf_op jit(solution)/shard_map/ppermute | solution.py:219
  111.4 0.6 fusion.1
  (23 shorter events, 0.2 us)
Async XLA Ops:
  1.0 1.4 %collective-permute-start = (bf16[16,4096]{1,0:T(8,128)(2,1)S(1)}, bf16[16,4096]{1,0:T(8,128)(2,1)S(1)}, u32[]{:S(2)}, u32[]{:S(2)}) collective-permute-start(bf16[16,4096]{1,0:T(8,128)(2,1)S(1)} %get-tuple-element.33), channel_id=1, source_target_pairs={{0,4},{4,0},{8,12},{12,8},{16,20},{20,16},{24,28},{28,24},{32,36},... | collective-permute-start | bytes 393224 | tf_op jit(solution)/shard_map/ppermute | solution.py:237
  2.5 9.9 %collective-permute-start.1 = (bf16[32,4096]{1,0:T(8,128)(2,1)S(1)}, bf16[32,4096]{1,0:T(8,128)(2,1)S(1)}, u32[]{:S(2)}, u32[]{:S(2)}) collective-permute-start(bf16[32,4096]{1,0:T(8,128)(2,1)S(1)} %pad_maximum_fusion.10.refs_1_), channel_id=1, source_target_pairs={{0,64},{4,68},{8,72},{12,76},{16,80},{20,84},{24,88},{28,92},{32,9... | collective-permute-start | bytes 786440 | tf_op jit(solution)/shard_map/ppermute | solution.py:86
  4.1 8.3 %collective-permute-start.7 = (bf16[32,4096]{1,0:T(8,128)(2,1)S(1)}, bf16[32,4096]{1,0:T(8,128)(2,1)S(1)}, u32[]{:S(2)}, u32[]{:S(2)}) collective-permute-start(bf16[32,4096]{1,0:T(8,128)(2,1)S(1)} %pad_maximum_fusion.10.refs_1_), channel_id=1, source_target_pairs={{0,32},{4,36},{8,40},{12,44},{16,48},{20,52},{24,56},{28,60},{32,0... | collective-permute-start | bytes 786440 | tf_op jit(solution)/shard_map/ppermute | solution.py:86
  6.0 7.8 %collective-permute-start.3 = (bf16[32,4096]{1,0:T(8,128)(2,1)S(1)}, bf16[32,4096]{1,0:T(8,128)(2,1)S(1)}, u32[]{:S(2)}, u32[]{:S(2)}) collective-permute-start(bf16[32,4096]{1,0:T(8,128)(2,1)S(1)} %pad_maximum_fusion.10.refs_1_), channel_id=1, source_target_pairs={{0,24},{4,28},{8,0},{12,4},{16,8},{20,12},{24,16},{28,20},{32,56},... | collective-permute-start | bytes 786440 | tf_op jit(solution)/shard_map/ppermute | solution.py:86
  6.6 8.5 %collective-permute-start.5 = (bf16[32,4096]{1,0:T(8,128)(2,1)S(1)}, bf16[32,4096]{1,0:T(8,128)(2,1)S(1)}, u32[]{:S(2)}, u32[]{:S(2)}) collective-permute-start(bf16[32,4096]{1,0:T(8,128)(2,1)S(1)} %pad_maximum_fusion.10.refs_1_), channel_id=1, source_target_pairs={{0,8},{4,12},{8,16},{12,20},{16,24},{20,28},{24,0},{28,4},{32,40},... | collective-permute-start | bytes 786440 | tf_op jit(solution)/shard_map/ppermute | solution.py:86
  8.1 7.2 %collective-permute-start.2 = (bf16[32,4096]{1,0:T(8,128)(2,1)S(1)}, bf16[32,4096]{1,0:T(8,128)(2,1)S(1)}, u32[]{:S(2)}, u32[]{:S(2)}) collective-permute-start(bf16[32,4096]{1,0:T(8,128)(2,1)S(1)} %pad_maximum_fusion.10.refs_1_), channel_id=1, source_target_pairs={{0,192},{4,196},{8,200},{12,204},{16,208},{20,212},{24,216},{28,22... | collective-permute-start | bytes 786440 | tf_op jit(solution)/shard_map/ppermute | solution.py:86
  9.7 30.5 %slice-start = ((s8[8388608]{0:T(1024)(128)(4,1)}), s8[4194304]{0:T(1024)(128)(4,1)S(1)}, s32[]{:S(2)}) async-start(s8[8388608]{0:T(1024)(128)(4,1)} %bitcast.9), calls=%async_computation.1 | async-start | bytes 8388608
  12.4 27.9 %slice-start.1 = ((s8[8388608]{0:T(1024)(128)(4,1)}), s8[4194304]{0:T(1024)(128)(4,1)S(1)}, s32[]{:S(2)}) async-start(s8[8388608]{0:T(1024)(128)(4,1)} %bitcast.9), calls=%async_computation.2 | async-start | bytes 8388608
  15.6 18.4 %collective-permute-start.8 = (bf16[512,4096]{1,0:T(8,128)(2,1)S(1)}, bf16[512,4096]{1,0:T(8,128)(2,1)S(1)}, u32[]{:S(2)}, u32[]{:S(2)}) collective-permute-start(bf16[512,4096]{1,0:T(8,128)(2,1)S(1)} %constant_dynamic-slice_fusion.5), channel_id=1, source_target_pairs={{0,4},{4,0},{8,12},{12,8},{16,20},{20,16},{24,28},{28,24},{32,36},... | collective-permute-start | bytes 12582920 | tf_op jit(solution)/shard_map/ppermute | solution.py:256
  15.7 15.3 %collective-permute-start.11 = (bf16[64,4096]{1,0:T(8,128)(2,1)S(1)}, bf16[64,4096]{1,0:T(8,128)(2,1)S(1)}, u32[]{:S(2)}, u32[]{:S(2)}) collective-permute-start(bf16[64,4096]{1,0:T(8,128)(2,1)S(1)} %get-tuple-element.38), channel_id=1, source_target_pairs={{0,8},{4,12},{8,16},{12,20},{16,24},{20,28},{24,0},{28,4},{32,40},... | collective-permute-start | bytes 1572872 | tf_op jit(solution)/shard_map/ppermute | solution.py:86
  17.3 14.6 %collective-permute-start.10 = (bf16[64,4096]{1,0:T(8,128)(2,1)S(1)}, bf16[64,4096]{1,0:T(8,128)(2,1)S(1)}, u32[]{:S(2)}, u32[]{:S(2)}) collective-permute-start(bf16[64,4096]{1,0:T(8,128)(2,1)S(1)} %get-tuple-element.37), channel_id=1, source_target_pairs={{0,24},{4,28},{8,0},{12,4},{16,8},{20,12},{24,16},{28,20},{32,56},... | collective-permute-start | bytes 1572872 | tf_op jit(solution)/shard_map/ppermute | solution.py:86
  18.7 15.1 %collective-permute-start.4 = (bf16[64,4096]{1,0:T(8,128)(2,1)S(1)}, bf16[64,4096]{1,0:T(8,128)(2,1)S(1)}, u32[]{:S(2)}, u32[]{:S(2)}) collective-permute-start(bf16[64,4096]{1,0:T(8,128)(2,1)S(1)} %get-tuple-element.34), channel_id=1, source_target_pairs={{0,64},{4,68},{8,72},{12,76},{16,80},{20,84},{24,88},{28,92},{32,9... | collective-permute-start | bytes 1572872 | tf_op jit(solution)/shard_map/ppermute | solution.py:86
  20.2 13.6 %collective-permute-start.6 = (bf16[64,4096]{1,0:T(8,128)(2,1)S(1)}, bf16[64,4096]{1,0:T(8,128)(2,1)S(1)}, u32[]{:S(2)}, u32[]{:S(2)}) collective-permute-start(bf16[64,4096]{1,0:T(8,128)(2,1)S(1)} %get-tuple-element.35), channel_id=1, source_target_pairs={{0,192},{4,196},{8,200},{12,204},{16,208},{20,212},{24,216},{28,22... | collective-permute-start | bytes 1572872 | tf_op jit(solution)/shard_map/ppermute | solution.py:86
  34.0 13.1 %collective-permute-start.9 = (bf16[64,4096]{1,0:T(8,128)(2,1)S(1)}, bf16[64,4096]{1,0:T(8,128)(2,1)S(1)}, u32[]{:S(2)}, u32[]{:S(2)}) collective-permute-start(bf16[64,4096]{1,0:T(8,128)(2,1)S(1)} %get-tuple-element.40), channel_id=1, source_target_pairs={{0,32},{4,36},{8,40},{12,44},{16,48},{20,52},{24,56},{28,60},{32,0... | collective-permute-start | bytes 1572872 | tf_op jit(solution)/shard_map/ppermute | solution.py:86
  34.4 14.0 %collective-permute-start.13 = (bf16[64,4096]{1,0:T(8,128)(2,1)S(1)}, bf16[64,4096]{1,0:T(8,128)(2,1)S(1)}, u32[]{:S(2)}, u32[]{:S(2)}) collective-permute-start(bf16[64,4096]{1,0:T(8,128)(2,1)S(1)} %collective-permute-done.10.refs_8_), channel_id=1, source_target_pairs={{0,192},{4,196},{8,200},{12,204},{16,208},{20,212},{24,216},{28,22... | collective-permute-start | bytes 1572872 | tf_op jit(solution)/shard_map/ppermute | solution.py:86
  37.3 14.4 %collective-permute-start.15 = (bf16[64,4096]{1,0:T(8,128)(2,1)S(1)}, bf16[64,4096]{1,0:T(8,128)(2,1)S(1)}, u32[]{:S(2)}, u32[]{:S(2)}) collective-permute-start(bf16[64,4096]{1,0:T(8,128)(2,1)S(1)} %collective-permute-done.4.refs_7_), channel_id=1, source_target_pairs={{0,24},{4,28},{8,0},{12,4},{16,8},{20,12},{24,16},{28,20},{32,56},... | collective-permute-start | bytes 1572872 | tf_op jit(solution)/shard_map/ppermute | solution.py:86
  40.2 13.7 %collective-permute-start.17 = (bf16[64,4096]{1,0:T(8,128)(2,1)S(1)}, bf16[64,4096]{1,0:T(8,128)(2,1)S(1)}, u32[]{:S(2)}, u32[]{:S(2)}) collective-permute-start(bf16[64,4096]{1,0:T(8,128)(2,1)S(1)} %get-tuple-element.48), channel_id=1, source_target_pairs={{0,64},{4,68},{8,72},{12,76},{16,80},{20,84},{24,88},{28,92},{32,9... | collective-permute-start | bytes 1572872 | tf_op jit(solution)/shard_map/ppermute | solution.py:86
  40.2 13.7 %collective-permute-start.18 = (bf16[64,4096]{1,0:T(8,128)(2,1)S(1)}, bf16[64,4096]{1,0:T(8,128)(2,1)S(1)}, u32[]{:S(2)}, u32[]{:S(2)}) collective-permute-start(bf16[64,4096]{1,0:T(8,128)(2,1)S(1)} %get-tuple-element.49), channel_id=1, source_target_pairs={{0,8},{4,12},{8,16},{12,20},{16,24},{20,28},{24,0},{28,4},{32,40},... | collective-permute-start | bytes 1572872 | tf_op jit(solution)/shard_map/ppermute | solution.py:86
  47.1 19.7 %collective-permute-start.12 = (bf16[64,4096]{1,0:T(8,128)(2,1)S(1)}, bf16[64,4096]{1,0:T(8,128)(2,1)S(1)}, u32[]{:S(2)}, u32[]{:S(2)}) collective-permute-start(bf16[64,4096]{1,0:T(8,128)(2,1)S(1)} %get-tuple-element.43), channel_id=1, source_target_pairs={{0,32},{4,36},{8,40},{12,44},{16,48},{20,52},{24,56},{28,60},{32,0... | collective-permute-start | bytes 1572872 | tf_op jit(solution)/shard_map/ppermute | solution.py:86
  48.4 10.3 %collective-permute-start.14 = (bf16[32,4096]{1,0:T(8,128)(2,1)S(1)}, bf16[32,4096]{1,0:T(8,128)(2,1)S(1)}, u32[]{:S(2)}, u32[]{:S(2)}) collective-permute-start(bf16[32,4096]{1,0:T(8,128)(2,1)S(1)} %slice.58), channel_id=1, source_target_pairs={{0,192},{4,196},{8,200},{12,204},{16,208},{20,212},{24,216},{28,22... | collective-permute-start | bytes 786440 | tf_op jit(solution)/shard_map/ppermute | solution.py:86
  51.7 7.0 %collective-permute-start.16 = (bf16[32,4096]{1,0:T(8,128)(2,1)S(1)}, bf16[32,4096]{1,0:T(8,128)(2,1)S(1)}, u32[]{:S(2)}, u32[]{:S(2)}) collective-permute-start(bf16[32,4096]{1,0:T(8,128)(2,1)S(1)} %slice.58), channel_id=1, source_target_pairs={{0,24},{4,28},{8,0},{12,4},{16,8},{20,12},{24,16},{28,20},{32,56},... | collective-permute-start | bytes 786440 | tf_op jit(solution)/shard_map/ppermute | solution.py:86
  54.0 10.2 %collective-permute-start.19 = (bf16[48,4096]{1,0:T(8,128)(2,1)S(1)}, bf16[48,4096]{1,0:T(8,128)(2,1)S(1)}, u32[]{:S(2)}, u32[]{:S(2)}) collective-permute-start(bf16[48,4096]{1,0:T(8,128)(2,1)S(1)} %get-tuple-element.50), channel_id=1, source_target_pairs={{0,8},{4,12},{8,16},{12,20},{16,24},{20,28},{24,0},{28,4},{32,40},... | collective-permute-start | bytes 1179656 | tf_op jit(solution)/shard_map/ppermute | solution.py:110
  54.1 10.1 %collective-permute-start.20 = (bf16[48,4096]{1,0:T(8,128)(2,1)S(1)}, bf16[48,4096]{1,0:T(8,128)(2,1)S(1)}, u32[]{:S(2)}, u32[]{:S(2)}) collective-permute-start(bf16[48,4096]{1,0:T(8,128)(2,1)S(1)} %get-tuple-element.51), channel_id=1, source_target_pairs={{0,64},{4,68},{8,72},{12,76},{16,80},{20,84},{24,88},{28,92},{32,9... | collective-permute-start | bytes 1179656 | tf_op jit(solution)/shard_map/ppermute | solution.py:110
  58.7 5.5 %collective-permute-start.21 = (bf16[16,4096]{1,0:T(8,128)(2,1)S(1)}, bf16[16,4096]{1,0:T(8,128)(2,1)S(1)}, u32[]{:S(2)}, u32[]{:S(2)}) collective-permute-start(bf16[16,4096]{1,0:T(8,128)(2,1)S(1)} %slice.64), channel_id=1, source_target_pairs={{0,24},{4,28},{8,0},{12,4},{16,8},{20,12},{24,16},{28,20},{32,56},... | collective-permute-start | bytes 393224 | tf_op jit(solution)/shard_map/ppermute | solution.py:95
  61.0 5.8 %collective-permute-start.22 = (bf16[16,4096]{1,0:T(8,128)(2,1)S(1)}, bf16[16,4096]{1,0:T(8,128)(2,1)S(1)}, u32[]{:S(2)}, u32[]{:S(2)}) collective-permute-start(bf16[16,4096]{1,0:T(8,128)(2,1)S(1)} %slice.65), channel_id=1, source_target_pairs={{0,192},{4,196},{8,200},{12,204},{16,208},{20,212},{24,216},{28,22... | collective-permute-start | bytes 393224 | tf_op jit(solution)/shard_map/ppermute | solution.py:95
  70.6 2.7 %collective-permute-start.23 = (f32[32,16,512]{2,1,0:T(8,128)S(1)}, f32[32,16,512]{2,1,0:T(8,128)S(1)}, u32[]{:S(2)}, u32[]{:S(2)}) collective-permute-start(f32[32,16,512]{2,1,0:T(8,128)S(1)} %get-tuple-element.58), channel_id=1, source_target_pairs={{0,4},{4,0},{8,12},{12,8},{16,20},{20,16},{24,28},{28,24},{32,36},... | collective-permute-start | bytes 3145736 | tf_op jit(solution)/shard_map/ppermute | solution.py:275
  74.5 24.7 %all-to-all-start = ((f32[32,16,512]{2,1,0:T(8,128)}), f32[32,16,512]{2,1,0:T(8,128)S(1)}, u32[]{:S(2)}, u32[]{:S(2)}) async-start(f32[32,16,512]{2,1,0:T(8,128)} %add.36), calls=%async_computation | async-start | bytes 2097152 | tf_op jit(solution)/shard_map/all_to_all | solution.py:278
  99.4 5.1 %collective-permute-start.24 = (f32[16,256]{1,0:T(8,128)S(1)}, f32[16,256]{1,0:T(8,128)S(1)}, u32[]{:S(2)}, u32[]{:S(2)}) collective-permute-start(f32[16,256]{1,0:T(8,128)S(1)} %pad_maximum_fusion.11), channel_id=1, source_target_pairs={{0,1},{1,0},{2,3},{3,2},{4,5},{5,4},{6,7},{7,6},{8,9},{9,8},{10,11... | collective-permute-start | bytes 49160 | tf_op jit(solution)/shard_map/ppermute | solution.py:219
  104.5 7.0 %collective-permute-start.25 = (f32[16,128]{1,0:T(8,128)S(1)}, f32[16,128]{1,0:T(8,128)S(1)}, u32[]{:S(2)}, u32[]{:S(2)}) collective-permute-start(f32[16,128]{1,0:T(8,128)S(1)} %slice.67), channel_id=1, source_target_pairs={{0,3},{1,2},{2,1},{3,0},{4,7},{5,6},{6,5},{7,4},{8,11},{9,10},{10,... | collective-permute-start | bytes 24584 | tf_op jit(solution)/shard_map/ppermute | solution.py:219

commit v5 on v4

--- a/solution.py
+++ b/solution.py
@@ -175,7 +175,7 @@
             place(out, keep, 1 - core, columns)
 
 
-TILE = 256
+TILE = 512
 
 
 def multiply(me, names, bundles, weights, before, name):

time: 112 us -> 110 us (0.982)
  Pallas kernels: 14 us -> 11.5 us
  waiting for transfers between devices: 41.9 us -> 44.1 us
  starting transfers between devices: 49.1 us -> 47.5 us
    pallas_call x3, Pallas kernels: 14 us -> 11.5 us  [multiply(): pl.pallas_call(functools.partial(multiply_kernel, names, len(bundles), k,...]
    ppermute x17, waiting for transfers between devices: 15.4 us -> 17.1 us  [send(): chain[link] = [lax.ppermute(r, 'tm', pairs(link))]]
  transfers between devices with their start and end apart: 27 -> 27, of which waited for: 14 -> 16; matrix products, arithmetic and copies ran while one was open for 3% -> 3% of each run, Pallas kernels for 9% -> 8%
where the time goes in v5:
time: 110 us
  starting transfers between devices  47.5 us (43%)
  waiting for transfers between devices  44.1 us (40%)
  Pallas kernels  11.5 us (10%)
  local copies, waits for them, and re-layouts  4.27 us (4%)
  other arithmetic  2.42 us (2%)
    ppermute x17, starting transfers between devices, send(): chain[link] = [lax.ppermute(r, 'tm', pairs(link))]  26.4 us
    ppermute x17, waiting for transfers between devices, send(): chain[link] = [lax.ppermute(r, 'tm', pairs(link))]  17.1 us
    all_to_all x1, waiting for transfers between devices, local(): lax.all_to_all(both, 'tm', 0, 0, tiled=True, axis_index_groups=SAME_CORE)  16.6 us
    pallas_call x3, Pallas kernels, multiply(): pl.pallas_call(functools.partial(multiply_kernel, names, len(bundles), k,...  11.5 us
    ppermute x2, starting transfers between devices, swap(): return lax.ppermute(value, 'floor', [(f, f ^ by) for f in range(len(at))])  8.39 us
    all_to_all x1, starting transfers between devices, local(): lax.all_to_all(both, 'tm', 0, 0, tiled=True, axis_index_groups=SAME_CORE)  7.56 us
    ppermute x2, starting transfers between devices, send_last(): lax.ppermute(after(r[n * k:(n + 1) * k], wait, *chain[link]), 'tm', pairs...  4.73 us
    dynamic_slice x3, local copies, waits for them, and re-layouts, columns(): return lax.dynamic_slice_in_dim(rows, which * half, half, 1)  4.09 us
  transfers between devices with their start and end apart: 27, of which 16 were waited for; matrix products, arithmetic and copies ran while one was open for 3% of the time, Pallas kernels for 8%

profile of v5, /device:TPU:2, one launch (start us, length us, event | category | flops | bytes accessed | tf_op | source)
XLA Modules:
  0.0 110.1 jit_solution(3943475506873854385)
XLA Ops:
  0.0 1.0 dynamic-slice_bitcast_fusion
  1.0 0.1 collective-permute-start
  1.1 1.3 %collective-permute-done = bf16[16,4096]{1,0:T(8,128)(2,1)S(1)} collective-permute-done((bf16[16,4096]{1,0:T(8,128)(2,1)S(1)}, bf16[16,4096]{1,0:T(8,128)(2,1)S(1)}, u32[]{:S(2)}, u32[]{:S(2)}) %collective-permute-start) | collective-permute-done | bytes 131104 | tf_op jit(solution)/shard_map/ppermute | solution.py:237
  2.5 1.7 %collective-permute-start.1 = (bf16[32,4096]{1,0:T(8,128)(2,1)S(1)}, bf16[32,4096]{1,0:T(8,128)(2,1)S(1)}, u32[]{:S(2)}, u32[]{:S(2)}) collective-permute-start(bf16[32,4096]{1,0:T(8,128)(2,1)S(1)} %pad_maximum_fusion.10.refs_1_), channel_id=1, source_target_pairs={{0,64},{4,68},{8,72},{12,76},{16,80},{20,84},{24,88},{28,92},{32,9... | collective-permute-start | bytes 786440 | tf_op jit(solution)/shard_map/ppermute | solution.py:86
  4.1 1.9 %collective-permute-start.7 = (bf16[32,4096]{1,0:T(8,128)(2,1)S(1)}, bf16[32,4096]{1,0:T(8,128)(2,1)S(1)}, u32[]{:S(2)}, u32[]{:S(2)}) collective-permute-start(bf16[32,4096]{1,0:T(8,128)(2,1)S(1)} %pad_maximum_fusion.10.refs_1_), channel_id=1, source_target_pairs={{0,32},{4,36},{8,40},{12,44},{16,48},{20,52},{24,56},{28,60},{32,0... | collective-permute-start | bytes 786440 | tf_op jit(solution)/shard_map/ppermute | solution.py:86
  6.0 0.5 collective-permute-start.3
  6.6 1.5 %collective-permute-start.5 = (bf16[32,4096]{1,0:T(8,128)(2,1)S(1)}, bf16[32,4096]{1,0:T(8,128)(2,1)S(1)}, u32[]{:S(2)}, u32[]{:S(2)}) collective-permute-start(bf16[32,4096]{1,0:T(8,128)(2,1)S(1)} %pad_maximum_fusion.10.refs_1_), channel_id=1, source_target_pairs={{0,8},{4,12},{8,16},{12,20},{16,24},{20,28},{24,0},{28,4},{32,40},... | collective-permute-start | bytes 786440 | tf_op jit(solution)/shard_map/ppermute | solution.py:86
  8.1 1.7 %collective-permute-start.2 = (bf16[32,4096]{1,0:T(8,128)(2,1)S(1)}, bf16[32,4096]{1,0:T(8,128)(2,1)S(1)}, u32[]{:S(2)}, u32[]{:S(2)}) collective-permute-start(bf16[32,4096]{1,0:T(8,128)(2,1)S(1)} %pad_maximum_fusion.10.refs_1_), channel_id=1, source_target_pairs={{0,192},{4,196},{8,200},{12,204},{16,208},{20,212},{24,216},{28,22... | collective-permute-start | bytes 786440 | tf_op jit(solution)/shard_map/ppermute | solution.py:86
  9.7 2.6 %constant_dynamic-slice_fusion.5 = bf16[512,4096]{1,0:T(8,128)(2,1)S(1)} fusion(bf16[512,8192]{1,0:T(8,128)(2,1)} %bitcast.8, s32[]{:T(128)S(6)} %select_n.42), kind=kLoop, calls=%fused_computation.25 | loop fusion | bytes 8388612 | tf_op jit(solution)/shard_map/dynamic_slice | solution.py:232
  12.4 0.0 slice-start.1
  12.4 0.0 collective-permute-done.1.refs_3_
  12.4 0.0 collective-permute-done.7.refs_4_
  12.4 1.5 %collective-permute-done.3.refs_2_ = bf16[32,4096]{1,0:T(8,128)(2,1)S(1)} collective-permute-done((bf16[32,4096]{1,0:T(8,128)(2,1)S(1)}, bf16[32,4096]{1,0:T(8,128)(2,1)S(1)}, u32[]{:S(2)}, u32[]{:S(2)}) %collective-permute-start.3) | collective-permute-done | bytes 262176 | tf_op jit(solution)/shard_map/ppermute | solution.py:86
  13.8 1.3 %collective-permute-done.5.refs_5_ = bf16[32,4096]{1,0:T(8,128)(2,1)S(1)} collective-permute-done((bf16[32,4096]{1,0:T(8,128)(2,1)S(1)}, bf16[32,4096]{1,0:T(8,128)(2,1)S(1)}, u32[]{:S(2)}, u32[]{:S(2)}) %collective-permute-start.5) | collective-permute-done | bytes 262176 | tf_op jit(solution)/shard_map/ppermute | solution.py:86
  15.1 0.2 collective-permute-done.2.refs_6_
  15.3 0.3 pad_maximum_fusion.7
  15.6 0.1 collective-permute-start.8
  15.7 1.6 %collective-permute-start.11 = (bf16[64,4096]{1,0:T(8,128)(2,1)S(1)}, bf16[64,4096]{1,0:T(8,128)(2,1)S(1)}, u32[]{:S(2)}, u32[]{:S(2)}) collective-permute-start(bf16[64,4096]{1,0:T(8,128)(2,1)S(1)} %get-tuple-element.38), channel_id=1, source_target_pairs={{0,8},{4,12},{8,16},{12,20},{16,24},{20,28},{24,0},{28,4},{32,40},... | collective-permute-start | bytes 1572872 | tf_op jit(solution)/shard_map/ppermute | solution.py:86
  17.3 1.4 %collective-permute-start.10 = (bf16[64,4096]{1,0:T(8,128)(2,1)S(1)}, bf16[64,4096]{1,0:T(8,128)(2,1)S(1)}, u32[]{:S(2)}, u32[]{:S(2)}) collective-permute-start(bf16[64,4096]{1,0:T(8,128)(2,1)S(1)} %get-tuple-element.37), channel_id=1, source_target_pairs={{0,24},{4,28},{8,0},{12,4},{16,8},{20,12},{24,16},{28,20},{32,56},... | collective-permute-start | bytes 1572872 | tf_op jit(solution)/shard_map/ppermute | solution.py:86
  18.7 1.6 %collective-permute-start.4 = (bf16[64,4096]{1,0:T(8,128)(2,1)S(1)}, bf16[64,4096]{1,0:T(8,128)(2,1)S(1)}, u32[]{:S(2)}, u32[]{:S(2)}) collective-permute-start(bf16[64,4096]{1,0:T(8,128)(2,1)S(1)} %get-tuple-element.34), channel_id=1, source_target_pairs={{0,64},{4,68},{8,72},{12,76},{16,80},{20,84},{24,88},{28,92},{32,9... | collective-permute-start | bytes 1572872 | tf_op jit(solution)/shard_map/ppermute | solution.py:86
  20.2 1.7 %collective-permute-start.6 = (bf16[64,4096]{1,0:T(8,128)(2,1)S(1)}, bf16[64,4096]{1,0:T(8,128)(2,1)S(1)}, u32[]{:S(2)}, u32[]{:S(2)}) collective-permute-start(bf16[64,4096]{1,0:T(8,128)(2,1)S(1)} %get-tuple-element.35), channel_id=1, source_target_pairs={{0,192},{4,196},{8,200},{12,204},{16,208},{20,212},{24,216},{28,22... | collective-permute-start | bytes 1572872 | tf_op jit(solution)/shard_map/ppermute | solution.py:86
  21.9 9.2 %collective-permute-done.11.refs_9_ = bf16[64,4096]{1,0:T(8,128)(2,1)S(1)} collective-permute-done((bf16[64,4096]{1,0:T(8,128)(2,1)S(1)}, bf16[64,4096]{1,0:T(8,128)(2,1)S(1)}, u32[]{:S(2)}, u32[]{:S(2)}) %collective-permute-start.11) | collective-permute-done | bytes 524320 | tf_op jit(solution)/shard_map/ppermute | solution.py:86
  31.1 0.8 collective-permute-done.10.refs_8_
  32.0 1.8 %collective-permute-done.4.refs_7_ = bf16[64,4096]{1,0:T(8,128)(2,1)S(1)} collective-permute-done((bf16[64,4096]{1,0:T(8,128)(2,1)S(1)}, bf16[64,4096]{1,0:T(8,128)(2,1)S(1)}, u32[]{:S(2)}, u32[]{:S(2)}) %collective-permute-start.4) | collective-permute-done | bytes 524320 | tf_op jit(solution)/shard_map/ppermute | solution.py:86
  33.8 0.1 collective-permute-done.6.refs_10_
  33.9 0.2 pad_maximum_fusion.4
  34.0 0.0 collective-permute-done.8.refs_12_.refs_7_.refs_9_
  34.0 0.4 collective-permute-start.9
  34.4 2.9 %collective-permute-start.13 = (bf16[64,4096]{1,0:T(8,128)(2,1)S(1)}, bf16[64,4096]{1,0:T(8,128)(2,1)S(1)}, u32[]{:S(2)}, u32[]{:S(2)}) collective-permute-start(bf16[64,4096]{1,0:T(8,128)(2,1)S(1)} %collective-permute-done.10.refs_8_), channel_id=1, source_target_pairs={{0,192},{4,196},{8,200},{12,204},{16,208},{20,212},{24,216},{28,22... | collective-permute-start | bytes 1572872 | tf_op jit(solution)/shard_map/ppermute | solution.py:86
  37.3 3.0 %collective-permute-start.15 = (bf16[64,4096]{1,0:T(8,128)(2,1)S(1)}, bf16[64,4096]{1,0:T(8,128)(2,1)S(1)}, u32[]{:S(2)}, u32[]{:S(2)}) collective-permute-start(bf16[64,4096]{1,0:T(8,128)(2,1)S(1)} %collective-permute-done.4.refs_7_), channel_id=1, source_target_pairs={{0,24},{4,28},{8,0},{12,4},{16,8},{20,12},{24,16},{28,20},{32,56},... | collective-permute-start | bytes 1572872 | tf_op jit(solution)/shard_map/ppermute | solution.py:86
  40.2 0.0 collective-permute-start.17
  40.2 0.0 collective-permute-start.18
  40.3 0.5 constant_dynamic-slice_fusion.4.refs_11_.refs_6_.refs_8_
  40.8 4.8 %early.1 = (f32[32,16,512]{2,1,0:T(8,128)S(1)}, f32[32,16,512]{2,1,0:T(8,128)S(1)}) custom-call(s32[1]{0:T(128)} %bitcast.refs_0_, bf16[32,4096]{1,0:T(8,128)(2,1)S(1)} %pad_maximum_fusion.10.refs_1_, bf16[32,4096]{1,0:T(8,128)(2,1)S(1)} %collective-permute-done.3.refs_2_, bf16[32,4096]{1,0:T(8,128)(2,1)S(1)} %collective-permute-done.1.refs_3_, ...), custom_call_target="tpu_custom_call" | custom-call | flops 3758096384 | bytes 16252928 | tf_op jit(solution)/shard_map/early/pallas_call | solution.py:192
  45.6 1.5 %collective-permute-done.9.refs_4_ = bf16[64,4096]{1,0:T(8,128)(2,1)S(1)} collective-permute-done((bf16[64,4096]{1,0:T(8,128)(2,1)S(1)}, bf16[64,4096]{1,0:T(8,128)(2,1)S(1)}, u32[]{:S(2)}, u32[]{:S(2)}) %collective-permute-start.9) | collective-permute-done | bytes 524320 | tf_op jit(solution)/shard_map/ppermute | solution.py:86
  47.1 0.3 collective-permute-start.12
  47.4 0.0 collective-permute-done.13.refs_2_
  47.4 3.7 %collective-permute-start.14 = (bf16[32,4096]{1,0:T(8,128)(2,1)S(1)}, bf16[32,4096]{1,0:T(8,128)(2,1)S(1)}, u32[]{:S(2)}, u32[]{:S(2)}) collective-permute-start(bf16[32,4096]{1,0:T(8,128)(2,1)S(1)} %slice.58), channel_id=1, source_target_pairs={{0,192},{4,196},{8,200},{12,204},{16,208},{20,212},{24,216},{28,22... | collective-permute-start | bytes 786440 | tf_op jit(solution)/shard_map/ppermute | solution.py:86
  51.1 0.0 collective-permute-done.15.refs_1_
  51.1 2.8 %collective-permute-start.16 = (bf16[32,4096]{1,0:T(8,128)(2,1)S(1)}, bf16[32,4096]{1,0:T(8,128)(2,1)S(1)}, u32[]{:S(2)}, u32[]{:S(2)}) collective-permute-start(bf16[32,4096]{1,0:T(8,128)(2,1)S(1)} %slice.58), channel_id=1, source_target_pairs={{0,24},{4,28},{8,0},{12,4},{16,8},{20,12},{24,16},{28,20},{32,56},... | collective-permute-start | bytes 786440 | tf_op jit(solution)/shard_map/ppermute | solution.py:86
  53.9 0.0 collective-permute-done.17.refs_3_
  54.0 0.1 pad_maximum_fusion.9
  54.0 0.1 collective-permute-start.19
  54.1 0.1 collective-permute-start.20
  54.2 3.6 %mid.1 = (f32[32,16,512]{2,1,0:T(8,128)S(1)}, f32[32,16,512]{2,1,0:T(8,128)S(1)}) custom-call(s32[1]{0:T(128)} %bitcast.refs_0_, bf16[64,4096]{1,0:T(8,128)(2,1)S(1)} %collective-permute-done.15.refs_1_, bf16[64,4096]{1,0:T(8,128)(2,1)S(1)} %collective-permute-done.13.refs_2_, bf16[64,4096]{1,0:T(8,128)(2,1)S(1)} %collective-permute-done.17.refs_3_, ...), custom_call_target="tpu_custom_call" | custom-call | flops 2684354560 | bytes 15204352 | tf_op jit(solution)/shard_map/mid/pallas_call | solution.py:192
  57.9 0.8 collective-permute-done.16.refs_3_
  58.7 2.5 %collective-permute-start.21 = (bf16[16,4096]{1,0:T(8,128)(2,1)S(1)}, bf16[16,4096]{1,0:T(8,128)(2,1)S(1)}, u32[]{:S(2)}, u32[]{:S(2)}) collective-permute-start(bf16[16,4096]{1,0:T(8,128)(2,1)S(1)} %slice.64), channel_id=1, source_target_pairs={{0,24},{4,28},{8,0},{12,4},{16,8},{20,12},{24,16},{28,20},{32,56},... | collective-permute-start | bytes 393224 | tf_op jit(solution)/shard_map/ppermute | solution.py:95
  61.2 2.3 %collective-permute-start.22 = (bf16[16,4096]{1,0:T(8,128)(2,1)S(1)}, bf16[16,4096]{1,0:T(8,128)(2,1)S(1)}, u32[]{:S(2)}, u32[]{:S(2)}) collective-permute-start(bf16[16,4096]{1,0:T(8,128)(2,1)S(1)} %slice.65), channel_id=1, source_target_pairs={{0,192},{4,196},{8,200},{12,204},{16,208},{20,212},{24,216},{28,22... | collective-permute-start | bytes 393224 | tf_op jit(solution)/shard_map/ppermute | solution.py:95
  63.4 0.0 collective-permute-done.19.refs_4_
  63.4 0.0 collective-permute-done.20.refs_5_
  63.4 0.2 collective-permute-done.21.refs_6_
  63.7 2.8 %collective-permute-done.22.refs_7_ = bf16[16,4096]{1,0:T(8,128)(2,1)S(1)} collective-permute-done((bf16[16,4096]{1,0:T(8,128)(2,1)S(1)}, bf16[16,4096]{1,0:T(8,128)(2,1)S(1)}, u32[]{:S(2)}, u32[]{:S(2)}) %collective-permute-start.22) | collective-permute-done | bytes 131104 | tf_op jit(solution)/shard_map/ppermute | solution.py:95
  66.4 3.0 %late.1 = (f32[32,16,512]{2,1,0:T(8,128)S(1)}, f32[32,16,512]{2,1,0:T(8,128)S(1)}) custom-call(s32[1]{0:T(128)} %bitcast.refs_0_, bf16[64,4096]{1,0:T(8,128)(2,1)S(1)} %collective-permute-done.12.refs_1_, bf16[32,4096]{1,0:T(8,128)(2,1)S(1)} %collective-permute-done.14.refs_2_, bf16[32,4096]{1,0:T(8,128)(2,1)S(1)} %collective-permute-done.16.refs_3_, ...), custom_call_target="tpu_custom_call" | custom-call | flops 2147483648 | bytes 14680064 | tf_op jit(solution)/shard_map/late/pallas_call | solution.py:192
  69.5 0.1 collective-permute-start.23
  69.6 2.6 %collective-permute-done.23 = f32[32,16,512]{2,1,0:T(8,128)S(1)} collective-permute-done((f32[32,16,512]{2,1,0:T(8,128)S(1)}, f32[32,16,512]{2,1,0:T(8,128)S(1)}, u32[]{:S(2)}, u32[]{:S(2)}) %collective-permute-start.23) | collective-permute-done | bytes 1048608 | tf_op jit(solution)/shard_map/ppermute | solution.py:275
  72.2 1.2 %add.36 = f32[32,16,512]{2,1,0:T(8,128)} add(f32[32,16,512]{2,1,0:T(8,128)S(1)} %get-tuple-element.57, f32[32,16,512]{2,1,0:T(8,128)S(1)} %collective-permute-done.23) | non-fusion elementwise | flops 262144 | bytes 3145728 | tf_op jit(solution)/shard_map/add | solution.py:275
  73.4 7.6 %all-to-all-start = ((f32[32,16,512]{2,1,0:T(8,128)}), f32[32,16,512]{2,1,0:T(8,128)S(1)}, u32[]{:S(2)}, u32[]{:S(2)}) async-start(f32[32,16,512]{2,1,0:T(8,128)} %add.36), calls=%async_computation | async-start | bytes 2097152 | tf_op jit(solution)/shard_map/all_to_all | solution.py:278
  81.0 16.6 %all-to-all-done = f32[32,16,512]{2,1,0:T(8,128)S(1)} async-done(((f32[32,16,512]{2,1,0:T(8,128)}), f32[32,16,512]{2,1,0:T(8,128)S(1)}, u32[]{:S(2)}, u32[]{:S(2)}) %all-to-all-start) | async-done | bytes 1048608 | tf_op jit(solution)/shard_map/all_to_all | solution.py:278
  97.6 0.1 reduce_sum.9
  97.7 3.3 %collective-permute-start.24 = (f32[16,256]{1,0:T(8,128)S(1)}, f32[16,256]{1,0:T(8,128)S(1)}, u32[]{:S(2)}, u32[]{:S(2)}) collective-permute-start(f32[16,256]{1,0:T(8,128)S(1)} %pad_maximum_fusion.11), channel_id=1, source_target_pairs={{0,1},{1,0},{2,3},{3,2},{4,5},{5,4},{6,7},{7,6},{8,9},{9,8},{10,11... | collective-permute-start | bytes 49160 | tf_op jit(solution)/shard_map/ppermute | solution.py:219
  101.1 1.7 %collective-permute-done.24 = f32[16,256]{1,0:T(8,128)S(1)} collective-permute-done((f32[16,256]{1,0:T(8,128)S(1)}, f32[16,256]{1,0:T(8,128)S(1)}, u32[]{:S(2)}, u32[]{:S(2)}) %collective-permute-start.24) | collective-permute-done | bytes 16416 | tf_op jit(solution)/shard_map/ppermute | solution.py:219
  102.8 5.0 %collective-permute-start.25 = (f32[16,128]{1,0:T(8,128)S(1)}, f32[16,128]{1,0:T(8,128)S(1)}, u32[]{:S(2)}, u32[]{:S(2)}) collective-permute-start(f32[16,128]{1,0:T(8,128)S(1)} %slice.67), channel_id=1, source_target_pairs={{0,3},{1,2},{2,1},{3,0},{4,7},{5,6},{6,5},{7,4},{8,11},{9,10},{10,... | collective-permute-start | bytes 24584 | tf_op jit(solution)/shard_map/ppermute | solution.py:219
  107.9 1.6 %collective-permute-done.25 = f32[16,128]{1,0:T(8,128)S(1)} collective-permute-done((f32[16,128]{1,0:T(8,128)S(1)}, f32[16,128]{1,0:T(8,128)S(1)}, u32[]{:S(2)}, u32[]{:S(2)}) %collective-permute-start.25) | collective-permute-done | bytes 8224 | tf_op jit(solution)/shard_map/ppermute | solution.py:219
  109.5 0.6 fusion.1
  (23 shorter events, 0.2 us)
Async XLA Ops:
  1.0 1.4 %collective-permute-start = (bf16[16,4096]{1,0:T(8,128)(2,1)S(1)}, bf16[16,4096]{1,0:T(8,128)(2,1)S(1)}, u32[]{:S(2)}, u32[]{:S(2)}) collective-permute-start(bf16[16,4096]{1,0:T(8,128)(2,1)S(1)} %get-tuple-element.33), channel_id=1, source_target_pairs={{0,4},{4,0},{8,12},{12,8},{16,20},{20,16},{24,28},{28,24},{32,36},... | collective-permute-start | bytes 393224 | tf_op jit(solution)/shard_map/ppermute | solution.py:237
  2.5 9.9 %collective-permute-start.1 = (bf16[32,4096]{1,0:T(8,128)(2,1)S(1)}, bf16[32,4096]{1,0:T(8,128)(2,1)S(1)}, u32[]{:S(2)}, u32[]{:S(2)}) collective-permute-start(bf16[32,4096]{1,0:T(8,128)(2,1)S(1)} %pad_maximum_fusion.10.refs_1_), channel_id=1, source_target_pairs={{0,64},{4,68},{8,72},{12,76},{16,80},{20,84},{24,88},{28,92},{32,9... | collective-permute-start | bytes 786440 | tf_op jit(solution)/shard_map/ppermute | solution.py:86
  4.1 8.3 %collective-permute-start.7 = (bf16[32,4096]{1,0:T(8,128)(2,1)S(1)}, bf16[32,4096]{1,0:T(8,128)(2,1)S(1)}, u32[]{:S(2)}, u32[]{:S(2)}) collective-permute-start(bf16[32,4096]{1,0:T(8,128)(2,1)S(1)} %pad_maximum_fusion.10.refs_1_), channel_id=1, source_target_pairs={{0,32},{4,36},{8,40},{12,44},{16,48},{20,52},{24,56},{28,60},{32,0... | collective-permute-start | bytes 786440 | tf_op jit(solution)/shard_map/ppermute | solution.py:86
  6.0 7.8 %collective-permute-start.3 = (bf16[32,4096]{1,0:T(8,128)(2,1)S(1)}, bf16[32,4096]{1,0:T(8,128)(2,1)S(1)}, u32[]{:S(2)}, u32[]{:S(2)}) collective-permute-start(bf16[32,4096]{1,0:T(8,128)(2,1)S(1)} %pad_maximum_fusion.10.refs_1_), channel_id=1, source_target_pairs={{0,24},{4,28},{8,0},{12,4},{16,8},{20,12},{24,16},{28,20},{32,56},... | collective-permute-start | bytes 786440 | tf_op jit(solution)/shard_map/ppermute | solution.py:86
  6.6 8.5 %collective-permute-start.5 = (bf16[32,4096]{1,0:T(8,128)(2,1)S(1)}, bf16[32,4096]{1,0:T(8,128)(2,1)S(1)}, u32[]{:S(2)}, u32[]{:S(2)}) collective-permute-start(bf16[32,4096]{1,0:T(8,128)(2,1)S(1)} %pad_maximum_fusion.10.refs_1_), channel_id=1, source_target_pairs={{0,8},{4,12},{8,16},{12,20},{16,24},{20,28},{24,0},{28,4},{32,40},... | collective-permute-start | bytes 786440 | tf_op jit(solution)/shard_map/ppermute | solution.py:86
  8.1 7.2 %collective-permute-start.2 = (bf16[32,4096]{1,0:T(8,128)(2,1)S(1)}, bf16[32,4096]{1,0:T(8,128)(2,1)S(1)}, u32[]{:S(2)}, u32[]{:S(2)}) collective-permute-start(bf16[32,4096]{1,0:T(8,128)(2,1)S(1)} %pad_maximum_fusion.10.refs_1_), channel_id=1, source_target_pairs={{0,192},{4,196},{8,200},{12,204},{16,208},{20,212},{24,216},{28,22... | collective-permute-start | bytes 786440 | tf_op jit(solution)/shard_map/ppermute | solution.py:86
  9.7 30.5 %slice-start = ((s8[8388608]{0:T(1024)(128)(4,1)}), s8[4194304]{0:T(1024)(128)(4,1)S(1)}, s32[]{:S(2)}) async-start(s8[8388608]{0:T(1024)(128)(4,1)} %bitcast.9), calls=%async_computation.1 | async-start | bytes 8388608
  12.4 27.9 %slice-start.1 = ((s8[8388608]{0:T(1024)(128)(4,1)}), s8[4194304]{0:T(1024)(128)(4,1)S(1)}, s32[]{:S(2)}) async-start(s8[8388608]{0:T(1024)(128)(4,1)} %bitcast.9), calls=%async_computation.2 | async-start | bytes 8388608
  15.6 18.4 %collective-permute-start.8 = (bf16[512,4096]{1,0:T(8,128)(2,1)S(1)}, bf16[512,4096]{1,0:T(8,128)(2,1)S(1)}, u32[]{:S(2)}, u32[]{:S(2)}) collective-permute-start(bf16[512,4096]{1,0:T(8,128)(2,1)S(1)} %constant_dynamic-slice_fusion.5), channel_id=1, source_target_pairs={{0,4},{4,0},{8,12},{12,8},{16,20},{20,16},{24,28},{28,24},{32,36},... | collective-permute-start | bytes 12582920 | tf_op jit(solution)/shard_map/ppermute | solution.py:256
  15.7 15.3 %collective-permute-start.11 = (bf16[64,4096]{1,0:T(8,128)(2,1)S(1)}, bf16[64,4096]{1,0:T(8,128)(2,1)S(1)}, u32[]{:S(2)}, u32[]{:S(2)}) collective-permute-start(bf16[64,4096]{1,0:T(8,128)(2,1)S(1)} %get-tuple-element.38), channel_id=1, source_target_pairs={{0,8},{4,12},{8,16},{12,20},{16,24},{20,28},{24,0},{28,4},{32,40},... | collective-permute-start | bytes 1572872 | tf_op jit(solution)/shard_map/ppermute | solution.py:86
  17.3 14.6 %collective-permute-start.10 = (bf16[64,4096]{1,0:T(8,128)(2,1)S(1)}, bf16[64,4096]{1,0:T(8,128)(2,1)S(1)}, u32[]{:S(2)}, u32[]{:S(2)}) collective-permute-start(bf16[64,4096]{1,0:T(8,128)(2,1)S(1)} %get-tuple-element.37), channel_id=1, source_target_pairs={{0,24},{4,28},{8,0},{12,4},{16,8},{20,12},{24,16},{28,20},{32,56},... | collective-permute-start | bytes 1572872 | tf_op jit(solution)/shard_map/ppermute | solution.py:86
  18.7 15.1 %collective-permute-start.4 = (bf16[64,4096]{1,0:T(8,128)(2,1)S(1)}, bf16[64,4096]{1,0:T(8,128)(2,1)S(1)}, u32[]{:S(2)}, u32[]{:S(2)}) collective-permute-start(bf16[64,4096]{1,0:T(8,128)(2,1)S(1)} %get-tuple-element.34), channel_id=1, source_target_pairs={{0,64},{4,68},{8,72},{12,76},{16,80},{20,84},{24,88},{28,92},{32,9... | collective-permute-start | bytes 1572872 | tf_op jit(solution)/shard_map/ppermute | solution.py:86
  20.2 13.6 %collective-permute-start.6 = (bf16[64,4096]{1,0:T(8,128)(2,1)S(1)}, bf16[64,4096]{1,0:T(8,128)(2,1)S(1)}, u32[]{:S(2)}, u32[]{:S(2)}) collective-permute-start(bf16[64,4096]{1,0:T(8,128)(2,1)S(1)} %get-tuple-element.35), channel_id=1, source_target_pairs={{0,192},{4,196},{8,200},{12,204},{16,208},{20,212},{24,216},{28,22... | collective-permute-start | bytes 1572872 | tf_op jit(solution)/shard_map/ppermute | solution.py:86
  34.0 13.1 %collective-permute-start.9 = (bf16[64,4096]{1,0:T(8,128)(2,1)S(1)}, bf16[64,4096]{1,0:T(8,128)(2,1)S(1)}, u32[]{:S(2)}, u32[]{:S(2)}) collective-permute-start(bf16[64,4096]{1,0:T(8,128)(2,1)S(1)} %get-tuple-element.40), channel_id=1, source_target_pairs={{0,32},{4,36},{8,40},{12,44},{16,48},{20,52},{24,56},{28,60},{32,0... | collective-permute-start | bytes 1572872 | tf_op jit(solution)/shard_map/ppermute | solution.py:86
  34.4 13.0 %collective-permute-start.13 = (bf16[64,4096]{1,0:T(8,128)(2,1)S(1)}, bf16[64,4096]{1,0:T(8,128)(2,1)S(1)}, u32[]{:S(2)}, u32[]{:S(2)}) collective-permute-start(bf16[64,4096]{1,0:T(8,128)(2,1)S(1)} %collective-permute-done.10.refs_8_), channel_id=1, source_target_pairs={{0,192},{4,196},{8,200},{12,204},{16,208},{20,212},{24,216},{28,22... | collective-permute-start | bytes 1572872 | tf_op jit(solution)/shard_map/ppermute | solution.py:86
  37.3 13.8 %collective-permute-start.15 = (bf16[64,4096]{1,0:T(8,128)(2,1)S(1)}, bf16[64,4096]{1,0:T(8,128)(2,1)S(1)}, u32[]{:S(2)}, u32[]{:S(2)}) collective-permute-start(bf16[64,4096]{1,0:T(8,128)(2,1)S(1)} %collective-permute-done.4.refs_7_), channel_id=1, source_target_pairs={{0,24},{4,28},{8,0},{12,4},{16,8},{20,12},{24,16},{28,20},{32,56},... | collective-permute-start | bytes 1572872 | tf_op jit(solution)/shard_map/ppermute | solution.py:86
  40.2 13.7 %collective-permute-start.17 = (bf16[64,4096]{1,0:T(8,128)(2,1)S(1)}, bf16[64,4096]{1,0:T(8,128)(2,1)S(1)}, u32[]{:S(2)}, u32[]{:S(2)}) collective-permute-start(bf16[64,4096]{1,0:T(8,128)(2,1)S(1)} %get-tuple-element.48), channel_id=1, source_target_pairs={{0,64},{4,68},{8,72},{12,76},{16,80},{20,84},{24,88},{28,92},{32,9... | collective-permute-start | bytes 1572872 | tf_op jit(solution)/shard_map/ppermute | solution.py:86
  40.2 13.7 %collective-permute-start.18 = (bf16[64,4096]{1,0:T(8,128)(2,1)S(1)}, bf16[64,4096]{1,0:T(8,128)(2,1)S(1)}, u32[]{:S(2)}, u32[]{:S(2)}) collective-permute-start(bf16[64,4096]{1,0:T(8,128)(2,1)S(1)} %get-tuple-element.49), channel_id=1, source_target_pairs={{0,8},{4,12},{8,16},{12,20},{16,24},{20,28},{24,0},{28,4},{32,40},... | collective-permute-start | bytes 1572872 | tf_op jit(solution)/shard_map/ppermute | solution.py:86
  47.1 19.3 %collective-permute-start.12 = (bf16[64,4096]{1,0:T(8,128)(2,1)S(1)}, bf16[64,4096]{1,0:T(8,128)(2,1)S(1)}, u32[]{:S(2)}, u32[]{:S(2)}) collective-permute-start(bf16[64,4096]{1,0:T(8,128)(2,1)S(1)} %get-tuple-element.43), channel_id=1, source_target_pairs={{0,32},{4,36},{8,40},{12,44},{16,48},{20,52},{24,56},{28,60},{32,0... | collective-permute-start | bytes 1572872 | tf_op jit(solution)/shard_map/ppermute | solution.py:86
  47.4 10.4 %collective-permute-start.14 = (bf16[32,4096]{1,0:T(8,128)(2,1)S(1)}, bf16[32,4096]{1,0:T(8,128)(2,1)S(1)}, u32[]{:S(2)}, u32[]{:S(2)}) collective-permute-start(bf16[32,4096]{1,0:T(8,128)(2,1)S(1)} %slice.58), channel_id=1, source_target_pairs={{0,192},{4,196},{8,200},{12,204},{16,208},{20,212},{24,216},{28,22... | collective-permute-start | bytes 786440 | tf_op jit(solution)/shard_map/ppermute | solution.py:86
  51.1 7.6 %collective-permute-start.16 = (bf16[32,4096]{1,0:T(8,128)(2,1)S(1)}, bf16[32,4096]{1,0:T(8,128)(2,1)S(1)}, u32[]{:S(2)}, u32[]{:S(2)}) collective-permute-start(bf16[32,4096]{1,0:T(8,128)(2,1)S(1)} %slice.58), channel_id=1, source_target_pairs={{0,24},{4,28},{8,0},{12,4},{16,8},{20,12},{24,16},{28,20},{32,56},... | collective-permute-start | bytes 786440 | tf_op jit(solution)/shard_map/ppermute | solution.py:86
  54.0 9.4 %collective-permute-start.19 = (bf16[48,4096]{1,0:T(8,128)(2,1)S(1)}, bf16[48,4096]{1,0:T(8,128)(2,1)S(1)}, u32[]{:S(2)}, u32[]{:S(2)}) collective-permute-start(bf16[48,4096]{1,0:T(8,128)(2,1)S(1)} %get-tuple-element.50), channel_id=1, source_target_pairs={{0,8},{4,12},{8,16},{12,20},{16,24},{20,28},{24,0},{28,4},{32,40},... | collective-permute-start | bytes 1179656 | tf_op jit(solution)/shard_map/ppermute | solution.py:110
  54.1 9.3 %collective-permute-start.20 = (bf16[48,4096]{1,0:T(8,128)(2,1)S(1)}, bf16[48,4096]{1,0:T(8,128)(2,1)S(1)}, u32[]{:S(2)}, u32[]{:S(2)}) collective-permute-start(bf16[48,4096]{1,0:T(8,128)(2,1)S(1)} %get-tuple-element.51), channel_id=1, source_target_pairs={{0,64},{4,68},{8,72},{12,76},{16,80},{20,84},{24,88},{28,92},{32,9... | collective-permute-start | bytes 1179656 | tf_op jit(solution)/shard_map/ppermute | solution.py:110
  58.7 5.0 %collective-permute-start.21 = (bf16[16,4096]{1,0:T(8,128)(2,1)S(1)}, bf16[16,4096]{1,0:T(8,128)(2,1)S(1)}, u32[]{:S(2)}, u32[]{:S(2)}) collective-permute-start(bf16[16,4096]{1,0:T(8,128)(2,1)S(1)} %slice.64), channel_id=1, source_target_pairs={{0,24},{4,28},{8,0},{12,4},{16,8},{20,12},{24,16},{28,20},{32,56},... | collective-permute-start | bytes 393224 | tf_op jit(solution)/shard_map/ppermute | solution.py:95
  61.2 5.3 %collective-permute-start.22 = (bf16[16,4096]{1,0:T(8,128)(2,1)S(1)}, bf16[16,4096]{1,0:T(8,128)(2,1)S(1)}, u32[]{:S(2)}, u32[]{:S(2)}) collective-permute-start(bf16[16,4096]{1,0:T(8,128)(2,1)S(1)} %slice.65), channel_id=1, source_target_pairs={{0,192},{4,196},{8,200},{12,204},{16,208},{20,212},{24,216},{28,22... | collective-permute-start | bytes 393224 | tf_op jit(solution)/shard_map/ppermute | solution.py:95
  69.5 2.7 %collective-permute-start.23 = (f32[32,16,512]{2,1,0:T(8,128)S(1)}, f32[32,16,512]{2,1,0:T(8,128)S(1)}, u32[]{:S(2)}, u32[]{:S(2)}) collective-permute-start(f32[32,16,512]{2,1,0:T(8,128)S(1)} %get-tuple-element.58), channel_id=1, source_target_pairs={{0,4},{4,0},{8,12},{12,8},{16,20},{20,16},{24,28},{28,24},{32,36},... | collective-permute-start | bytes 3145736 | tf_op jit(solution)/shard_map/ppermute | solution.py:275
  73.4 24.2 %all-to-all-start = ((f32[32,16,512]{2,1,0:T(8,128)}), f32[32,16,512]{2,1,0:T(8,128)S(1)}, u32[]{:S(2)}, u32[]{:S(2)}) async-start(f32[32,16,512]{2,1,0:T(8,128)} %add.36), calls=%async_computation | async-start | bytes 2097152 | tf_op jit(solution)/shard_map/all_to_all | solution.py:278
  97.7 5.1 %collective-permute-start.24 = (f32[16,256]{1,0:T(8,128)S(1)}, f32[16,256]{1,0:T(8,128)S(1)}, u32[]{:S(2)}, u32[]{:S(2)}) collective-permute-start(f32[16,256]{1,0:T(8,128)S(1)} %pad_maximum_fusion.11), channel_id=1, source_target_pairs={{0,1},{1,0},{2,3},{3,2},{4,5},{5,4},{6,7},{7,6},{8,9},{9,8},{10,11... | collective-permute-start | bytes 49160 | tf_op jit(solution)/shard_map/ppermute | solution.py:219
  102.8 6.7 %collective-permute-start.25 = (f32[16,128]{1,0:T(8,128)S(1)}, f32[16,128]{1,0:T(8,128)S(1)}, u32[]{:S(2)}, u32[]{:S(2)}) collective-permute-start(f32[16,128]{1,0:T(8,128)S(1)} %slice.67), channel_id=1, source_target_pairs={{0,3},{1,2},{2,1},{3,0},{4,7},{5,6},{6,5},{7,4},{8,11},{9,10},{10,... | collective-permute-start | bytes 24584 | tf_op jit(solution)/shard_map/ppermute | solution.py:219

commit v6 on v5

--- a/solution.py
+++ b/solution.py
@@ -88,11 +88,11 @@
     return got
 
 
-def send_last(held, chain, wait):
+def send_last(held, wait):
     rows = [fetch(held, (moved(LAST, link),)) for link in FINISH]
     k = rows[0].shape[0] // len(FINISH)
     return [
-        lax.ppermute(after(r[n * k : (n + 1) * k], wait, *chain[link]), "tm", pairs(link))
+        lax.ppermute(after(r[n * k : (n + 1) * k], wait), "tm", pairs(link))
         for n, (link, r) in enumerate(zip(FINISH, rows))
     ]
 
@@ -262,7 +262,7 @@
     got = send(held + mid_blocks, PHASES[3], chain, early[:1])
     shared = send_shared(held + mid_blocks, chain, early[0])
     mid = multiply(at, names(mid_blocks), rows(mid_blocks), weights, early, "mid")
-    last = send_last(got, chain, mid[0])
+    last = send_last(got, mid[0])
     keep, out = multiply(
         at,
         names(got) + [SHARING[0][1], SHARED, SHARING[1][1], LAST],

time: 110 us -> 110 us (level)
  waiting for transfers between devices: 44.1 us -> 42.8 us
  starting transfers between devices: 47.5 us -> 48.8 us
  transfers between devices with their start and end apart: 27 -> 27, of which waited for: 16 -> 14; matrix products, arithmetic and copies ran while one was open for 3% -> 3% of each run, Pallas kernels for 8% -> 8%
where the time goes in v6:
time: 110 us
  starting transfers between devices  48.8 us (44%)
  waiting for transfers between devices  42.8 us (39%)
  Pallas kernels  11.5 us (10%)
  local copies, waits for them, and re-layouts  4.27 us (4%)
  other arithmetic  2.42 us (2%)
    ppermute x17, starting transfers between devices, send(): chain[link] = [lax.ppermute(r, 'tm', pairs(link))]  26.4 us
    all_to_all x1, waiting for transfers between devices, local(): lax.all_to_all(both, 'tm', 0, 0, tiled=True, axis_index_groups=SAME_CORE)  16.6 us
    ppermute x17, waiting for transfers between devices, send(): chain[link] = [lax.ppermute(r, 'tm', pairs(link))]  16.4 us
    pallas_call x3, Pallas kernels, multiply(): pl.pallas_call(functools.partial(multiply_kernel, names, len(bundles), k,...  11.5 us
    ppermute x2, starting transfers between devices, swap(): return lax.ppermute(value, 'floor', [(f, f ^ by) for f in range(len(at))])  8.39 us
    all_to_all x1, starting transfers between devices, local(): lax.all_to_all(both, 'tm', 0, 0, tiled=True, axis_index_groups=SAME_CORE)  8.05 us
    ppermute x2, starting transfers between devices, send_last(): lax.ppermute(after(r[n * k:(n + 1) * k], wait), 'tm', pairs(link))  5.5 us
    dynamic_slice x3, local copies, waits for them, and re-layouts, columns(): return lax.dynamic_slice_in_dim(rows, which * half, half, 1)  4.09 us
  transfers between devices with their start and end apart: 27, of which 14 were waited for; matrix products, arithmetic and copies ran while one was open for 3% of the time, Pallas kernels for 8%

profile of v6, /device:TPU:2, one launch (start us, length us, event | category | flops | bytes accessed | tf_op | source)
XLA Modules:
  0.0 110.1 jit_solution(4532569120073236579)
XLA Ops:
  0.0 1.0 dynamic-slice_bitcast_fusion
  1.0 0.1 collective-permute-start
  1.1 1.3 %collective-permute-done = bf16[16,4096]{1,0:T(8,128)(2,1)S(1)} collective-permute-done((bf16[16,4096]{1,0:T(8,128)(2,1)S(1)}, bf16[16,4096]{1,0:T(8,128)(2,1)S(1)}, u32[]{:S(2)}, u32[]{:S(2)}) %collective-permute-start) | collective-permute-done | bytes 131104 | tf_op jit(solution)/shard_map/ppermute | solution.py:237
  2.5 1.7 %collective-permute-start.1 = (bf16[32,4096]{1,0:T(8,128)(2,1)S(1)}, bf16[32,4096]{1,0:T(8,128)(2,1)S(1)}, u32[]{:S(2)}, u32[]{:S(2)}) collective-permute-start(bf16[32,4096]{1,0:T(8,128)(2,1)S(1)} %pad_maximum_fusion.10.refs_1_), channel_id=1, source_target_pairs={{0,64},{4,68},{8,72},{12,76},{16,80},{20,84},{24,88},{28,92},{32,9... | collective-permute-start | bytes 786440 | tf_op jit(solution)/shard_map/ppermute | solution.py:86
  4.1 1.9 %collective-permute-start.7 = (bf16[32,4096]{1,0:T(8,128)(2,1)S(1)}, bf16[32,4096]{1,0:T(8,128)(2,1)S(1)}, u32[]{:S(2)}, u32[]{:S(2)}) collective-permute-start(bf16[32,4096]{1,0:T(8,128)(2,1)S(1)} %pad_maximum_fusion.10.refs_1_), channel_id=1, source_target_pairs={{0,32},{4,36},{8,40},{12,44},{16,48},{20,52},{24,56},{28,60},{32,0... | collective-permute-start | bytes 786440 | tf_op jit(solution)/shard_map/ppermute | solution.py:86
  6.0 0.5 collective-permute-start.3
  6.6 1.5 %collective-permute-start.5 = (bf16[32,4096]{1,0:T(8,128)(2,1)S(1)}, bf16[32,4096]{1,0:T(8,128)(2,1)S(1)}, u32[]{:S(2)}, u32[]{:S(2)}) collective-permute-start(bf16[32,4096]{1,0:T(8,128)(2,1)S(1)} %pad_maximum_fusion.10.refs_1_), channel_id=1, source_target_pairs={{0,8},{4,12},{8,16},{12,20},{16,24},{20,28},{24,0},{28,4},{32,40},... | collective-permute-start | bytes 786440 | tf_op jit(solution)/shard_map/ppermute | solution.py:86
  8.1 1.7 %collective-permute-start.2 = (bf16[32,4096]{1,0:T(8,128)(2,1)S(1)}, bf16[32,4096]{1,0:T(8,128)(2,1)S(1)}, u32[]{:S(2)}, u32[]{:S(2)}) collective-permute-start(bf16[32,4096]{1,0:T(8,128)(2,1)S(1)} %pad_maximum_fusion.10.refs_1_), channel_id=1, source_target_pairs={{0,192},{4,196},{8,200},{12,204},{16,208},{20,212},{24,216},{28,22... | collective-permute-start | bytes 786440 | tf_op jit(solution)/shard_map/ppermute | solution.py:86
  9.7 2.6 %constant_dynamic-slice_fusion.5 = bf16[512,4096]{1,0:T(8,128)(2,1)S(1)} fusion(bf16[512,8192]{1,0:T(8,128)(2,1)} %bitcast.8, s32[]{:T(128)S(6)} %select_n.42), kind=kLoop, calls=%fused_computation.25 | loop fusion | bytes 8388612 | tf_op jit(solution)/shard_map/dynamic_slice | solution.py:232
  12.4 0.0 slice-start.1
  12.4 0.0 collective-permute-done.1.refs_3_
  12.4 0.0 collective-permute-done.7.refs_4_
  12.4 1.5 %collective-permute-done.3.refs_2_ = bf16[32,4096]{1,0:T(8,128)(2,1)S(1)} collective-permute-done((bf16[32,4096]{1,0:T(8,128)(2,1)S(1)}, bf16[32,4096]{1,0:T(8,128)(2,1)S(1)}, u32[]{:S(2)}, u32[]{:S(2)}) %collective-permute-start.3) | collective-permute-done | bytes 262176 | tf_op jit(solution)/shard_map/ppermute | solution.py:86
  13.8 1.3 %collective-permute-done.5.refs_5_ = bf16[32,4096]{1,0:T(8,128)(2,1)S(1)} collective-permute-done((bf16[32,4096]{1,0:T(8,128)(2,1)S(1)}, bf16[32,4096]{1,0:T(8,128)(2,1)S(1)}, u32[]{:S(2)}, u32[]{:S(2)}) %collective-permute-start.5) | collective-permute-done | bytes 262176 | tf_op jit(solution)/shard_map/ppermute | solution.py:86
  15.1 0.2 collective-permute-done.2.refs_6_
  15.3 0.3 pad_maximum_fusion.7
  15.6 0.1 collective-permute-start.8
  15.7 1.6 %collective-permute-start.11 = (bf16[64,4096]{1,0:T(8,128)(2,1)S(1)}, bf16[64,4096]{1,0:T(8,128)(2,1)S(1)}, u32[]{:S(2)}, u32[]{:S(2)}) collective-permute-start(bf16[64,4096]{1,0:T(8,128)(2,1)S(1)} %get-tuple-element.38), channel_id=1, source_target_pairs={{0,8},{4,12},{8,16},{12,20},{16,24},{20,28},{24,0},{28,4},{32,40},... | collective-permute-start | bytes 1572872 | tf_op jit(solution)/shard_map/ppermute | solution.py:86
  17.3 1.4 %collective-permute-start.10 = (bf16[64,4096]{1,0:T(8,128)(2,1)S(1)}, bf16[64,4096]{1,0:T(8,128)(2,1)S(1)}, u32[]{:S(2)}, u32[]{:S(2)}) collective-permute-start(bf16[64,4096]{1,0:T(8,128)(2,1)S(1)} %get-tuple-element.37), channel_id=1, source_target_pairs={{0,24},{4,28},{8,0},{12,4},{16,8},{20,12},{24,16},{28,20},{32,56},... | collective-permute-start | bytes 1572872 | tf_op jit(solution)/shard_map/ppermute | solution.py:86
  18.7 1.6 %collective-permute-start.4 = (bf16[64,4096]{1,0:T(8,128)(2,1)S(1)}, bf16[64,4096]{1,0:T(8,128)(2,1)S(1)}, u32[]{:S(2)}, u32[]{:S(2)}) collective-permute-start(bf16[64,4096]{1,0:T(8,128)(2,1)S(1)} %get-tuple-element.34), channel_id=1, source_target_pairs={{0,64},{4,68},{8,72},{12,76},{16,80},{20,84},{24,88},{28,92},{32,9... | collective-permute-start | bytes 1572872 | tf_op jit(solution)/shard_map/ppermute | solution.py:86
  20.2 1.7 %collective-permute-start.6 = (bf16[64,4096]{1,0:T(8,128)(2,1)S(1)}, bf16[64,4096]{1,0:T(8,128)(2,1)S(1)}, u32[]{:S(2)}, u32[]{:S(2)}) collective-permute-start(bf16[64,4096]{1,0:T(8,128)(2,1)S(1)} %get-tuple-element.35), channel_id=1, source_target_pairs={{0,192},{4,196},{8,200},{12,204},{16,208},{20,212},{24,216},{28,22... | collective-permute-start | bytes 1572872 | tf_op jit(solution)/shard_map/ppermute | solution.py:86
  21.9 9.2 %collective-permute-done.11.refs_9_ = bf16[64,4096]{1,0:T(8,128)(2,1)S(1)} collective-permute-done((bf16[64,4096]{1,0:T(8,128)(2,1)S(1)}, bf16[64,4096]{1,0:T(8,128)(2,1)S(1)}, u32[]{:S(2)}, u32[]{:S(2)}) %collective-permute-start.11) | collective-permute-done | bytes 524320 | tf_op jit(solution)/shard_map/ppermute | solution.py:86
  31.1 0.8 collective-permute-done.10.refs_8_
  32.0 1.8 %collective-permute-done.4.refs_7_ = bf16[64,4096]{1,0:T(8,128)(2,1)S(1)} collective-permute-done((bf16[64,4096]{1,0:T(8,128)(2,1)S(1)}, bf16[64,4096]{1,0:T(8,128)(2,1)S(1)}, u32[]{:S(2)}, u32[]{:S(2)}) %collective-permute-start.4) | collective-permute-done | bytes 524320 | tf_op jit(solution)/shard_map/ppermute | solution.py:86
  33.8 0.1 collective-permute-done.6.refs_10_
  33.9 0.2 pad_maximum_fusion.4
  34.0 0.0 collective-permute-done.8.refs_12_.refs_7_.refs_9_
  34.0 0.4 collective-permute-start.9
  34.4 2.9 %collective-permute-start.13 = (bf16[64,4096]{1,0:T(8,128)(2,1)S(1)}, bf16[64,4096]{1,0:T(8,128)(2,1)S(1)}, u32[]{:S(2)}, u32[]{:S(2)}) collective-permute-start(bf16[64,4096]{1,0:T(8,128)(2,1)S(1)} %collective-permute-done.10.refs_8_), channel_id=1, source_target_pairs={{0,192},{4,196},{8,200},{12,204},{16,208},{20,212},{24,216},{28,22... | collective-permute-start | bytes 1572872 | tf_op jit(solution)/shard_map/ppermute | solution.py:86
  37.3 3.0 %collective-permute-start.15 = (bf16[64,4096]{1,0:T(8,128)(2,1)S(1)}, bf16[64,4096]{1,0:T(8,128)(2,1)S(1)}, u32[]{:S(2)}, u32[]{:S(2)}) collective-permute-start(bf16[64,4096]{1,0:T(8,128)(2,1)S(1)} %collective-permute-done.4.refs_7_), channel_id=1, source_target_pairs={{0,24},{4,28},{8,0},{12,4},{16,8},{20,12},{24,16},{28,20},{32,56},... | collective-permute-start | bytes 1572872 | tf_op jit(solution)/shard_map/ppermute | solution.py:86
  40.2 0.0 collective-permute-start.17
  40.2 0.0 collective-permute-start.18
  40.3 0.5 constant_dynamic-slice_fusion.4.refs_11_.refs_6_.refs_8_
  40.8 4.8 %early.1 = (f32[32,16,512]{2,1,0:T(8,128)S(1)}, f32[32,16,512]{2,1,0:T(8,128)S(1)}) custom-call(s32[1]{0:T(128)} %bitcast.refs_0_, bf16[32,4096]{1,0:T(8,128)(2,1)S(1)} %pad_maximum_fusion.10.refs_1_, bf16[32,4096]{1,0:T(8,128)(2,1)S(1)} %collective-permute-done.3.refs_2_, bf16[32,4096]{1,0:T(8,128)(2,1)S(1)} %collective-permute-done.1.refs_3_, ...), custom_call_target="tpu_custom_call" | custom-call | flops 3758096384 | bytes 16252928 | tf_op jit(solution)/shard_map/early/pallas_call | solution.py:192
  45.6 1.5 %collective-permute-done.9.refs_4_ = bf16[64,4096]{1,0:T(8,128)(2,1)S(1)} collective-permute-done((bf16[64,4096]{1,0:T(8,128)(2,1)S(1)}, bf16[64,4096]{1,0:T(8,128)(2,1)S(1)}, u32[]{:S(2)}, u32[]{:S(2)}) %collective-permute-start.9) | collective-permute-done | bytes 524320 | tf_op jit(solution)/shard_map/ppermute | solution.py:86
  47.1 0.3 collective-permute-start.12
  47.4 0.0 collective-permute-done.13.refs_2_
  47.4 3.7 %collective-permute-start.14 = (bf16[32,4096]{1,0:T(8,128)(2,1)S(1)}, bf16[32,4096]{1,0:T(8,128)(2,1)S(1)}, u32[]{:S(2)}, u32[]{:S(2)}) collective-permute-start(bf16[32,4096]{1,0:T(8,128)(2,1)S(1)} %slice.58), channel_id=1, source_target_pairs={{0,192},{4,196},{8,200},{12,204},{16,208},{20,212},{24,216},{28,22... | collective-permute-start | bytes 786440 | tf_op jit(solution)/shard_map/ppermute | solution.py:86
  51.1 0.0 collective-permute-done.15.refs_1_
  51.1 2.8 %collective-permute-start.16 = (bf16[32,4096]{1,0:T(8,128)(2,1)S(1)}, bf16[32,4096]{1,0:T(8,128)(2,1)S(1)}, u32[]{:S(2)}, u32[]{:S(2)}) collective-permute-start(bf16[32,4096]{1,0:T(8,128)(2,1)S(1)} %slice.58), channel_id=1, source_target_pairs={{0,24},{4,28},{8,0},{12,4},{16,8},{20,12},{24,16},{28,20},{32,56},... | collective-permute-start | bytes 786440 | tf_op jit(solution)/shard_map/ppermute | solution.py:86
  53.9 0.0 collective-permute-done.17.refs_3_
  53.9 0.0 collective-permute-done.18.refs_5_
  54.0 0.1 pad_maximum_fusion.9
  54.0 0.1 collective-permute-start.19
  54.1 0.1 collective-permute-start.20
  54.2 3.6 %mid.1 = (f32[32,16,512]{2,1,0:T(8,128)S(1)}, f32[32,16,512]{2,1,0:T(8,128)S(1)}) custom-call(s32[1]{0:T(128)} %bitcast.refs_0_, bf16[64,4096]{1,0:T(8,128)(2,1)S(1)} %collective-permute-done.15.refs_1_, bf16[64,4096]{1,0:T(8,128)(2,1)S(1)} %collective-permute-done.13.refs_2_, bf16[64,4096]{1,0:T(8,128)(2,1)S(1)} %collective-permute-done.17.refs_3_, ...), custom_call_target="tpu_custom_call" | custom-call | flops 2684354560 | bytes 15204352 | tf_op jit(solution)/shard_map/mid/pallas_call | solution.py:192
  57.9 2.0 %collective-permute-start.21 = (bf16[16,4096]{1,0:T(8,128)(2,1)S(1)}, bf16[16,4096]{1,0:T(8,128)(2,1)S(1)}, u32[]{:S(2)}, u32[]{:S(2)}) collective-permute-start(bf16[16,4096]{1,0:T(8,128)(2,1)S(1)} %slice.64), channel_id=1, source_target_pairs={{0,24},{4,28},{8,0},{12,4},{16,8},{20,12},{24,16},{28,20},{32,56},... | collective-permute-start | bytes 393224 | tf_op jit(solution)/shard_map/ppermute | solution.py:95
  59.9 0.0 collective-permute-done.16.refs_3_
  59.9 3.5 %collective-permute-start.22 = (bf16[16,4096]{1,0:T(8,128)(2,1)S(1)}, bf16[16,4096]{1,0:T(8,128)(2,1)S(1)}, u32[]{:S(2)}, u32[]{:S(2)}) collective-permute-start(bf16[16,4096]{1,0:T(8,128)(2,1)S(1)} %slice.65), channel_id=1, source_target_pairs={{0,192},{4,196},{8,200},{12,204},{16,208},{20,212},{24,216},{28,22... | collective-permute-start | bytes 393224 | tf_op jit(solution)/shard_map/ppermute | solution.py:95
  63.4 0.0 collective-permute-done.20.refs_5_
  63.4 0.0 collective-permute-done.21.refs_6_
  63.5 2.5 %collective-permute-done.22.refs_7_ = bf16[16,4096]{1,0:T(8,128)(2,1)S(1)} collective-permute-done((bf16[16,4096]{1,0:T(8,128)(2,1)S(1)}, bf16[16,4096]{1,0:T(8,128)(2,1)S(1)}, u32[]{:S(2)}, u32[]{:S(2)}) %collective-permute-start.22) | collective-permute-done | bytes 131104 | tf_op jit(solution)/shard_map/ppermute | solution.py:95
  65.9 3.0 %late.1 = (f32[32,16,512]{2,1,0:T(8,128)S(1)}, f32[32,16,512]{2,1,0:T(8,128)S(1)}) custom-call(s32[1]{0:T(128)} %bitcast.refs_0_, bf16[64,4096]{1,0:T(8,128)(2,1)S(1)} %collective-permute-done.12.refs_1_, bf16[32,4096]{1,0:T(8,128)(2,1)S(1)} %collective-permute-done.14.refs_2_, bf16[32,4096]{1,0:T(8,128)(2,1)S(1)} %collective-permute-done.16.refs_3_, ...), custom_call_target="tpu_custom_call" | custom-call | flops 2147483648 | bytes 14680064 | tf_op jit(solution)/shard_map/late/pallas_call | solution.py:192
  69.0 0.1 collective-permute-start.23
  69.1 2.6 %collective-permute-done.23 = f32[32,16,512]{2,1,0:T(8,128)S(1)} collective-permute-done((f32[32,16,512]{2,1,0:T(8,128)S(1)}, f32[32,16,512]{2,1,0:T(8,128)S(1)}, u32[]{:S(2)}, u32[]{:S(2)}) %collective-permute-start.23) | collective-permute-done | bytes 1048608 | tf_op jit(solution)/shard_map/ppermute | solution.py:275
  71.7 1.2 %add.36 = f32[32,16,512]{2,1,0:T(8,128)} add(f32[32,16,512]{2,1,0:T(8,128)S(1)} %get-tuple-element.57, f32[32,16,512]{2,1,0:T(8,128)S(1)} %collective-permute-done.23) | non-fusion elementwise | flops 262144 | bytes 3145728 | tf_op jit(solution)/shard_map/add | solution.py:275
  72.9 8.1 %all-to-all-start = ((f32[32,16,512]{2,1,0:T(8,128)}), f32[32,16,512]{2,1,0:T(8,128)S(1)}, u32[]{:S(2)}, u32[]{:S(2)}) async-start(f32[32,16,512]{2,1,0:T(8,128)} %add.36), calls=%async_computation | async-start | bytes 2097152 | tf_op jit(solution)/shard_map/all_to_all | solution.py:278
  81.0 16.6 %all-to-all-done = f32[32,16,512]{2,1,0:T(8,128)S(1)} async-done(((f32[32,16,512]{2,1,0:T(8,128)}), f32[32,16,512]{2,1,0:T(8,128)S(1)}, u32[]{:S(2)}, u32[]{:S(2)}) %all-to-all-start) | async-done | bytes 1048608 | tf_op jit(solution)/shard_map/all_to_all | solution.py:278
  97.6 0.1 reduce_sum.9
  97.7 3.4 %collective-permute-start.24 = (f32[16,256]{1,0:T(8,128)S(1)}, f32[16,256]{1,0:T(8,128)S(1)}, u32[]{:S(2)}, u32[]{:S(2)}) collective-permute-start(f32[16,256]{1,0:T(8,128)S(1)} %pad_maximum_fusion.11), channel_id=1, source_target_pairs={{0,1},{1,0},{2,3},{3,2},{4,5},{5,4},{6,7},{7,6},{8,9},{9,8},{10,11... | collective-permute-start | bytes 49160 | tf_op jit(solution)/shard_map/ppermute | solution.py:219
  101.1 1.7 %collective-permute-done.24 = f32[16,256]{1,0:T(8,128)S(1)} collective-permute-done((f32[16,256]{1,0:T(8,128)S(1)}, f32[16,256]{1,0:T(8,128)S(1)}, u32[]{:S(2)}, u32[]{:S(2)}) %collective-permute-start.24) | collective-permute-done | bytes 16416 | tf_op jit(solution)/shard_map/ppermute | solution.py:219
  102.8 5.0 %collective-permute-start.25 = (f32[16,128]{1,0:T(8,128)S(1)}, f32[16,128]{1,0:T(8,128)S(1)}, u32[]{:S(2)}, u32[]{:S(2)}) collective-permute-start(f32[16,128]{1,0:T(8,128)S(1)} %slice.67), channel_id=1, source_target_pairs={{0,3},{1,2},{2,1},{3,0},{4,7},{5,6},{6,5},{7,4},{8,11},{9,10},{10,... | collective-permute-start | bytes 24584 | tf_op jit(solution)/shard_map/ppermute | solution.py:219
  107.9 1.6 %collective-permute-done.25 = f32[16,128]{1,0:T(8,128)S(1)} collective-permute-done((f32[16,128]{1,0:T(8,128)S(1)}, f32[16,128]{1,0:T(8,128)S(1)}, u32[]{:S(2)}, u32[]{:S(2)}) %collective-permute-start.25) | collective-permute-done | bytes 8224 | tf_op jit(solution)/shard_map/ppermute | solution.py:219
  109.5 0.6 fusion.1
  (23 shorter events, 0.2 us)
Async XLA Ops:
  1.0 1.4 %collective-permute-start = (bf16[16,4096]{1,0:T(8,128)(2,1)S(1)}, bf16[16,4096]{1,0:T(8,128)(2,1)S(1)}, u32[]{:S(2)}, u32[]{:S(2)}) collective-permute-start(bf16[16,4096]{1,0:T(8,128)(2,1)S(1)} %get-tuple-element.33), channel_id=1, source_target_pairs={{0,4},{4,0},{8,12},{12,8},{16,20},{20,16},{24,28},{28,24},{32,36},... | collective-permute-start | bytes 393224 | tf_op jit(solution)/shard_map/ppermute | solution.py:237
  2.5 9.9 %collective-permute-start.1 = (bf16[32,4096]{1,0:T(8,128)(2,1)S(1)}, bf16[32,4096]{1,0:T(8,128)(2,1)S(1)}, u32[]{:S(2)}, u32[]{:S(2)}) collective-permute-start(bf16[32,4096]{1,0:T(8,128)(2,1)S(1)} %pad_maximum_fusion.10.refs_1_), channel_id=1, source_target_pairs={{0,64},{4,68},{8,72},{12,76},{16,80},{20,84},{24,88},{28,92},{32,9... | collective-permute-start | bytes 786440 | tf_op jit(solution)/shard_map/ppermute | solution.py:86
  4.1 8.3 %collective-permute-start.7 = (bf16[32,4096]{1,0:T(8,128)(2,1)S(1)}, bf16[32,4096]{1,0:T(8,128)(2,1)S(1)}, u32[]{:S(2)}, u32[]{:S(2)}) collective-permute-start(bf16[32,4096]{1,0:T(8,128)(2,1)S(1)} %pad_maximum_fusion.10.refs_1_), channel_id=1, source_target_pairs={{0,32},{4,36},{8,40},{12,44},{16,48},{20,52},{24,56},{28,60},{32,0... | collective-permute-start | bytes 786440 | tf_op jit(solution)/shard_map/ppermute | solution.py:86
  6.0 7.8 %collective-permute-start.3 = (bf16[32,4096]{1,0:T(8,128)(2,1)S(1)}, bf16[32,4096]{1,0:T(8,128)(2,1)S(1)}, u32[]{:S(2)}, u32[]{:S(2)}) collective-permute-start(bf16[32,4096]{1,0:T(8,128)(2,1)S(1)} %pad_maximum_fusion.10.refs_1_), channel_id=1, source_target_pairs={{0,24},{4,28},{8,0},{12,4},{16,8},{20,12},{24,16},{28,20},{32,56},... | collective-permute-start | bytes 786440 | tf_op jit(solution)/shard_map/ppermute | solution.py:86
  6.6 8.5 %collective-permute-start.5 = (bf16[32,4096]{1,0:T(8,128)(2,1)S(1)}, bf16[32,4096]{1,0:T(8,128)(2,1)S(1)}, u32[]{:S(2)}, u32[]{:S(2)}) collective-permute-start(bf16[32,4096]{1,0:T(8,128)(2,1)S(1)} %pad_maximum_fusion.10.refs_1_), channel_id=1, source_target_pairs={{0,8},{4,12},{8,16},{12,20},{16,24},{20,28},{24,0},{28,4},{32,40},... | collective-permute-start | bytes 786440 | tf_op jit(solution)/shard_map/ppermute | solution.py:86
  8.1 7.2 %collective-permute-start.2 = (bf16[32,4096]{1,0:T(8,128)(2,1)S(1)}, bf16[32,4096]{1,0:T(8,128)(2,1)S(1)}, u32[]{:S(2)}, u32[]{:S(2)}) collective-permute-start(bf16[32,4096]{1,0:T(8,128)(2,1)S(1)} %pad_maximum_fusion.10.refs_1_), channel_id=1, source_target_pairs={{0,192},{4,196},{8,200},{12,204},{16,208},{20,212},{24,216},{28,22... | collective-permute-start | bytes 786440 | tf_op jit(solution)/shard_map/ppermute | solution.py:86
  9.7 30.5 %slice-start = ((s8[8388608]{0:T(1024)(128)(4,1)}), s8[4194304]{0:T(1024)(128)(4,1)S(1)}, s32[]{:S(2)}) async-start(s8[8388608]{0:T(1024)(128)(4,1)} %bitcast.9), calls=%async_computation.1 | async-start | bytes 8388608
  12.4 27.9 %slice-start.1 = ((s8[8388608]{0:T(1024)(128)(4,1)}), s8[4194304]{0:T(1024)(128)(4,1)S(1)}, s32[]{:S(2)}) async-start(s8[8388608]{0:T(1024)(128)(4,1)} %bitcast.9), calls=%async_computation.2 | async-start | bytes 8388608
  15.6 18.4 %collective-permute-start.8 = (bf16[512,4096]{1,0:T(8,128)(2,1)S(1)}, bf16[512,4096]{1,0:T(8,128)(2,1)S(1)}, u32[]{:S(2)}, u32[]{:S(2)}) collective-permute-start(bf16[512,4096]{1,0:T(8,128)(2,1)S(1)} %constant_dynamic-slice_fusion.5), channel_id=1, source_target_pairs={{0,4},{4,0},{8,12},{12,8},{16,20},{20,16},{24,28},{28,24},{32,36},... | collective-permute-start | bytes 12582920 | tf_op jit(solution)/shard_map/ppermute | solution.py:256
  15.7 15.3 %collective-permute-start.11 = (bf16[64,4096]{1,0:T(8,128)(2,1)S(1)}, bf16[64,4096]{1,0:T(8,128)(2,1)S(1)}, u32[]{:S(2)}, u32[]{:S(2)}) collective-permute-start(bf16[64,4096]{1,0:T(8,128)(2,1)S(1)} %get-tuple-element.38), channel_id=1, source_target_pairs={{0,8},{4,12},{8,16},{12,20},{16,24},{20,28},{24,0},{28,4},{32,40},... | collective-permute-start | bytes 1572872 | tf_op jit(solution)/shard_map/ppermute | solution.py:86
  17.3 14.6 %collective-permute-start.10 = (bf16[64,4096]{1,0:T(8,128)(2,1)S(1)}, bf16[64,4096]{1,0:T(8,128)(2,1)S(1)}, u32[]{:S(2)}, u32[]{:S(2)}) collective-permute-start(bf16[64,4096]{1,0:T(8,128)(2,1)S(1)} %get-tuple-element.37), channel_id=1, source_target_pairs={{0,24},{4,28},{8,0},{12,4},{16,8},{20,12},{24,16},{28,20},{32,56},... | collective-permute-start | bytes 1572872 | tf_op jit(solution)/shard_map/ppermute | solution.py:86
  18.7 15.1 %collective-permute-start.4 = (bf16[64,4096]{1,0:T(8,128)(2,1)S(1)}, bf16[64,4096]{1,0:T(8,128)(2,1)S(1)}, u32[]{:S(2)}, u32[]{:S(2)}) collective-permute-start(bf16[64,4096]{1,0:T(8,128)(2,1)S(1)} %get-tuple-element.34), channel_id=1, source_target_pairs={{0,64},{4,68},{8,72},{12,76},{16,80},{20,84},{24,88},{28,92},{32,9... | collective-permute-start | bytes 1572872 | tf_op jit(solution)/shard_map/ppermute | solution.py:86
  20.2 13.6 %collective-permute-start.6 = (bf16[64,4096]{1,0:T(8,128)(2,1)S(1)}, bf16[64,4096]{1,0:T(8,128)(2,1)S(1)}, u32[]{:S(2)}, u32[]{:S(2)}) collective-permute-start(bf16[64,4096]{1,0:T(8,128)(2,1)S(1)} %get-tuple-element.35), channel_id=1, source_target_pairs={{0,192},{4,196},{8,200},{12,204},{16,208},{20,212},{24,216},{28,22... | collective-permute-start | bytes 1572872 | tf_op jit(solution)/shard_map/ppermute | solution.py:86
  34.0 13.1 %collective-permute-start.9 = (bf16[64,4096]{1,0:T(8,128)(2,1)S(1)}, bf16[64,4096]{1,0:T(8,128)(2,1)S(1)}, u32[]{:S(2)}, u32[]{:S(2)}) collective-permute-start(bf16[64,4096]{1,0:T(8,128)(2,1)S(1)} %get-tuple-element.40), channel_id=1, source_target_pairs={{0,32},{4,36},{8,40},{12,44},{16,48},{20,52},{24,56},{28,60},{32,0... | collective-permute-start | bytes 1572872 | tf_op jit(solution)/shard_map/ppermute | solution.py:86
  34.4 13.0 %collective-permute-start.13 = (bf16[64,4096]{1,0:T(8,128)(2,1)S(1)}, bf16[64,4096]{1,0:T(8,128)(2,1)S(1)}, u32[]{:S(2)}, u32[]{:S(2)}) collective-permute-start(bf16[64,4096]{1,0:T(8,128)(2,1)S(1)} %collective-permute-done.10.refs_8_), channel_id=1, source_target_pairs={{0,192},{4,196},{8,200},{12,204},{16,208},{20,212},{24,216},{28,22... | collective-permute-start | bytes 1572872 | tf_op jit(solution)/shard_map/ppermute | solution.py:86
  37.3 13.8 %collective-permute-start.15 = (bf16[64,4096]{1,0:T(8,128)(2,1)S(1)}, bf16[64,4096]{1,0:T(8,128)(2,1)S(1)}, u32[]{:S(2)}, u32[]{:S(2)}) collective-permute-start(bf16[64,4096]{1,0:T(8,128)(2,1)S(1)} %collective-permute-done.4.refs_7_), channel_id=1, source_target_pairs={{0,24},{4,28},{8,0},{12,4},{16,8},{20,12},{24,16},{28,20},{32,56},... | collective-permute-start | bytes 1572872 | tf_op jit(solution)/shard_map/ppermute | solution.py:86
  40.2 13.7 %collective-permute-start.17 = (bf16[64,4096]{1,0:T(8,128)(2,1)S(1)}, bf16[64,4096]{1,0:T(8,128)(2,1)S(1)}, u32[]{:S(2)}, u32[]{:S(2)}) collective-permute-start(bf16[64,4096]{1,0:T(8,128)(2,1)S(1)} %get-tuple-element.48), channel_id=1, source_target_pairs={{0,64},{4,68},{8,72},{12,76},{16,80},{20,84},{24,88},{28,92},{32,9... | collective-permute-start | bytes 1572872 | tf_op jit(solution)/shard_map/ppermute | solution.py:86
  40.2 13.7 %collective-permute-start.18 = (bf16[64,4096]{1,0:T(8,128)(2,1)S(1)}, bf16[64,4096]{1,0:T(8,128)(2,1)S(1)}, u32[]{:S(2)}, u32[]{:S(2)}) collective-permute-start(bf16[64,4096]{1,0:T(8,128)(2,1)S(1)} %get-tuple-element.49), channel_id=1, source_target_pairs={{0,8},{4,12},{8,16},{12,20},{16,24},{20,28},{24,0},{28,4},{32,40},... | collective-permute-start | bytes 1572872 | tf_op jit(solution)/shard_map/ppermute | solution.py:86
  47.1 18.8 %collective-permute-start.12 = (bf16[64,4096]{1,0:T(8,128)(2,1)S(1)}, bf16[64,4096]{1,0:T(8,128)(2,1)S(1)}, u32[]{:S(2)}, u32[]{:S(2)}) collective-permute-start(bf16[64,4096]{1,0:T(8,128)(2,1)S(1)} %get-tuple-element.43), channel_id=1, source_target_pairs={{0,32},{4,36},{8,40},{12,44},{16,48},{20,52},{24,56},{28,60},{32,0... | collective-permute-start | bytes 1572872 | tf_op jit(solution)/shard_map/ppermute | solution.py:86
  47.4 10.4 %collective-permute-start.14 = (bf16[32,4096]{1,0:T(8,128)(2,1)S(1)}, bf16[32,4096]{1,0:T(8,128)(2,1)S(1)}, u32[]{:S(2)}, u32[]{:S(2)}) collective-permute-start(bf16[32,4096]{1,0:T(8,128)(2,1)S(1)} %slice.58), channel_id=1, source_target_pairs={{0,192},{4,196},{8,200},{12,204},{16,208},{20,212},{24,216},{28,22... | collective-permute-start | bytes 786440 | tf_op jit(solution)/shard_map/ppermute | solution.py:86
  51.1 8.8 %collective-permute-start.16 = (bf16[32,4096]{1,0:T(8,128)(2,1)S(1)}, bf16[32,4096]{1,0:T(8,128)(2,1)S(1)}, u32[]{:S(2)}, u32[]{:S(2)}) collective-permute-start(bf16[32,4096]{1,0:T(8,128)(2,1)S(1)} %slice.58), channel_id=1, source_target_pairs={{0,24},{4,28},{8,0},{12,4},{16,8},{20,12},{24,16},{28,20},{32,56},... | collective-permute-start | bytes 786440 | tf_op jit(solution)/shard_map/ppermute | solution.py:86
  54.0 9.4 %collective-permute-start.19 = (bf16[48,4096]{1,0:T(8,128)(2,1)S(1)}, bf16[48,4096]{1,0:T(8,128)(2,1)S(1)}, u32[]{:S(2)}, u32[]{:S(2)}) collective-permute-start(bf16[48,4096]{1,0:T(8,128)(2,1)S(1)} %get-tuple-element.50), channel_id=1, source_target_pairs={{0,8},{4,12},{8,16},{12,20},{16,24},{20,28},{24,0},{28,4},{32,40},... | collective-permute-start | bytes 1179656 | tf_op jit(solution)/shard_map/ppermute | solution.py:110
  54.1 9.3 %collective-permute-start.20 = (bf16[48,4096]{1,0:T(8,128)(2,1)S(1)}, bf16[48,4096]{1,0:T(8,128)(2,1)S(1)}, u32[]{:S(2)}, u32[]{:S(2)}) collective-permute-start(bf16[48,4096]{1,0:T(8,128)(2,1)S(1)} %get-tuple-element.51), channel_id=1, source_target_pairs={{0,64},{4,68},{8,72},{12,76},{16,80},{20,84},{24,88},{28,92},{32,9... | collective-permute-start | bytes 1179656 | tf_op jit(solution)/shard_map/ppermute | solution.py:110
  57.9 5.6 %collective-permute-start.21 = (bf16[16,4096]{1,0:T(8,128)(2,1)S(1)}, bf16[16,4096]{1,0:T(8,128)(2,1)S(1)}, u32[]{:S(2)}, u32[]{:S(2)}) collective-permute-start(bf16[16,4096]{1,0:T(8,128)(2,1)S(1)} %slice.64), channel_id=1, source_target_pairs={{0,24},{4,28},{8,0},{12,4},{16,8},{20,12},{24,16},{28,20},{32,56},... | collective-permute-start | bytes 393224 | tf_op jit(solution)/shard_map/ppermute | solution.py:95
  59.9 6.0 %collective-permute-start.22 = (bf16[16,4096]{1,0:T(8,128)(2,1)S(1)}, bf16[16,4096]{1,0:T(8,128)(2,1)S(1)}, u32[]{:S(2)}, u32[]{:S(2)}) collective-permute-start(bf16[16,4096]{1,0:T(8,128)(2,1)S(1)} %slice.65), channel_id=1, source_target_pairs={{0,192},{4,196},{8,200},{12,204},{16,208},{20,212},{24,216},{28,22... | collective-permute-start | bytes 393224 | tf_op jit(solution)/shard_map/ppermute | solution.py:95
  69.0 2.7 %collective-permute-start.23 = (f32[32,16,512]{2,1,0:T(8,128)S(1)}, f32[32,16,512]{2,1,0:T(8,128)S(1)}, u32[]{:S(2)}, u32[]{:S(2)}) collective-permute-start(f32[32,16,512]{2,1,0:T(8,128)S(1)} %get-tuple-element.58), channel_id=1, source_target_pairs={{0,4},{4,0},{8,12},{12,8},{16,20},{20,16},{24,28},{28,24},{32,36},... | collective-permute-start | bytes 3145736 | tf_op jit(solution)/shard_map/ppermute | solution.py:275
  72.9 24.7 %all-to-all-start = ((f32[32,16,512]{2,1,0:T(8,128)}), f32[32,16,512]{2,1,0:T(8,128)S(1)}, u32[]{:S(2)}, u32[]{:S(2)}) async-start(f32[32,16,512]{2,1,0:T(8,128)} %add.36), calls=%async_computation | async-start | bytes 2097152 | tf_op jit(solution)/shard_map/all_to_all | solution.py:278
  97.7 5.1 %collective-permute-start.24 = (f32[16,256]{1,0:T(8,128)S(1)}, f32[16,256]{1,0:T(8,128)S(1)}, u32[]{:S(2)}, u32[]{:S(2)}) collective-permute-start(f32[16,256]{1,0:T(8,128)S(1)} %pad_maximum_fusion.11), channel_id=1, source_target_pairs={{0,1},{1,0},{2,3},{3,2},{4,5},{5,4},{6,7},{7,6},{8,9},{9,8},{10,11... | collective-permute-start | bytes 49160 | tf_op jit(solution)/shard_map/ppermute | solution.py:219
  102.8 6.7 %collective-permute-start.25 = (f32[16,128]{1,0:T(8,128)S(1)}, f32[16,128]{1,0:T(8,128)S(1)}, u32[]{:S(2)}, u32[]{:S(2)}) collective-permute-start(f32[16,128]{1,0:T(8,128)S(1)} %slice.67), channel_id=1, source_target_pairs={{0,3},{1,2},{2,1},{3,0},{4,7},{5,6},{6,5},{7,4},{8,11},{9,10},{10,... | collective-permute-start | bytes 24584 | tf_op jit(solution)/shard_map/ppermute | solution.py:219
